TPU v7x, 32 devices: a whole 2x2x4 slice. The times are simulated.
32 devices in a mesh: ctx: 8 (over y, x, core), fsdp: 4 (over z).
Axes of the slice: x: 2, y: 2, z: 4, core: 2. Of those that a mesh axis runs over, the one named last changes fastest.
Arguments:
- layer_input: bfloat16 [4, 2048, 2048], P('fsdp', 'ctx'), may hold values from -6 to 6
- dy: bfloat16 [4, 2048, 2048], P('fsdp', 'ctx'), may hold values from -6 to 6
- block_order: int32 [8, 2], replicated, may hold values from 0 to 15, as said below
- lengths: int32 [4], P('fsdp'), may hold values from 512 to 2048, as said below
- attn_gain: bfloat16 [2048], P('fsdp'), may hold values from 0.25 to 1.75
- wq: bfloat16 [2048, 2048], P('fsdp'), may hold values from -0.125 to 0.125
- wk: bfloat16 [2048, 1024], P('fsdp'), may hold values from -0.125 to 0.125
- wv: bfloat16 [2048, 1024], P('fsdp'), may hold values from -0.125 to 0.125
- q_gain: bfloat16 [128], replicated, may hold values from 0.5 to 3
- k_gain: bfloat16 [128], replicated, may hold values from 0.5 to 3
- wo: bfloat16 [2048, 2048], P('fsdp'), may hold values from -1.5 to 1.5
- mlp_gain: bfloat16 [2048], P('fsdp'), may hold values from 0.25 to 1.75
- wg: bfloat16 [2048, 6144], P('fsdp'), may hold values from -0.125 to 0.125
- wu: bfloat16 [2048, 6144], P('fsdp'), may hold values from -0.125 to 0.125
- wd: bfloat16 [2048, 6144], P('fsdp'), may hold values from -0.078125 to 0.078125
Outputs:
- layer_output: bfloat16 [4, 2048, 2048], P('fsdp', 'ctx')
- dx: float32 [4, 2048, 2048], P('fsdp', 'ctx')
- d_wq: float32 [2048, 2048], P(('ctx', 'fsdp'))
- d_wk: float32 [2048, 1024], P(('ctx', 'fsdp'))
- d_wv: float32 [2048, 1024], P(('ctx', 'fsdp'))
- d_wo: float32 [2048, 2048], P(('ctx', 'fsdp'))
- d_wg: float32 [2048, 6144], P(('ctx', 'fsdp'))
- d_wu: float32 [2048, 6144], P(('ctx', 'fsdp'))
- d_wd: float32 [2048, 6144], P(('ctx', 'fsdp'))
- d_attn_gain: float32 [2048], replicated
- d_mlp_gain: float32 [2048], replicated
- d_q_gain: float32 [128], replicated
- d_k_gain: float32 [128], replicated
Inputs may be any that keep to these rules, and one draw needn't show every extreme that they name: `block_order`: row c holds a pair of blocks b and 15 - b; the first column is a permutation of 0 to 7. `lengths`: at least one sequence has the full length 2048.
All inputs are finite; a program needn't handle non-finite values.
Results may differ from a plain program's by a relative error of at most 0.023.
Values may be sent and summed in bfloat16 or wider, within the bound.
No kernel may reach another device: no remote copies, remote signals or barrier semaphores. Data moves between devices by JAX's collectives and lax.ppermute only.
A program may use at most 640 MiB of HBM per device.

v0:
```python
import math

import jax
import jax.numpy as jnp
from jax import lax
from jax.sharding import PartitionSpec as P

QUERY_HEADS = 16
KEY_VALUE_HEADS = 8
HEAD_SIZE = 128
FF = 6144


epsilon = 1e-06
rope_base = 1000000.0
large_negative = -1e30


def rms_scale(values):
    return lax.rsqrt(jnp.mean(values * values, axis=-1, keepdims=True) + epsilon)


def rotate(values, places):
    half_width = values.shape[-1] // 2
    frequency = jnp.exp(
        -math.log(rope_base) * 2.0 * jnp.arange(half_width, dtype=jnp.float32) / values.shape[-1]
    )
    angle = places[:, None].astype(jnp.float32) * frequency[None, :]
    cosine = jnp.cos(angle)[:, None, :]
    sine = jnp.sin(angle)[:, None, :]
    first = values[..., :half_width]
    second = values[..., half_width:]
    return jnp.concatenate(
        [first * cosine - second * sine, second * cosine + first * sine], axis=-1
    )


def head_prepare(values, gain_row, places):
    return rotate(values * rms_scale(values) * gain_row, places)


def dot_nt(left, right):
    return lax.dot_general(
        left, right, (((1,), (1,)), ((), ())), preferred_element_type=jnp.float32
    )


def dot_tn(left, right):
    return lax.dot_general(
        left, right, (((0,), (0,)), ((), ())), preferred_element_type=jnp.float32
    )


def rounding_round_trip(values):
    return lax.optimization_barrier(values.astype(jnp.bfloat16)).astype(jnp.float32)


def per_device(
    layer_input,
    dy,
    block_order,
    lengths,
    attn_gain,
    wq,
    wk,
    wv,
    q_gain,
    k_gain,
    wo,
    mlp_gain,
    wg,
    wu,
    wd,
):
    total_row_count = layer_input.shape[1]
    block_rows = total_row_count // 2
    query_group_count = QUERY_HEADS // KEY_VALUE_HEADS
    score_scale = 1.0 / math.sqrt(HEAD_SIZE)
    all_places = (
        block_order[:, :, None] * block_rows
        + jnp.arange(block_rows, dtype=jnp.int32)[None, None, :]
    ).reshape(-1)
    my_places = lax.dynamic_slice_in_dim(
        all_places, lax.axis_index("ctx") * total_row_count, total_row_count
    )
    seq_length = lengths[0]
    x_float = layer_input[0].astype(jnp.float32)
    scale_one = rms_scale(x_float)
    x_hat = x_float * scale_one

    def fold_rows(pieces):
        portion_rows = pieces[0].shape[0]
        normalized_input = (x_source[0] * pieces[0].astype(jnp.float32)).astype(jnp.bfloat16)
        return tuple(
            (
                jnp.dot(normalized_input, piece, preferred_element_type=jnp.float32)
                for piece in pieces[1:]
            )
        )

    x_source = [x_hat]
    query_raw, key_unnormed, value_unprojected = fold_rows(
        (
            lax.all_gather(attn_gain, "fsdp", axis=0, tiled=True),
            lax.all_gather(wq, "fsdp", axis=0, tiled=True),
            lax.all_gather(wk, "fsdp", axis=0, tiled=True),
            lax.all_gather(wv, "fsdp", axis=0, tiled=True),
        )
    )
    query_gain = q_gain.astype(jnp.float32)
    key_gain = k_gain.astype(jnp.float32)
    query_rotated, query_pull = jax.vjp(
        lambda values, gain_row: head_prepare(values, gain_row, my_places),
        query_raw.reshape(total_row_count, QUERY_HEADS, HEAD_SIZE),
        query_gain,
    )
    key_rot, key_pullback_fn = jax.vjp(
        lambda values, gain_row: head_prepare(values, gain_row, my_places),
        key_unnormed.reshape(total_row_count, KEY_VALUE_HEADS, HEAD_SIZE),
        key_gain,
    )
    query_bfloat_rows = query_rotated.astype(jnp.bfloat16).reshape(
        total_row_count, KEY_VALUE_HEADS, query_group_count, HEAD_SIZE
    )
    key_bf = key_rot.astype(jnp.bfloat16)
    value_bfloat_rows = value_unprojected.astype(jnp.bfloat16).reshape(
        total_row_count, KEY_VALUE_HEADS, HEAD_SIZE
    )

    def score_piece(key_piece):
        portion_rows = key_piece.shape[0]
        allowed = (all_places[None, :] <= my_places[:, None]) & (all_places[None, :] < seq_length)
        raw = jnp.einsum(
            "rkgd,nkd->rkgn", query_bfloat_rows, key_piece, preferred_element_type=jnp.float32
        )
        return (raw * score_scale, allowed[:, None, None, :])

    pieces = (
        lax.all_gather(key_bf, "ctx", axis=0, tiled=True),
        lax.all_gather(value_bfloat_rows, "ctx", axis=0, tiled=True),
    )
    running_maximum_score = jnp.full(
        (total_row_count, KEY_VALUE_HEADS, query_group_count), large_negative, jnp.float32
    )
    scores, allowed = score_piece(pieces[0])
    masked = jnp.where(allowed, scores, large_negative)
    new_max = jnp.maximum(running_maximum_score, jnp.max(masked, axis=-1))
    weights_now = jnp.where(allowed, jnp.exp(masked - new_max[..., None]), 0.0)
    new_sum = jnp.sum(weights_now, axis=-1)
    new_out = jnp.einsum(
        "rkgn,nkd->rkgd",
        weights_now.astype(jnp.bfloat16),
        pieces[1],
        preferred_element_type=jnp.float32,
    )
    attn_out = new_out / new_sum[..., None]
    log_total = new_max + jnp.log(new_sum)
    attn_bf = attn_out.reshape(total_row_count, QUERY_HEADS * HEAD_SIZE).astype(jnp.bfloat16)
    branch_one = dot_nt(attn_bf, lax.all_gather(wo, "fsdp", axis=0, tiled=True))
    hidden_one = x_float + branch_one
    scale_two = rms_scale(hidden_one)
    hat_two = hidden_one * scale_two
    x_source[0] = hat_two
    gate, up_val = fold_rows(
        (
            lax.all_gather(mlp_gain, "fsdp", axis=0, tiled=True),
            lax.all_gather(wg, "fsdp", axis=0, tiled=True),
            lax.all_gather(wu, "fsdp", axis=0, tiled=True),
        )
    )
    sigma = jax.nn.sigmoid(gate)
    silu_val = gate * sigma
    activated = (silu_val * up_val).astype(jnp.bfloat16)
    branch_two = dot_nt(activated, lax.all_gather(wd, "fsdp", axis=0, tiled=True))
    output = (hidden_one + branch_two).astype(jnp.bfloat16)
    grad_out = dy[0]
    grad_float = grad_out.astype(jnp.float32)
    mlp_full = (
        lax.all_gather(mlp_gain, "fsdp", axis=0, tiled=True),
        lax.all_gather(wg, "fsdp", axis=0, tiled=True),
        lax.all_gather(wu, "fsdp", axis=0, tiled=True),
        lax.all_gather(wd, "fsdp", axis=0, tiled=True),
    )
    grad_act = jnp.dot(grad_out, mlp_full[3], preferred_element_type=jnp.float32)
    grad_gate = (grad_act * up_val * sigma * (1.0 + gate * (1.0 - sigma))).astype(jnp.bfloat16)
    grad_up = (grad_act * silu_val).astype(jnp.bfloat16)
    grad_norm_two = dot_nt(grad_gate, mlp_full[1]) + dot_nt(grad_up, mlp_full[2])
    mlp_gain_f = mlp_full[0].astype(jnp.float32)
    term_mlp_gain = jnp.sum(grad_norm_two * hat_two, axis=0)
    grad_hat_two = grad_norm_two * mlp_gain_f
    grad_hidden = grad_float + scale_two * (
        grad_hat_two - hat_two * jnp.mean(grad_hat_two * hat_two, axis=-1, keepdims=True)
    )
    normalized_input = (hat_two * mlp_gain_f).astype(jnp.bfloat16)
    mlp_share = lax.psum_scatter(
        jnp.concatenate(
            [
                dot_tn(normalized_input, grad_gate),
                dot_tn(normalized_input, grad_up),
                dot_tn(grad_out, activated),
            ],
            axis=1,
        ),
        ("ctx", "fsdp"),
        scatter_dimension=0,
        tiled=True,
    )
    grad_branch = grad_hidden.astype(jnp.bfloat16)
    attn_full = (
        lax.all_gather(attn_gain, "fsdp", axis=0, tiled=True),
        lax.all_gather(wq, "fsdp", axis=0, tiled=True),
        lax.all_gather(wk, "fsdp", axis=0, tiled=True),
        lax.all_gather(wv, "fsdp", axis=0, tiled=True),
        lax.all_gather(wo, "fsdp", axis=0, tiled=True),
    )
    attention_gradient_half = jnp.dot(
        grad_branch, attn_full[4], preferred_element_type=jnp.float32
    ).astype(jnp.bfloat16)
    attention_gradient_half = attention_gradient_half.reshape(
        total_row_count, KEY_VALUE_HEADS, query_group_count, HEAD_SIZE
    )
    delta = jnp.sum(attention_gradient_half.astype(jnp.float32) * attn_out, axis=-1)
    pieces = (
        lax.all_gather(key_bf, "ctx", axis=0, tiled=True),
        lax.all_gather(value_bfloat_rows, "ctx", axis=0, tiled=True),
    )
    portion_rows = pieces[0].shape[0]
    scores, allowed = score_piece(pieces[0])
    probs = jnp.where(
        allowed, jnp.exp(jnp.where(allowed, scores, large_negative) - log_total[..., None]), 0.0
    )
    grad_probs = jnp.einsum(
        "rkgd,nkd->rkgn", attention_gradient_half, pieces[1], preferred_element_type=jnp.float32
    )
    grad_scores = (probs * (grad_probs - delta[..., None])).astype(jnp.bfloat16)
    grad_query = score_scale * jnp.einsum(
        "rkgn,nkd->rkgd", grad_scores, pieces[0], preferred_element_type=jnp.float32
    )
    portion_keys = score_scale * jnp.einsum(
        "rkgn,rkgd->nkd", grad_scores, query_bfloat_rows, preferred_element_type=jnp.float32
    )
    portion_values = jnp.einsum(
        "rkgn,rkgd->nkd",
        probs.astype(jnp.bfloat16),
        attention_gradient_half,
        preferred_element_type=jnp.float32,
    )
    key_gradient_rows = portion_keys.reshape(portion_rows, KEY_VALUE_HEADS * HEAD_SIZE)
    value_gradient_rows = portion_values.reshape(portion_rows, KEY_VALUE_HEADS * HEAD_SIZE)
    key_gradient_total, value_grad_sum = (
        lax.psum_scatter(
            key_gradient_rows.astype(jnp.bfloat16), "ctx", scatter_dimension=0, tiled=True
        ).astype(jnp.float32),
        lax.psum_scatter(
            value_gradient_rows.astype(jnp.bfloat16), "ctx", scatter_dimension=0, tiled=True
        ).astype(jnp.float32),
    )
    grad_query_pre, grad_qgain = query_pull(
        rounding_round_trip(grad_query).reshape(total_row_count, QUERY_HEADS, HEAD_SIZE)
    )
    key_gradient_unrotated, key_gain_gradient = key_pullback_fn(
        rounding_round_trip(key_gradient_total).reshape(total_row_count, KEY_VALUE_HEADS, HEAD_SIZE)
    )
    grad_query_b = grad_query_pre.reshape(total_row_count, QUERY_HEADS * HEAD_SIZE).astype(
        jnp.bfloat16
    )
    key_gradient_half = key_gradient_unrotated.reshape(
        total_row_count, KEY_VALUE_HEADS * HEAD_SIZE
    ).astype(jnp.bfloat16)
    grad_value_b = value_grad_sum.astype(jnp.bfloat16)
    grad_norm_one = (
        dot_nt(grad_query_b, attn_full[1])
        + dot_nt(key_gradient_half, attn_full[2])
        + dot_nt(grad_value_b, attn_full[3])
    )
    attn_gain_f = attn_full[0].astype(jnp.float32)
    term_attn_gain = jnp.sum(grad_norm_one * x_hat, axis=0)
    grad_hat_one = grad_norm_one * attn_gain_f
    grad_input = grad_hidden + scale_one * (
        grad_hat_one - x_hat * jnp.mean(grad_hat_one * x_hat, axis=-1, keepdims=True)
    )
    normalized_input = (x_hat * attn_gain_f).astype(jnp.bfloat16)
    attn_share = lax.psum_scatter(
        jnp.concatenate(
            [
                dot_tn(normalized_input, grad_query_b),
                dot_tn(normalized_input, key_gradient_half),
                dot_tn(normalized_input, grad_value_b),
                dot_tn(grad_branch, attn_bf),
            ],
            axis=1,
        ),
        ("ctx", "fsdp"),
        scatter_dimension=0,
        tiled=True,
    )
    gain_attn, gain_mlp, gain_query, gain_key = lax.psum(
        (term_attn_gain, term_mlp_gain, grad_qgain, key_gain_gradient), ("ctx", "fsdp")
    )
    query_cols = QUERY_HEADS * HEAD_SIZE
    key_value_columns = KEY_VALUE_HEADS * HEAD_SIZE
    d_wq = attn_share[:, :query_cols]
    d_wk = attn_share[:, query_cols : query_cols + key_value_columns]
    d_wv = attn_share[:, query_cols + key_value_columns : query_cols + 2 * key_value_columns]
    d_wo = attn_share[:, query_cols + 2 * key_value_columns :]
    d_wg = mlp_share[:, :FF]
    d_wu = mlp_share[:, FF : 2 * FF]
    d_wd = mlp_share[:, 2 * FF :]
    return (
        output[None],
        grad_input[None],
        d_wq,
        d_wk,
        d_wv,
        d_wo,
        d_wg,
        d_wu,
        d_wd,
        gain_attn,
        gain_mlp,
        gain_query,
        gain_key,
    )


def solution(mesh):
    placed = (
        P("fsdp", "ctx", None),
        P("fsdp", "ctx", None),
        P(),
        P("fsdp"),
        P("fsdp"),
        P("fsdp", None),
        P("fsdp", None),
        P("fsdp", None),
        P(),
        P(),
        P("fsdp", None),
        P("fsdp"),
        P("fsdp", None),
        P("fsdp", None),
        P("fsdp", None),
    )
    return jax.shard_map(
        per_device,
        mesh=mesh,
        in_specs=placed,
        out_specs=(
            P("fsdp", "ctx", None),
            P("fsdp", "ctx", None),
            P(("ctx", "fsdp"), None),
            P(("ctx", "fsdp"), None),
            P(("ctx", "fsdp"), None),
            P(("ctx", "fsdp"), None),
            P(("ctx", "fsdp"), None),
            P(("ctx", "fsdp"), None),
            P(("ctx", "fsdp"), None),
            P(),
            P(),
            P(),
            P(),
        ),
        check_vma=False,
    )
```

profile of v0, /device:TPU:0, one launch (start us, length us, event | category | flops | bytes accessed | tf_op | source)
XLA Modules:
  0.0 3830.8 jit_solution(5912537097548198103)
XLA Ops:
  9.6 13.5 all-gather
  24.0 69.1 %all-gather.16.cloned.1.call-done = bf16[2048,1024]{1,0:T(8,128)(2,1)} async-done(((bf16[512,1024]{1,0:T(8,128)(2,1)}), bf16[2048,1024]{1,0:T(8,128)(2,1)}) %all-gather.16.cloned.1.call-update) | async-done | bytes 4194320 | tf_op jit(solution)/shard_map/all_gather | solution.py:106
  93.1 6.5 copy.50
  99.6 4.0 multiply_reduce_fusion.9
  105.8 68.2 %all-gather.12.cloned.1.call-done = bf16[2048,1024]{1,0:T(8,128)(2,1)} async-done(((bf16[512,1024]{1,0:T(8,128)(2,1)}), bf16[2048,1024]{1,0:T(8,128)(2,1)}) %all-gather.12.cloned.1.call-update) | async-done | bytes 4194320 | tf_op jit(solution)/shard_map/all_gather | solution.py:107
  182.1 12.2 all-gather.1
  196.7 127.2 %all-gather.20.cloned.1.call-done = bf16[2048,2048]{1,0:T(8,128)(2,1)} async-done(((bf16[512,2048]{1,0:T(8,128)(2,1)}), bf16[2048,2048]{1,0:T(8,128)(2,1)}) %all-gather.20.cloned.1.call-update) | async-done | bytes 8388624 | tf_op jit(solution)/shard_map/all_gather | solution.py:105
  323.9 12.4 copy.51
  336.3 5.9 multiply_reduce_fusion.6
  347.4 14.4 all-gather.18.cloned.1.call-done
  361.8 16.8 fusion.5
  378.7 15.1 fusion.2
  393.8 7.8 all-gather.14.cloned.1.call-done
  401.6 19.2 fusion.87
  420.8 131.9 %all-gather.22.cloned.1.call-done = bf16[2048,2048]{1,0:T(8,128)(2,1)} async-done(((bf16[512,2048]{1,0:T(8,128)(2,1)}), bf16[2048,2048]{1,0:T(8,128)(2,1)}) %all-gather.22.cloned.1.call-update) | async-done | bytes 8388624 | tf_op jit(solution)/shard_map/all_gather | solution.py:159
  552.7 5.9 multiply_reduce_fusion.5
  560.2 417.5 %all-gather.26.cloned.1.call-done = bf16[2048,6144]{1,0:T(8,128)(2,1)} async-done(((bf16[512,6144]{1,0:T(8,128)(2,1)}), bf16[2048,6144]{1,0:T(8,128)(2,1)}) %all-gather.26.cloned.1.call-update) | async-done | bytes 25165840 | tf_op jit(solution)/shard_map/all_gather | solution.py:168
  977.7 15.9 fusion.89
  993.6 409.1 %all-gather.24.cloned.1.call-done = bf16[2048,6144]{1,0:T(8,128)(2,1)} async-done(((bf16[512,6144]{1,0:T(8,128)(2,1)}), bf16[2048,6144]{1,0:T(8,128)(2,1)}) %all-gather.24.cloned.1.call-update) | async-done | bytes 25165840 | tf_op jit(solution)/shard_map/all_gather | solution.py:167
  1402.7 15.9 fusion.88
  1418.6 409.1 %all-gather.28.cloned.1.call-done = bf16[2048,6144]{1,0:T(8,128)(2,1)} async-done(((bf16[512,6144]{1,0:T(8,128)(2,1)}), bf16[2048,6144]{1,0:T(8,128)(2,1)}) %all-gather.28.cloned.1.call-update) | async-done | bytes 25165840 | tf_op jit(solution)/shard_map/all_gather | solution.py:174
  1827.7 22.5 multiply_convert_fusion
  1850.2 13.5 fusion.90
  1863.8 16.0 multiply_reduce_fusion.1
  1883.9 5.7 convolution_convert_fusion
  1892.0 22.9 fusion.1
  1914.9 10.7 fusion.12
  1925.7 19.5 bitcast_convert_fusion
  1945.5 10.0 fusion.48
  1960.1 8.4 fusion.59
  1968.4 8.1 fusion.63
  1979.1 4.7 fusion.61
  1983.8 46.6 %reduce-scatter.9.cloned.1.call-done = bf16[256,1024]{0,1:T(8,128)(2,1)} async-done(((bf16[2048,1024]{0,1:T(8,128)(2,1)}), bf16[256,1024]{0,1:T(8,128)(2,1)}) %reduce-scatter.9.cloned.1.call-update) | async-done | bytes 524304 | tf_op jit(solution)/shard_map/reduce_scatter | solution.py:254
  2030.4 6.1 fusion.66
  2036.5 31.6 pad_maximum_fusion.1
  2068.1 48.9 %copy.86 = f32[2048,6144]{1,0:T(8,128)} copy(f32[2048,6144]{0,1:T(8,128)} %pad_maximum_fusion.1) | data formatting | bytes 100663296
  2118.3 32.1 convolution_bitcast_fusion
  2150.4 32.7 fusion.93
  2183.0 22.6 fusion.92
  2205.7 101.0 %pad_maximum_fusion = f32[2048,18432]{1,0:T(8,128)} fusion(f32[2048,6144]{1,0:T(8,128)} %convolution_bitcast_fusion, f32[2048,6144]{1,0:T(8,128)} %fusion.93, f32[2048,6144]{1,0:T(8,128)} %fusion.92), kind=kLoop, calls=%fused_computation | loop fusion | flops 75497472 | bytes 301989888 | tf_op jit(solution)/shard_map/concatenate | solution.py:196
  2307.9 7.3 fusion.91
  2315.2 13.8 fusion.30
  2329.0 4.5 convolution_add_fusion.3
  2336.7 40.8 %all-reduce.4 = (f32[2048]{0:T(1024)}, f32[2048]{0:T(1024)}, f32[128]{0:T(128)}, f32[128]{0:T(128)}) all-reduce(f32[2048]{0:T(1024)S(1)} %get-tuple-element.43, f32[2048]{0:T(1024)S(1)} %copy-done.49, f32[128]{0:T(128)S(1)} %copy-done.54, f32[128]{0:T(128)S(1)} %copy-done.55), channel_id=1, replica_groups=mesh['ctx'=8,'fsdp'=4] {'ctx','fsdp'}, use_global_device_ids=true, to_apply=%region_16.17 | all-reduce | flops 4352 | bytes 34816 | tf_op jit(solution)/shard_map/psum | solution.py:297
  2377.6 3.5 fusion.36
  2381.1 168.6 %reduce-scatter.13.cloned.1.call-done = f32[64,6144]{1,0:T(8,128)} async-done(((f32[2048,6144]{1,0:T(8,128)}), f32[64,6144]{1,0:T(8,128)}) %reduce-scatter.13.cloned.1.call-update) | async-done | bytes 1572880
  2553.8 1265.4 %reduce-scatter.11.cloned.1.call-done = f32[64,18432]{1,0:T(8,128)} async-done(((f32[2048,18432]{1,0:T(8,128)}), f32[64,18432]{1,0:T(8,128)}) %reduce-scatter.11.cloned.1.call-update) | async-done | bytes 4718608 | tf_op jit(solution)/shard_map/reduce_scatter | solution.py:195
  3819.2 4.6 fusion.84
  (198 shorter events, 45.2 us)
Async XLA Ops:
  7.2 16.2 copy-start.1
  7.2 85.9 %all-gather.16.cloned.1.call-start = ((), (), s32[]{:S(2)}) async-start(), calls=%async_computation.6 | async-start | bytes 5242880 | tf_op jit(solution)/shard_map/all_gather | solution.py:106
  8.0 166.1 %all-gather.12.cloned.1.call-start = ((), (), s32[]{:S(2)}) async-start(), calls=%async_computation.4 | async-start | bytes 5242880 | tf_op jit(solution)/shard_map/all_gather | solution.py:107
  8.7 315.2 %all-gather.20.cloned.1.call-start = ((), (), s32[]{:S(2)}) async-start(), calls=%async_computation.8 | async-start | bytes 10485760 | tf_op jit(solution)/shard_map/all_gather | solution.py:105
  9.4 352.4 %all-gather.18.cloned.1.call-start = ((), (), s32[]{:S(2)}) async-start(), calls=%async_computation.7 | async-start | bytes 4718592 | tf_op jit(solution)/shard_map/all_gather | solution.py:139
  9.5 94.1 %copy-start.50 = (f32[128]{0:T(128)}, f32[128]{0:T(128)S(1)}, u32[]{:S(2)}) copy-start(f32[128]{0:T(128)S(1)} %convert_element_type.144) | copy-start | bytes 1540
  23.2 313.1 %copy-start.35 = (f32[4,1,512]{2,1,0:T(1,128)}, f32[4,1,512]{2,1,0:T(1,128)S(1)}, u32[]{:S(2)}) copy-start(f32[4,1,512]{2,1,0:T(1,128)S(1)} %convert_element_type.175) | copy-start | bytes 24580
  23.7 312.6 %copy-start.42 = (f32[256]{0:T(256)}, f32[256]{0:T(256)S(1)}, u32[]{:S(2)}) copy-start(f32[256]{0:T(256)S(1)} %add_rsqrt_fusion.1) | copy-start | bytes 3076
  24.0 319.9 %copy-start.29 = (f32[256,64]{0,1:T(8,128)}, f32[256,64]{0,1:T(8,128)S(1)}, u32[]{:S(2)}) copy-start(f32[256,64]{0,1:T(8,128)S(1)} %get-tuple-element.71) | copy-start | bytes 196612
  24.0 319.9 %copy-start.31 = (f32[256,64]{0,1:T(8,128)}, f32[256,64]{0,1:T(8,128)S(1)}, u32[]{:S(2)}) copy-start(f32[256,64]{0,1:T(8,128)S(1)} %get-tuple-element.72) | copy-start | bytes 196612
  105.8 295.8 %all-gather.14.cloned.1.call-start = ((), (), s32[]{:S(2)}) async-start(), calls=%async_computation.5 | async-start | bytes 4718592 | tf_op jit(solution)/shard_map/all_gather | solution.py:140
  178.5 374.2 %all-gather.22.cloned.1.call-start = ((), (), s32[]{:S(2)}) async-start(), calls=%async_computation.9 | async-start | bytes 10485760 | tf_op jit(solution)/shard_map/all_gather | solution.py:159
  179.1 798.6 %all-gather.26.cloned.1.call-start = ((), (), s32[]{:S(2)}) async-start(), calls=%async_computation.11 | async-start | bytes 31457280 | tf_op jit(solution)/shard_map/all_gather | solution.py:168
  179.9 1222.9 %all-gather.24.cloned.1.call-start = ((), (), s32[]{:S(2)}) async-start(), calls=%async_computation.10 | async-start | bytes 31457280 | tf_op jit(solution)/shard_map/all_gather | solution.py:167
  180.6 1647.1 %all-gather.28.cloned.1.call-start = ((), (), s32[]{:S(2)}) async-start(), calls=%async_computation.12 | async-start | bytes 31457280 | tf_op jit(solution)/shard_map/all_gather | solution.py:174
  181.4 1795.2 %reduce-scatter.7.cloned.1.call-start = ((), (), s32[]{:S(2)}) async-start(), calls=%async_computation.13 | async-start | bytes 4718592 | tf_op jit(solution)/shard_map/reduce_scatter | solution.py:251
  182.1 160.1 %copy-start.52 = (f32[128]{0:T(128)}, f32[128]{0:T(128)S(1)}, u32[]{:S(2)}) copy-start(f32[128]{0:T(128)S(1)} %convert_element_type.146) | copy-start | bytes 1540
  345.5 33.1 copy-start.11
  347.4 31.2 copy-start.13
  361.8 16.8 copy-start.17
  378.7 22.9 copy-start.18
  420.8 137.8 %copy-start.33 = (bf16[256,8,2,128]{0,3,2,1:T(8,128)(2,1)}, bf16[256,8,2,128]{0,3,2,1:T(8,128)(2,1)S(1)}, u32[]{:S(2)}) copy-start(bf16[256,8,2,128]{0,3,2,1:T(8,128)(2,1)S(1)} %get-tuple-element.79) | copy-start | bytes 3145732
  560.2 842.5 %copy-start.9 = (bf16[256,2048]{1,0:T(8,128)(2,1)}, bf16[256,2048]{1,0:T(8,128)(2,1)S(1)}, u32[]{:S(2)}) copy-start(bf16[256,2048]{1,0:T(8,128)(2,1)S(1)} %multiply_convert_fusion.4) | copy-start | bytes 3145732
  993.6 834.1 %copy-start.26 = (bf16[1,256,2048]{2,1,0:T(8,128)(2,1)S(1)}, bf16[1,256,2048]{2,1,0:T(8,128)(2,1)}, u32[]{:S(2)}) copy-start(bf16[1,256,2048]{2,1,0:T(8,128)(2,1)} %param.16) | copy-start | bytes 3145732
  1892.0 22.9 copy-start.12
  1892.0 22.9 copy-start.14
  1925.6 104.8 %reduce-scatter.9.cloned.1.call-start = ((), (), s32[]{:S(2)}) async-start(), calls=%async_computation.14 | async-start | bytes 4718592 | tf_op jit(solution)/shard_map/reduce_scatter | solution.py:254
  1945.2 10.6 copy-start.30
  1945.2 10.6 copy-start.32
  1945.3 604.4 %reduce-scatter.13.cloned.1.call-start = ((), (), s32[]{:S(2)}) async-start(), calls=%async_computation.16 | async-start | bytes 51904512
  1960.0 8.4 copy-start.5
  1960.0 8.4 copy-start.34
  1968.4 9.5 copy-start.41
  1968.4 9.5 copy-start.51
  1979.1 4.7 copy-start.21
  2030.4 6.1 copy-start
  2117.1 1702.2 %reduce-scatter.11.cloned.1.call-start = ((), (), s32[]{:S(2)}) async-start(), calls=%async_computation.15 | async-start | bytes 155713536 | tf_op jit(solution)/shard_map/reduce_scatter | solution.py:195
  2118.3 32.1 copy-start.10
  2307.9 7.3 copy-start.20
  2315.2 13.8 copy-start.22
  2329.0 4.6 copy-start.3
  2329.0 4.6 copy-start.23
  2329.0 4.7 copy-start.28
  2329.0 4.7 copy-start.37
  2329.0 4.7 copy-start.44
  2333.7 3.0 copy-start.49
  2333.7 3.0 copy-start.54
  2333.7 43.9 %copy-start.6 = (f32[256,2048]{1,0:T(8,128)S(1)}, f32[256,2048]{1,0:T(8,128)}, u32[]{:S(2)}) copy-start(f32[256,2048]{1,0:T(8,128)} %copy-done.4) | copy-start | bytes 6291460
  (26 other events, 51.1 us)
Sparse Core Ops, SparseCore 0:
  9.6 83.4 all-gather.15
  94.7 79.2 all-gather.11
  175.6 148.2 all-gather.19
  326.2 35.6 all-gather.17
  364.1 37.4 all-gather.13
  403.0 149.6 all-gather.21
  554.3 423.3 all-gather.25
  979.3 423.3 all-gather.23
  1404.3 423.3 all-gather.27
  1925.8 49.4 reduce-scatter.6
  1979.0 51.3 reduce-scatter.8
  2117.2 432.4 reduce-scatter.12
  2556.1 1263.0 reduce-scatter.10
where the time goes:
time: 3840 us; the launch traced here: 3830 us
  waiting for transfers between devices  3140 us (82%)
  matrix products  351 us (9%)
  other arithmetic  167 us (4%)
  local copies, waits for them, and re-layouts  90 us (2%)
  blocking collectives  66.6 us (2%)
    reduce_scatter x1, waiting for transfers between devices, per_device(): lax.psum_scatter(jnp.concatenate([dot_tn(normalized_input, grad_gate), do...  1270 us
    all_gather x1, waiting for transfers between devices, per_device(): lax.all_gather(wu, 'fsdp', axis=0, tiled=True)  418 us
    all_gather x1, waiting for transfers between devices, per_device(): lax.all_gather(wd, 'fsdp', axis=0, tiled=True)  409 us
    all_gather x1, waiting for transfers between devices, per_device(): lax.all_gather(wg, 'fsdp', axis=0, tiled=True)  409 us
    unnamed x14, waiting for transfers between devices  173 us
    all_gather x1, waiting for transfers between devices, per_device(): branch_one = dot_nt(attn_bf, lax.all_gather(wo, 'fsdp', axis=0, tiled=True))  132 us
    all_gather x1, waiting for transfers between devices, per_device(): lax.all_gather(wq, 'fsdp', axis=0, tiled=True)  127 us
    dot_general x7, matrix products, dot_tn(): lax.dot_general(left, right, (((0,), (0,)), ((), ())), preferred_element_...  115 us
  transfers between devices with their start and end apart: 13, of which 12 were waited for; matrix products, arithmetic and copies ran while one was open for 11% of the time, Pallas kernels for 0%

commit v1 on v0

v1 whole, which is shorter than its diff:
```python
import functools
import math

import jax
import jax.numpy as jnp
from jax import lax
from jax.experimental import pallas as pl
from jax.experimental.pallas import tpu as pltpu
from jax.sharding import PartitionSpec as P

QUERY_HEADS = 16
KEY_VALUE_HEADS = 8
HEAD_SIZE = 128

epsilon = 1e-06
rope_base = 1000000.0
large_negative = -1e30

bf16 = jnp.bfloat16
f32 = jnp.float32
VMEM_LIMIT = 56 * 1024 * 1024


def dot_nn(left, right):
    return lax.dot_general(left, right, (((1,), (0,)), ((), ())), preferred_element_type=f32)


def dot_nt(left, right):
    return lax.dot_general(left, right, (((1,), (1,)), ((), ())), preferred_element_type=f32)


def dot_tn(left, right):
    return lax.dot_general(left, right, (((0,), (0,)), ((), ())), preferred_element_type=f32)


def rms_scale(values):
    return lax.rsqrt(jnp.mean(values * values, axis=-1, keepdims=True) + epsilon)


def swap(values, n, bits):
    return lax.ppermute(values, "ctx", [(c, c ^ bits) for c in range(n)])


def slot_order(n):
    return lax.axis_index("ctx") ^ jnp.arange(n, dtype=jnp.int32)


def gather_slots(rows, n):
    if n != 8:
        full = lax.all_gather(rows, "ctx", axis=0)
        return jnp.take(full, slot_order(n), axis=0)
    half = rows.shape[0] // 2
    from_x = swap(rows, n, 2)
    from_y = swap(rows, n, 4)
    from_s = swap(rows, n, 1)
    diag_a = swap(from_x[:half], n, 4)
    diag_b = swap(from_y[half:], n, 2)
    sib_x = swap(from_x, n, 1)
    sib_y = swap(from_y, n, 1)
    sib_a = swap(diag_a, n, 1)
    sib_b = swap(diag_b, n, 1)
    whole = jnp.concatenate(
        [rows, from_s, from_x, sib_x, from_y, sib_y, diag_a, diag_b, sib_a, sib_b], axis=0
    )
    return whole.reshape(n, rows.shape[0], rows.shape[1])


def scatter_slots(product, left, n):
    rows = left.shape[1]
    if n != 8:
        part = product(left.reshape(n * rows, -1)).astype(bf16)
        part = jnp.take(part.reshape(n, rows, -1), slot_order(n), axis=0)
        return lax.psum_scatter(part, "ctx", scatter_dimension=0, tiled=True)[0].astype(f32)
    half = rows // 2
    pairs = left.reshape(4, 2, rows, -1)
    odd = product(pairs[:, 1].reshape(4 * rows, -1)).astype(bf16).reshape(4, rows, -1)
    even = product(pairs[:, 0].reshape(4 * rows, -1)).astype(bf16).reshape(4, rows, -1)
    got = swap(odd, n, 1)
    total = even.astype(f32) + got.astype(f32)
    send_x = jnp.stack([total[1, :half], total[3, :half]]).astype(bf16)
    send_y = jnp.stack([total[2, half:], total[3, half:]]).astype(bf16)
    got_x = swap(send_x, n, 2).astype(f32)
    got_y = swap(send_y, n, 4).astype(f32)
    last_y = (total[2, :half] + got_x[1]).astype(bf16)
    last_x = (total[1, half:] + got_y[1]).astype(bf16)
    fin_y = swap(last_y, n, 4).astype(f32)
    fin_x = swap(last_x, n, 2).astype(f32)
    return jnp.concatenate(
        [total[0, :half] + got_x[0] + fin_y, total[0, half:] + got_y[0] + fin_x], axis=0
    )


def exchange_columns(blocks, n):
    if n != 8:
        got = lax.all_to_all(blocks, "ctx", 0, 0, tiled=True)
    else:
        order = slot_order(n)
        ordered = jnp.take(blocks, order, axis=0)
        got = jnp.stack([ordered[0]] + [swap(ordered[s], n, s) for s in range(1, n)])
        got = jnp.take(got, order, axis=0)
    return got


def reduce_rows(grad, n, n_fsdp):
    depth, width = grad.shape
    rows = depth // (n * n_fsdp)
    parts = grad.astype(bf16).reshape(n, n_fsdp, rows, width).transpose(1, 0, 2, 3)
    summed = lax.psum_scatter(
        parts.reshape(depth, width), "fsdp", scatter_dimension=0, tiled=True
    )
    return exchange_columns(summed.reshape(n, rows, width), n)


def join_columns(got):
    n, rows, width = got.shape
    return got.transpose(1, 0, 2).reshape(rows, n * width).astype(f32)


def project_kernel(
    heads, place_ref, x_ref, gain_ref, w_ref, qg_ref, kg_ref, cos_ref, sin_ref,
    xn_ref, qraw_ref, kraw_ref, qb_ref, kb_ref, vb_ref,
):
    slot = pl.program_id(0)
    x = x_ref[0].astype(f32)
    xn = (x * rms_scale(x) * gain_ref[...]).astype(bf16)
    xn_ref[0] = xn
    y = jnp.dot(xn, w_ref[...], preferred_element_type=f32)
    blk = x.shape[0] // 2
    for half in range(2):
        place = place_ref[2 * slot + half]
        at = pl.ds(pl.multiple_of(place * blk, blk), blk)
        cosine, sine = cos_ref[at, :], sin_ref[at, :]
        rows = y[half * blk : (half + 1) * blk]
        for head in range(heads + 1):
            raw = rows[:, head * HEAD_SIZE : (head + 1) * HEAD_SIZE]
            gain = (qg_ref if head < heads else kg_ref)[...]
            normed = raw * rms_scale(raw) * gain
            turned = normed * cosine + pltpu.roll(normed, HEAD_SIZE // 2, 1) * sine
            if head < heads:
                cols = slice(head * HEAD_SIZE, (head + 1) * HEAD_SIZE)
                qraw_ref[at, cols] = raw
                qb_ref[at, cols] = turned.astype(bf16)
            else:
                kraw_ref[at, :] = raw
                kb_ref[at, :] = turned.astype(bf16)
        vb_ref[at, :] = rows[:, (heads + 1) * HEAD_SIZE :].astype(bf16)


def project(x_slots, places, gain, w, q_gain, k_gain, cosine, sine, heads):
    n, rows, depth = x_slots.shape
    total = n * rows
    const = lambda i, p: (0, 0)
    whole = lambda a: pl.BlockSpec(a.shape, const)
    out = [
        jax.ShapeDtypeStruct((n, rows, depth), bf16),
        jax.ShapeDtypeStruct((total, heads * HEAD_SIZE), f32),
        jax.ShapeDtypeStruct((total, HEAD_SIZE), f32),
        jax.ShapeDtypeStruct((total, heads * HEAD_SIZE), bf16),
        jax.ShapeDtypeStruct((total, HEAD_SIZE), bf16),
        jax.ShapeDtypeStruct((total, HEAD_SIZE), bf16),
    ]
    args = (gain, w, q_gain, k_gain, cosine, sine)
    return pl.pallas_call(
        functools.partial(project_kernel, heads),
        grid_spec=pltpu.PrefetchScalarGridSpec(
            num_scalar_prefetch=1,
            grid=(n,),
            in_specs=[pl.BlockSpec((1, rows, depth), lambda i, p: (i, 0, 0))]
            + [whole(a) for a in args],
            out_specs=[pl.BlockSpec((1, rows, depth), lambda i, p: (i, 0, 0))]
            + [pl.BlockSpec(o.shape, const) for o in out[1:]],
        ),
        out_shape=out,
        compiler_params=pltpu.CompilerParams(
            dimension_semantics=("arbitrary",), vmem_limit_bytes=VMEM_LIMIT
        ),
        cost_estimate=pl.CostEstimate(
            flops=2 * total * depth * w.shape[1],
            bytes_accessed=4 * total * depth + 16 * total * HEAD_SIZE,
            transcendentals=total,
        ),
        name="project",
    )(places, x_slots, *args)


def attend_kernel(heads, tile, length_ref, place_ref, q_ref, k_ref, v_ref, o_ref, a_ref, lse_ref):
    total = q_ref.shape[0]
    blk = total // place_ref.shape[0]
    scale = 1.0 / math.sqrt(HEAD_SIZE)
    length = length_ref[0]
    key_tiles = (length + tile - 1) // tile

    def q_step(i, unused):
        q_at = pl.ds(pl.multiple_of(i * tile, tile), tile)
        q = [q_ref[q_at, h * HEAD_SIZE : (h + 1) * HEAD_SIZE] for h in range(heads)]

        def tile_step(j, carry, masked):
            k_at = pl.ds(pl.multiple_of(j * tile, tile), tile)
            k, v = k_ref[k_at, :], v_ref[k_at, :]
            if masked:
                key = j * tile + lax.broadcasted_iota(jnp.int32, (tile, tile), 0)
                query = i * tile + lax.broadcasted_iota(jnp.int32, (tile, tile), 1)
                allowed = (key <= query) & (key < length)
            new = []
            for h in range(heads):
                top, tot, out = carry[h]
                s = dot_nt(k, q[h]) * scale
                if masked:
                    s = jnp.where(allowed, s, large_negative)
                top_new = jnp.maximum(top, jnp.max(s, axis=0, keepdims=True))
                shrink = jnp.exp(top - top_new)
                p = jnp.exp(s - top_new)
                tot = tot * shrink + jnp.sum(p, axis=0, keepdims=True)
                out = out * shrink + dot_tn(v, p.astype(bf16))
                new.append((top_new, tot, out))
            return tuple(new)

        start = tuple(
            (
                jnp.full((1, tile), large_negative, f32),
                jnp.zeros((1, tile), f32),
                jnp.zeros((HEAD_SIZE, tile), f32),
            )
            for _ in range(heads)
        )
        full = jnp.minimum(i, length // tile)
        carry = lax.fori_loop(0, full, functools.partial(tile_step, masked=False), start)
        carry = lax.fori_loop(
            full, jnp.minimum(i + 1, key_tiles), functools.partial(tile_step, masked=True), carry
        )
        for h in range(heads):
            top, tot, out = carry[h]
            lse_ref[pl.ds(h, 1), q_at] = top + jnp.log(tot)
            o = jnp.transpose(out / tot)
            cols = slice(h * HEAD_SIZE, (h + 1) * HEAD_SIZE)
            o_ref[q_at, cols] = o
        return unused

    lax.fori_loop(0, total // tile, q_step, 0)

    def place_step(b, unused):
        src = pl.ds(pl.multiple_of(place_ref[b] * blk, blk), blk)
        dst = pl.ds(pl.multiple_of(b * blk, blk), blk)
        a_ref[dst, :] = o_ref[src, :].astype(bf16)
        return unused

    lax.fori_loop(0, place_ref.shape[0], place_step, 0)


def attend(length, places, q, k, v, heads):
    total = q.shape[0]
    tile = min(512, total)
    vm = lambda: pl.BlockSpec(memory_space=pltpu.VMEM)
    sm = lambda: pl.BlockSpec(memory_space=pltpu.SMEM)
    return pl.pallas_call(
        functools.partial(attend_kernel, heads, tile),
        in_specs=[sm(), sm(), vm(), vm(), vm()],
        out_specs=[vm(), vm(), vm()],
        out_shape=[
            jax.ShapeDtypeStruct((total, heads * HEAD_SIZE), f32),
            jax.ShapeDtypeStruct((total, heads * HEAD_SIZE), bf16),
            jax.ShapeDtypeStruct((heads, total), f32),
        ],
        compiler_params=pltpu.CompilerParams(vmem_limit_bytes=VMEM_LIMIT),
        cost_estimate=pl.CostEstimate(
            flops=2 * heads * total * total * HEAD_SIZE,
            bytes_accessed=12 * total * heads * HEAD_SIZE,
            transcendentals=heads * total * total // 2,
        ),
        name="attend",
    )(length, places, q, k, v)


def unturn(grad, raw, gain, cosine, sine):
    grad = grad * cosine - pltpu.roll(grad, HEAD_SIZE // 2, 1) * sine
    scale = rms_scale(raw)
    hat = raw * scale
    inner = grad * gain
    out = scale * (inner - hat * jnp.mean(inner * hat, axis=-1, keepdims=True))
    return out, jnp.sum(grad * hat, axis=0, keepdims=True)


def attend_back_kernel(
    heads, tile, finish_keys, length_ref, place_ref, q_ref, k_ref, v_ref, da_ref, o_ref, lse_ref,
    qraw_ref, kraw_ref, qg_ref, kg_ref, cos_ref, sin_ref,
    d_ref, dqg_ref, dkg_ref, *rest,
):
    if finish_keys:
        da_s, delta_s, dq_s, dk_s, dv_s = rest
    else:
        dk_s, dv_s, da_s, delta_s, dq_s = rest
    total = q_ref.shape[0]
    blocks = place_ref.shape[0]
    blk = total // blocks
    scale = 1.0 / math.sqrt(HEAD_SIZE)
    length = length_ref[0]
    tiles = total // tile

    def sort_step(b, unused):
        dst = pl.ds(pl.multiple_of(place_ref[b] * blk, blk), blk)
        src = pl.ds(pl.multiple_of(b * blk, blk), blk)
        piece = da_ref[src, :]
        da_s[dst, :] = piece
        prod = piece.astype(f32) * o_ref[dst, :]
        for h in range(heads):
            cols = slice(h * HEAD_SIZE, (h + 1) * HEAD_SIZE)
            delta_s[pl.ds(h, 1), dst] = jnp.sum(jnp.transpose(prod[:, cols]), axis=0, keepdims=True)
        return unused

    lax.fori_loop(0, blocks, sort_step, 0)
    dq_s[...] = jnp.zeros_like(dq_s)
    dk_s[...] = jnp.zeros_like(dk_s)
    dv_s[...] = jnp.zeros_like(dv_s)

    def k_step(j, unused):
        k_at = pl.ds(pl.multiple_of(j * tile, tile), tile)
        k, v = k_ref[k_at, :], v_ref[k_at, :]

        def tile_step(i, carry, masked):
            dk, dv = carry
            q_at = pl.ds(pl.multiple_of(i * tile, tile), tile)
            if masked:
                key = j * tile + lax.broadcasted_iota(jnp.int32, (tile, tile), 0)
                query = i * tile + lax.broadcasted_iota(jnp.int32, (tile, tile), 1)
                allowed = (key <= query) & (key < length)
            for h in range(heads):
                cols = slice(h * HEAD_SIZE, (h + 1) * HEAD_SIZE)
                q, da = q_ref[q_at, cols], da_s[q_at, cols]
                s = dot_nt(k, q) * scale - lse_ref[pl.ds(h, 1), q_at]
                if masked:
                    s = jnp.where(allowed, s, large_negative)
                p = jnp.exp(s)
                dp = dot_nt(v, da)
                ds = (p * (dp - delta_s[pl.ds(h, 1), q_at])).astype(bf16)
                dv = dv + dot_nn(p.astype(bf16), da)
                dk = dk + dot_nn(ds, q)
                dq_s[q_at, cols] += dot_tn(ds, k)
            return dk, dv

        zero = jnp.zeros((tile, HEAD_SIZE), f32)
        carry = (zero, zero)
        whole_tile = (j + 1) * tile <= length
        carry = lax.fori_loop(j, j + 1, functools.partial(tile_step, masked=True), carry)
        first_full = jnp.where(whole_tile, j + 1, tiles)
        carry = lax.fori_loop(
            j + 1, first_full, functools.partial(tile_step, masked=True), carry
        )
        carry = lax.fori_loop(first_full, tiles, functools.partial(tile_step, masked=False), carry)
        dk_s[k_at, :], dv_s[k_at, :] = carry[0] * scale, carry[1]
        return unused

    lax.fori_loop(0, (length + tile - 1) // tile, k_step, 0)

    dqg_ref[...] = jnp.zeros_like(dqg_ref)
    dkg_ref[...] = jnp.zeros_like(dkg_ref)

    def last_step(b, unused):
        src = pl.ds(pl.multiple_of(place_ref[b] * blk, blk), blk)
        dst = pl.ds(pl.multiple_of(b * blk, blk), blk)
        cosine, sine = cos_ref[src, :], sin_ref[src, :]
        for h in range(heads):
            cols = slice(h * HEAD_SIZE, (h + 1) * HEAD_SIZE)
            grad = (dq_s[src, cols] * scale).astype(bf16).astype(f32)
            out, gain = unturn(grad, qraw_ref[src, cols], qg_ref[...], cosine, sine)
            d_ref[dst, cols] = out.astype(bf16)
            dqg_ref[...] += gain
        if finish_keys:
            grad = dk_s[src, :].astype(bf16).astype(f32)
            out, gain = unturn(grad, kraw_ref[src, :], kg_ref[...], cosine, sine)
            d_ref[dst, heads * HEAD_SIZE : (heads + 1) * HEAD_SIZE] = out.astype(bf16)
            dkg_ref[...] += gain
            d_ref[dst, (heads + 1) * HEAD_SIZE :] = dv_s[src, :].astype(bf16)
        return unused

    lax.fori_loop(0, blocks, last_step, 0)


def attend_back(length, places, q, k, v, da, o, lse, qraw, kraw, qg, kg, cosine, sine, heads):
    total = q.shape[0]
    tile = min(512, total)
    vm = lambda: pl.BlockSpec(memory_space=pltpu.VMEM)
    sm = lambda: pl.BlockSpec(memory_space=pltpu.SMEM)
    return pl.pallas_call(
        functools.partial(attend_back_kernel, heads, tile, True),
        in_specs=[sm(), sm()] + [vm() for _ in range(12)],
        out_specs=[vm(), vm(), vm()],
        out_shape=[
            jax.ShapeDtypeStruct((total, (heads + 2) * HEAD_SIZE), bf16),
            jax.ShapeDtypeStruct((1, HEAD_SIZE), f32),
            jax.ShapeDtypeStruct((1, HEAD_SIZE), f32),
        ],
        scratch_shapes=[
            pltpu.VMEM((total, heads * HEAD_SIZE), bf16),
            pltpu.VMEM((heads, total), f32),
            pltpu.VMEM((total, heads * HEAD_SIZE), f32),
            pltpu.VMEM((total, HEAD_SIZE), f32),
            pltpu.VMEM((total, HEAD_SIZE), f32),
        ],
        compiler_params=pltpu.CompilerParams(vmem_limit_bytes=VMEM_LIMIT),
        cost_estimate=pl.CostEstimate(
            flops=5 * heads * total * total * HEAD_SIZE,
            bytes_accessed=24 * total * heads * HEAD_SIZE,
            transcendentals=heads * total * total // 2,
        ),
        name="attend_back",
    )(length, places, q, k, v, da, o, lse, qraw, kraw, qg, kg, cosine, sine)


def per_device(
    n, n_fsdp, layer_input, dy, block_order, lengths, attn_gain, wq, wk, wv, q_gain, k_gain, wo,
    mlp_gain, wg, wu, wd,
):
    me = lax.axis_index("ctx")
    rows = layer_input.shape[1]
    blk = rows // 2
    depth = layer_input.shape[2]
    shard = wq.shape[0]
    heads = QUERY_HEADS // n
    kv_share = n // KEY_VALUE_HEADS
    ff = wg.shape[1] // n
    q_cols = heads * HEAD_SIZE

    def cols(w, width, index):
        return lax.dynamic_slice_in_dim(w, index * width, width, axis=1)

    def whole(w):
        return lax.all_gather(w, "fsdp", axis=0, tiled=True)

    kv_index = me // kv_share
    w_in = jnp.concatenate(
        [cols(wq, q_cols, me), cols(wk, HEAD_SIZE, kv_index), cols(wv, HEAD_SIZE, kv_index)], axis=1
    )
    width = w_in.shape[1]
    gains = jnp.concatenate([attn_gain, mlp_gain])
    gain_rows = -(-gains.shape[0] // (16 * width)) * 16
    gains = jnp.pad(gains, (0, gain_rows * width - gains.shape[0])).reshape(gain_rows, width)
    pack = lax.all_gather(jnp.concatenate([w_in, gains], axis=0), "fsdp", axis=0)
    w_in = pack[:, :shard].reshape(n_fsdp * shard, width)
    gains = pack[:, shard:].reshape(n_fsdp, -1)
    attn_gain = gains[:, :shard].reshape(1, depth).astype(f32)
    mlp_gain = gains[:, shard : 2 * shard].reshape(1, depth).astype(f32)
    wo_c = whole(cols(wo, q_cols, me))
    wg_c = whole(cols(wg, ff, me))
    wu_c = whole(cols(wu, ff, me))
    wd_c = whole(cols(wd, ff, me))

    places = jnp.take(block_order, slot_order(n), axis=0).reshape(-1)
    half = HEAD_SIZE // 2
    lane = jnp.arange(HEAD_SIZE, dtype=jnp.int32)
    frequency = jnp.exp(-math.log(rope_base) * 2.0 * (lane % half).astype(f32) / HEAD_SIZE)
    angle = jnp.arange(n * rows, dtype=f32)[:, None] * frequency[None, :]
    cosine = jnp.cos(angle)
    sine = jnp.sin(angle) * jnp.where(lane < half, -1.0, 1.0)[None, :]
    qg = q_gain.astype(f32).reshape(1, HEAD_SIZE)
    kg = k_gain.astype(f32).reshape(1, HEAD_SIZE)

    x_slots = gather_slots(layer_input[0], n)
    dy_slots = gather_slots(dy[0], n)
    xn, q_raw, k_raw, qb, kb, vb = project(
        x_slots, places, attn_gain, w_in, qg, kg, cosine, sine, heads
    )
    o, a, lse = attend(lengths, places, qb, kb, vb, heads)
    z = scatter_slots(lambda v: dot_nt(v, wo_c), a.reshape(n, rows, q_cols), n)

    x = layer_input[0].astype(f32)
    h1 = x + z
    scale_two = rms_scale(h1)
    hat_two = h1 * scale_two
    xn2 = gather_slots((hat_two * mlp_gain).astype(bf16), n).reshape(n * rows, depth)
    gate = dot_nn(xn2, wg_c)
    up = dot_nn(xn2, wu_c)
    sigma = jax.nn.sigmoid(gate)
    silu = gate * sigma
    hm = (silu * up).astype(bf16)
    m = scatter_slots(lambda v: dot_nt(v, wd_c), hm.reshape(n, rows, ff), n)
    output = (h1 + m).astype(bf16)

    dy_all = dy_slots.reshape(n * rows, depth)
    d_wd = reduce_rows(dot_tn(dy_all, hm), n, n_fsdp)
    d_hm = dot_nn(dy_all, wd_c)
    d_gate = (d_hm * up * sigma * (1.0 + gate * (1.0 - sigma))).astype(bf16)
    d_up = (d_hm * silu).astype(bf16)
    d_gu = jnp.concatenate([d_gate, d_up], axis=1).reshape(n, rows, 2 * ff)
    d_xn2 = scatter_slots(lambda v: dot_nt(v[:, :ff], wg_c) + dot_nt(v[:, ff:], wu_c), d_gu, n)
    d_wg = reduce_rows(dot_tn(xn2, d_gate), n, n_fsdp)
    d_wu = reduce_rows(dot_tn(xn2, d_up), n, n_fsdp)
    d_mlp_gain = jnp.sum(d_xn2 * hat_two, axis=0)
    e = d_xn2 * mlp_gain
    d_h1 = dy[0].astype(f32) + scale_two * (
        e - hat_two * jnp.mean(e * hat_two, axis=-1, keepdims=True)
    )

    dz = gather_slots(d_h1.astype(bf16), n).reshape(n * rows, depth)
    da = dot_nn(dz, wo_c).astype(bf16)
    d_wo = reduce_rows(dot_tn(dz, a), n, n_fsdp)
    d_qkv, d_qg, d_kg = attend_back(
        lengths, places, qb, kb, vb, da, o, lse, q_raw, k_raw, qg, kg, cosine, sine, heads
    )
    d_xn = scatter_slots(lambda v: dot_nt(v, w_in), d_qkv.reshape(n, rows, width), n)
    d_win = reduce_rows(dot_tn(xn.reshape(n * rows, depth), d_qkv), n, n_fsdp)
    scale_one = rms_scale(x)
    hat_one = x * scale_one
    d_attn_gain = jnp.sum(d_xn * hat_one, axis=0)
    e = d_xn * attn_gain
    dx = d_h1 + scale_one * (e - hat_one * jnp.mean(e * hat_one, axis=-1, keepdims=True))

    sums = lax.psum(
        jnp.concatenate([d_attn_gain, d_mlp_gain, d_qg[0], d_kg[0]]), ("ctx", "fsdp")
    )
    kv = d_win[:: max(kv_share, 1)]
    return (
        output[None],
        dx[None],
        join_columns(d_win[:, :, :q_cols]),
        join_columns(kv[:, :, q_cols : q_cols + HEAD_SIZE]),
        join_columns(kv[:, :, q_cols + HEAD_SIZE :]),
        join_columns(d_wo),
        join_columns(d_wg),
        join_columns(d_wu),
        join_columns(d_wd),
        sums[:depth],
        sums[depth : 2 * depth],
        sums[2 * depth : 2 * depth + HEAD_SIZE],
        sums[2 * depth + HEAD_SIZE :],
    )


def solution(mesh):
    n, n_fsdp = mesh.shape["ctx"], mesh.shape["fsdp"]
    row, act = P("fsdp", None), P("fsdp", "ctx", None)
    own = P(("ctx", "fsdp"), None)
    return jax.shard_map(
        functools.partial(per_device, n, n_fsdp),
        mesh=mesh,
        in_specs=(
            act, act, P(), P("fsdp"), P("fsdp"), row, row, row, P(), P(), row, P("fsdp"), row, row, row,
        ),
        out_specs=(act, act) + (own,) * 7 + (P(),) * 4,
        check_vma=False,
    )
```

time: 3840 us -> 837 us (0.22)
  waiting for transfers between devices: 3140 us -> 289 us
  matrix products: 351 us -> 143 us
  other arithmetic: 167 us -> 82 us
  starting transfers between devices: 0.69 us -> 67.9 us
  Pallas kernels: 0 us -> 57.2 us
  local copies, waits for them, and re-layouts: 90 us -> 135 us
    all_gather x9 -> x5, waiting for transfers between devices: 1650 us -> 24.6 us  [the longest x4 24.6 us: whole(): return lax.all_gather(w, 'fsdp', axis=0, tiled=True)]
    reduce_scatter x3 -> x5, waiting for transfers between devices: 1310 us -> 35.2 us  [reduce_rows(): lax.psum_scatter(parts.reshape(depth, width), 'fsdp', scatter_dimension=0...]
    ppermute x0 -> x91, waiting for transfers between devices: none -> 229 us  [swap(): return lax.ppermute(values, 'ctx', [(c, c ^ bits) for c in range(n)])]
    unnamed x14 -> x10, waiting for transfers between devices: 173 us -> 0.16 us
    concatenate x3 -> x5, other arithmetic: 133 us -> 6.85 us  [the longest x1 3.31 us: per_device(): d_gu = jnp.concatenate([d_gate, d_up], axis=1).reshape(n, rows, 2 * ff)]
    dot_general x13 -> x4, matrix products: 172 us -> 46.6 us  [dot_nn(): lax.dot_general(left, right, (((1,), (0,)), ((), ())), preferred_element_...]
    dot_general x7 -> x5, matrix products: 115 us -> 39.3 us  [dot_tn(): lax.dot_general(left, right, (((0,), (0,)), ((), ())), preferred_element_...]
    ppermute x0 -> x91, starting transfers between devices: none -> 66.9 us  [swap(): return lax.ppermute(values, 'ctx', [(c, c ^ bits) for c in range(n)])]
  transfers between devices with their start and end apart: 13 -> 101, of which waited for: 12 -> 43; matrix products, arithmetic and copies ran while one was open for 11% -> 37% of each run, Pallas kernels for 0% -> 7%
where the time goes in v1:
time: 837 us; the launch traced here: 829 us
  waiting for transfers between devices  289 us (35%)
  matrix products  143 us (17%)
  local copies, waits for them, and re-layouts  135 us (16%)
  other arithmetic  82 us (10%)
  starting transfers between devices  67.9 us (8%)
  Pallas kernels  57.2 us (7%)
  blocking collectives  38.7 us (5%)
  between operations  16.3 us (2%)
    ppermute x91, waiting for transfers between devices, swap(): return lax.ppermute(values, 'ctx', [(c, c ^ bits) for c in range(n)])  229 us
    ppermute x91, starting transfers between devices, swap(): return lax.ppermute(values, 'ctx', [(c, c ^ bits) for c in range(n)])  66.9 us
    unnamed x180, local copies, waits for them, and re-layouts  59.3 us
    dot_general x10, matrix products, dot_nt(): lax.dot_general(left, right, (((1,), (1,)), ((), ())), preferred_element_...  56.7 us
    dot_general x4, matrix products, dot_nn(): lax.dot_general(left, right, (((1,), (0,)), ((), ())), preferred_element_...  46.6 us
    dot_general x5, matrix products, dot_tn(): lax.dot_general(left, right, (((0,), (0,)), ((), ())), preferred_element_...  39.3 us
    psum x1, blocking collectives, per_device(): lax.psum(jnp.concatenate([d_attn_gain, d_mlp_gain, d_qg[0], d_kg[0]]), ('...  38.7 us
    reduce_scatter x5, waiting for transfers between devices, reduce_rows(): lax.psum_scatter(parts.reshape(depth, width), 'fsdp', scatter_dimension=0...  35.2 us
  transfers between devices with their start and end apart: 101, of which 43 were waited for; matrix products, arithmetic and copies ran while one was open for 37% of the time, Pallas kernels for 7%

profile of v1, /device:TPU:0, one launch (start us, length us, event | category | flops | bytes accessed | tf_op | source)
XLA Modules:
  0.0 828.7 jit_solution(15787907716989780369)
XLA Ops:
  19.4 4.8 sine_multiply_fusion
  25.8 14.6 %collective-permute-done.1 = bf16[256,2048]{1,0:T(8,128)(2,1)S(1)} collective-permute-done((bf16[256,2048]{1,0:T(8,128)(2,1)}, bf16[256,2048]{1,0:T(8,128)(2,1)S(1)}, u32[]{:S(2)}, u32[]{:S(2)}) %collective-permute-start.1) | collective-permute-done | bytes 1048608 | tf_op jit(solution)/shard_map/ppermute | solution.py:41
  50.1 6.5 collective-permute-done.6
  75.0 16.6 %project.1 = (bf16[8,256,2048]{2,1,0:T(8,128)(2,1)}, f32[2048,256]{1,0:T(8,128)}, f32[2048,128]{1,0:T(8,128)}, bf16[2048,256]{1,0:T(8,128)(2,1)}, bf16[2048,128]{1,0:T(8,128)(2,1)}, /*index=5*/bf16[2048,128]{1,0:T(8,128)(2,1)}) custom-call(s32[16]{0:T(128)} %select_n.87.place_ref, bf16[8,256,2048]{2,1,0:T(8,128)(2,1)} %bitcast.427, f32[1,2048]{1,0:T(1,128)} %bitcast.435, ...), custom_call_target="tpu_custom_call" | custom-call | flops 4294967296 | bytes 20971520 | tf_op jit(solution)/shard_map/project/pallas_call | solution.py:163
  91.6 14.4 %attend.1 = (f32[2048,256]{1,0:T(8,128)}, bf16[2048,256]{1,0:T(8,128)(2,1)}, f32[2,2048]{1,0:T(2,128)}) custom-call(s32[1]{0:T(128)S(6)} %copy.141.length_ref, s32[16]{0:T(128)} %select_n.87.place_ref, bf16[2048,256]{1,0:T(8,128)(2,1)} %get-tuple-element.28.q_ref, bf16[2048,128]{1,0:T(8,128)(2,1)} %get-tuple-element.29.k_ref, ...), custom_call_target="tpu_custom_call" | custom-call | flops 2147483648 | bytes 6291456 | tf_op jit(solution)/shard_map/attend/pallas_call | solution.py:255
  108.3 4.9 convolution_convert_fusion.2
  120.8 7.7 convert_add_fusion.3
  134.8 7.7 collective-permute-done.31
  147.1 18.4 %collective-permute-done.10 = bf16[2,128,2048]{2,1,0:T(8,128)(2,1)S(1)} collective-permute-done((bf16[2,128,2048]{2,1,0:T(8,128)(2,1)}, bf16[2,128,2048]{2,1,0:T(8,128)(2,1)S(1)}, u32[]{:S(2)}, u32[]{:S(2)}) %collective-permute-start.10) | collective-permute-done | bytes 1048608 | tf_op jit(solution)/shard_map/ppermute | solution.py:41
  172.5 4.2 collective-permute-done.34
  178.8 7.6 collective-permute-done.11
  193.3 21.8 %collective-permute-done.17 = bf16[256,2048]{1,0:T(8,128)(2,1)S(1)} collective-permute-done((bf16[256,2048]{1,0:T(8,128)(2,1)}, bf16[256,2048]{1,0:T(8,128)(2,1)S(1)}, u32[]{:S(2)}, u32[]{:S(2)}) %collective-permute-start.17) | collective-permute-done | bytes 1048608 | tf_op jit(solution)/shard_map/ppermute | solution.py:41
  219.3 11.8 %fusion.77 = f32[2048,768]{1,0:T(8,128)} fusion(bf16[2048,2048]{1,0:T(8,128)(2,1)} %copy-done.25, bf16[2048,768]{1,0:T(8,128)(2,1)} %all-gather.13.cloned.1.call-done), kind=kOutput, calls=%fused_computation.306 | convolution fusion | flops 6442450944 | bytes 17825792 | tf_op jit(solution)/shard_map/dot_general | solution.py:25
  245.1 11.6 %fusion.76 = f32[2048,768]{1,0:T(8,128)} fusion(bf16[2048,2048]{1,0:T(8,128)(2,1)} %constant_dynamic-update-slice_fusion.10, bf16[2048,768]{1,0:T(8,128)(2,1)} %all-gather.11.cloned.1.call-done), kind=kOutput, calls=%fused_computation.305 | convolution fusion | flops 6442450944 | bytes 17825792 | tf_op jit(solution)/shard_map/dot_general | solution.py:25
  256.8 24.6 %all-gather.9.cloned.1.call-done = bf16[2048,768]{1,0:T(8,128)(2,1)} async-done(((bf16[512,768]{1,0:T(8,128)(2,1)}), bf16[2048,768]{1,0:T(8,128)(2,1)}) %all-gather.9.cloned.1.call-update) | async-done | bytes 3145744 | tf_op jit(solution)/shard_map/all_gather | solution.py:427
  281.4 16.5 %multiply_convert_fusion.1 = (bf16[2048,768]{1,0:T(8,128)(2,1)}, bf16[2048,768]{1,0:T(8,128)(2,1)}, bf16[2048,768]{1,0:T(8,128)(2,1)S(1)}) fusion(f32[2048,768]{1,0:T(8,128)} %fusion.77, f32[2048,768]{1,0:T(8,128)} %fusion.76, bf16[2048,2048]{1,0:T(8,128)(2,1)} %constant_dynamic-update-slice_fusion.10, bf16[2048,768]{1,0:T(8,128)(2,1)} %all-gather.9.cloned.1.call-done), kind=kOutput, calls=%fused_computation.19 | convolution fusion | flops 6466043904 | bytes 33554432 | tf_op jit(solution)/shard_map/dot_general | solution.py:25
  297.9 10.5 %convolution_convert_fusion.6 = bf16[2048,768]{1,0:T(8,128)(2,1)S(1)} fusion(bf16[2048,2048]{1,0:T(8,128)(2,1)} %copy-done.25, bf16[2048,768]{1,0:T(8,128)(2,1)S(1)} %get-tuple-element.51), kind=kOutput, calls=%fused_computation.29 | convolution fusion | flops 6444023808 | bytes 14680064 | tf_op jit(solution)/shard_map/dot_general | solution.py:33
  310.4 10.2 %convolution_convert_fusion.7 = bf16[2048,768]{1,0:T(8,128)(2,1)S(1)} fusion(bf16[2048,2048]{1,0:T(8,128)(2,1)} %constant_dynamic-update-slice_fusion.10, bf16[2048,768]{1,0:T(8,128)(2,1)} %get-tuple-element.50), kind=kOutput, calls=%fused_computation.30 | convolution fusion | flops 6444023808 | bytes 14680064 | tf_op jit(solution)/shard_map/dot_general | solution.py:33
  329.0 6.1 fusion.15
  335.1 7.5 add_convert_fusion
  342.6 7.4 convolution_convert_fusion.8
  354.2 5.0 convolution_convert_fusion.4
  359.8 7.1 convolution_convert_fusion.5
  367.0 5.7 fusion.18
  372.7 6.1 add_convert_fusion.1
  378.8 7.6 convert_add_fusion.1
  389.7 8.0 convert_add_fusion.2
  401.8 11.0 %collective-permute-done.38 = bf16[2,128,2048]{2,1,0:T(8,128)(2,1)S(1)} collective-permute-done((bf16[2,128,2048]{2,1,0:T(8,128)(2,1)S(1)}, bf16[2,128,2048]{2,1,0:T(8,128)(2,1)S(1)}, u32[]{:S(2)}, u32[]{:S(2)}) %collective-permute-start.38) | collective-permute-done | bytes 1048608 | tf_op jit(solution)/shard_map/ppermute | solution.py:41
  418.5 16.8 %collective-permute-done.24 = bf16[2,128,2048]{2,1,0:T(8,128)(2,1)S(1)} collective-permute-done((bf16[2,128,2048]{2,1,0:T(8,128)(2,1)S(1)}, bf16[2,128,2048]{2,1,0:T(8,128)(2,1)S(1)}, u32[]{:S(2)}, u32[]{:S(2)}) %collective-permute-start.24) | collective-permute-done | bytes 1048608 | tf_op jit(solution)/shard_map/ppermute | solution.py:41
  439.5 8.5 %collective-permute-done.39 = bf16[128,2048]{1,0:T(8,128)(2,1)S(1)} collective-permute-done((bf16[128,2048]{1,0:T(8,128)(2,1)S(1)}, bf16[128,2048]{1,0:T(8,128)(2,1)S(1)}, u32[]{:S(2)}, u32[]{:S(2)}) %collective-permute-start.39) | collective-permute-done | bytes 524320 | tf_op jit(solution)/shard_map/ppermute | solution.py:41
  468.8 25.9 %reduce-scatter.10.cloned.1.call-done = bf16[512,768]{1,0:T(8,128)(2,1)} async-done(((bf16[2048,768]{1,0:T(8,128)(2,1)}), bf16[512,768]{1,0:T(8,128)(2,1)}) %reduce-scatter.10.cloned.1.call-update) | async-done | bytes 786448 | tf_op jit(solution)/shard_map/reduce_scatter | solution.py:108
  515.9 4.1 collective-permute-done.88
  529.9 4.6 collective-permute-done.78
  534.5 4.8 collective-permute-done.79
  544.0 4.4 collective-permute-done.81
  549.8 4.1 collective-permute-done.82
  591.2 5.1 collective-permute-done.48
  605.8 6.7 convolution_convert_fusion.11.da_ref
  612.5 26.1 %attend_back.1 = (bf16[2048,512]{1,0:T(8,128)(2,1)}, f32[1,128]{1,0:T(1,128)}, f32[1,128]{1,0:T(1,128)}) custom-call(s32[1]{0:T(128)S(6)} %copy.141.length_ref, s32[16]{0:T(128)} %select_n.87.place_ref, bf16[2048,256]{1,0:T(8,128)(2,1)} %get-tuple-element.28.q_ref, bf16[2048,128]{1,0:T(8,128)(2,1)} %get-tuple-element.29.k_ref, ...), custom_call_target="tpu_custom_call" | custom-call | flops 5368709120 | bytes 12582912 | tf_op jit(solution)/shard_map/attend_back/pallas_call | solution.py:383
  638.6 8.5 %convolution_convert_fusion.9 = bf16[2048,512]{1,0:T(8,128)(2,1)S(1)} fusion(bf16[2048,2048]{1,0:T(8,128)(2,1)} %bitcast.438, bf16[2048,512]{1,0:T(8,128)(2,1)} %get-tuple-element.36), kind=kOutput, calls=%fused_computation.35 | convolution fusion | flops 4296015872 | bytes 12582912 | tf_op jit(solution)/shard_map/dot_general | solution.py:33
  651.1 5.6 convolution_convert_fusion
  668.2 6.3 convolution_convert_fusion.1
  691.4 9.3 %reduce-scatter.6.cloned.1.call-done = bf16[512,512]{1,0:T(8,128)(2,1)} async-done(((bf16[2048,512]{1,0:T(8,128)(2,1)}), bf16[512,512]{1,0:T(8,128)(2,1)}) %reduce-scatter.6.cloned.1.call-update) | async-done | bytes 524304 | tf_op jit(solution)/shard_map/reduce_scatter | solution.py:108
  708.5 9.0 %convert_add_fusion = (f32[4,256,2048]{2,1,0:T(8,128)}, bf16[4,256,2048]{2,1,0:T(8,128)(2,1)S(1)}) fusion(bf16[4,256,2048]{2,1,0:T(8,128)(2,1)} %bitcast.384, bf16[4,256,2048]{2,1,0:T(8,128)(2,1)} %collective-permute-done.51), kind=kLoop, calls=%fused_computation.11 | loop fusion | flops 8388608 | bytes 20971520 | tf_op jit(solution)/shard_map/add | solution.py:79
  727.4 22.0 %collective-permute-done.60 = bf16[64,512]{1,0:T(8,128)(2,1)S(1)} collective-permute-done((bf16[64,512]{1,0:T(8,128)(2,1)S(1)}, bf16[64,512]{1,0:T(8,128)(2,1)S(1)}, u32[]{:S(2)}, u32[]{:S(2)}) %collective-permute-start.60) | collective-permute-done | bytes 65568 | tf_op jit(solution)/shard_map/ppermute | solution.py:41
  761.7 9.1 %collective-permute-done.53 = bf16[128,2048]{1,0:T(8,128)(2,1)S(1)} collective-permute-done((bf16[128,2048]{1,0:T(8,128)(2,1)S(1)}, bf16[128,2048]{1,0:T(8,128)(2,1)S(1)}, u32[]{:S(2)}, u32[]{:S(2)}) %collective-permute-start.53) | collective-permute-done | bytes 524320 | tf_op jit(solution)/shard_map/ppermute | solution.py:41
  776.1 38.7 %psum.7 = f32[4352]{0:T(1024)S(1)} all-reduce(f32[4352]{0:T(1024)S(1)} %pad_maximum_fusion.8), channel_id=1, replica_groups=mesh['ctx'=8,'fsdp'=4] {'ctx','fsdp'}, use_global_device_ids=true, to_apply=%region_11.15 | all-reduce | flops 4352 | bytes 34816 | tf_op jit(solution)/shard_map/psum | solution.py:507
  815.9 5.7 fusion.8
  (494 shorter events, 301.0 us)
Async XLA Ops:
  7.2 62.6 %all-gather.15.cloned.1.call-start = ((), (), s32[]{:S(2)}) async-start(), calls=%async_computation.14 | async-start | bytes 2703360 | tf_op jit(solution)/shard_map/all_gather | solution.py:437
  10.7 97.5 %all-gather.7.cloned.1.call-start = ((), (), s32[]{:S(2)}) async-start(), calls=%async_computation.5 | async-start | bytes 1310720 | tf_op jit(solution)/shard_map/all_gather | solution.py:427
  12.5 206.8 %all-gather.13.cloned.1.call-start = ((), (), s32[]{:S(2)}) async-start(), calls=%async_computation.8 | async-start | bytes 3932160 | tf_op jit(solution)/shard_map/all_gather | solution.py:427
  12.5 28.5 %collective-permute-start.3 = (bf16[256,2048]{1,0:T(8,128)(2,1)}, bf16[256,2048]{1,0:T(8,128)(2,1)S(1)}, u32[]{:S(2)}, u32[]{:S(2)}) collective-permute-start(bf16[256,2048]{1,0:T(8,128)(2,1)} %bitcast.366), channel_id=1, source_target_pairs={{0,16},{4,20},{8,24},{12,28},{16,0},{20,4},{24,8},{28,12},{1,17},{... | collective-permute-start | bytes 3145736 | tf_op jit(solution)/shard_map/ppermute | solution.py:41
  15.6 24.8 %collective-permute-start.1 = (bf16[256,2048]{1,0:T(8,128)(2,1)}, bf16[256,2048]{1,0:T(8,128)(2,1)S(1)}, u32[]{:S(2)}, u32[]{:S(2)}) collective-permute-start(bf16[256,2048]{1,0:T(8,128)(2,1)} %bitcast.367), channel_id=1, source_target_pairs={{0,8},{4,12},{8,0},{12,4},{16,24},{20,28},{24,16},{28,20},{1,9},{5... | collective-permute-start | bytes 3145736 | tf_op jit(solution)/shard_map/ppermute | solution.py:41
  17.1 29.5 %collective-permute-start = (bf16[256,2048]{1,0:T(8,128)(2,1)}, bf16[256,2048]{1,0:T(8,128)(2,1)}, u32[]{:S(2)}, u32[]{:S(2)}) collective-permute-start(bf16[256,2048]{1,0:T(8,128)(2,1)} %bitcast.368), channel_id=1, source_target_pairs={{0,4},{4,0},{8,12},{12,8},{16,20},{20,16},{24,28},{28,24},{1,5},{5... | collective-permute-start | bytes 3145736 | tf_op jit(solution)/shard_map/ppermute | solution.py:41
  19.2 225.9 %all-gather.11.cloned.1.call-start = ((), (), s32[]{:S(2)}) async-start(), calls=%async_computation.7 | async-start | bytes 3932160 | tf_op jit(solution)/shard_map/all_gather | solution.py:427
  115.7 165.7 %all-gather.9.cloned.1.call-start = ((), (), s32[]{:S(2)}) async-start(), calls=%async_computation.6 | async-start | bytes 3932160 | tf_op jit(solution)/shard_map/all_gather | solution.py:427
  116.3 26.2 %collective-permute-start.31 = (bf16[256,2048]{1,0:T(8,128)(2,1)S(1)}, bf16[256,2048]{1,0:T(8,128)(2,1)}, u32[]{:S(2)}, u32[]{:S(2)}) collective-permute-start(bf16[256,2048]{1,0:T(8,128)(2,1)S(1)} %bitcast.380), channel_id=1, source_target_pairs={{0,16},{4,20},{8,24},{12,28},{16,0},{20,4},{24,8},{28,12},{1,17},{... | collective-permute-start | bytes 3145736 | tf_op jit(solution)/shard_map/ppermute | solution.py:41
  117.0 27.3 %collective-permute-start.29 = (bf16[256,2048]{1,0:T(8,128)(2,1)S(1)}, bf16[256,2048]{1,0:T(8,128)(2,1)}, u32[]{:S(2)}, u32[]{:S(2)}) collective-permute-start(bf16[256,2048]{1,0:T(8,128)(2,1)S(1)} %bitcast.381), channel_id=1, source_target_pairs={{0,8},{4,12},{8,0},{12,4},{16,24},{20,28},{24,16},{28,20},{1,9},{5... | collective-permute-start | bytes 3145736 | tf_op jit(solution)/shard_map/ppermute | solution.py:41
  117.4 28.4 %collective-permute-start.28 = (bf16[256,2048]{1,0:T(8,128)(2,1)S(1)}, bf16[256,2048]{1,0:T(8,128)(2,1)}, u32[]{:S(2)}, u32[]{:S(2)}) collective-permute-start(bf16[256,2048]{1,0:T(8,128)(2,1)S(1)} %bitcast.382), channel_id=1, source_target_pairs={{0,4},{4,0},{8,12},{12,8},{16,20},{20,16},{24,28},{28,24},{1,5},{5... | collective-permute-start | bytes 3145736 | tf_op jit(solution)/shard_map/ppermute | solution.py:41
  129.6 36.0 %collective-permute-start.10 = (bf16[2,128,2048]{2,1,0:T(8,128)(2,1)}, bf16[2,128,2048]{2,1,0:T(8,128)(2,1)S(1)}, u32[]{:S(2)}, u32[]{:S(2)}) collective-permute-start(bf16[2,128,2048]{2,1,0:T(8,128)(2,1)} %pad_maximum_fusion.3), channel_id=1, source_target_pairs={{0,8},{4,12},{8,0},{12,4},{16,24},{20,28},{24,16},{28,20},{1,9},{5... | collective-permute-start | bytes 3145736 | tf_op jit(solution)/shard_map/ppermute | solution.py:41
  131.2 34.6 %collective-permute-start.12 = (bf16[2,128,2048]{2,1,0:T(8,128)(2,1)}, bf16[2,128,2048]{2,1,0:T(8,128)(2,1)}, u32[]{:S(2)}, u32[]{:S(2)}) collective-permute-start(bf16[2,128,2048]{2,1,0:T(8,128)(2,1)} %stack.196), channel_id=1, source_target_pairs={{0,16},{4,20},{8,24},{12,28},{16,0},{20,4},{24,8},{28,12},{1,17},{... | collective-permute-start | bytes 3145736 | tf_op jit(solution)/shard_map/ppermute | solution.py:41
  134.7 326.3 %reduce-scatter.14.cloned.1.call-start = ((), (), s32[]{:S(2)}) async-start(), calls=%async_computation.13 | async-start | bytes 3932160 | tf_op jit(solution)/shard_map/reduce_scatter | solution.py:108
  143.6 33.2 %collective-permute-start.34 = (bf16[128,2048]{1,0:T(8,128)(2,1)S(1)}, bf16[128,2048]{1,0:T(8,128)(2,1)S(1)}, u32[]{:S(2)}, u32[]{:S(2)}) collective-permute-start(bf16[128,2048]{1,0:T(8,128)(2,1)S(1)} %slice.523), channel_id=1, source_target_pairs={{0,8},{4,12},{8,0},{12,4},{16,24},{20,28},{24,16},{28,20},{1,9},{5... | collective-permute-start | bytes 1572872 | tf_op jit(solution)/shard_map/ppermute | solution.py:41
  145.4 31.4 %collective-permute-start.33 = (bf16[128,2048]{1,0:T(8,128)(2,1)S(1)}, bf16[128,2048]{1,0:T(8,128)(2,1)S(1)}, u32[]{:S(2)}, u32[]{:S(2)}) collective-permute-start(bf16[128,2048]{1,0:T(8,128)(2,1)S(1)} %slice.522), channel_id=1, source_target_pairs={{0,16},{4,20},{8,24},{12,28},{16,0},{20,4},{24,8},{28,12},{1,17},{... | collective-permute-start | bytes 1572872 | tf_op jit(solution)/shard_map/ppermute | solution.py:41
  145.8 31.5 %collective-permute-start.30 = (bf16[256,2048]{1,0:T(8,128)(2,1)}, bf16[256,2048]{1,0:T(8,128)(2,1)S(1)}, u32[]{:S(2)}, u32[]{:S(2)}) collective-permute-start(bf16[256,2048]{1,0:T(8,128)(2,1)} %collective-permute-done.29), channel_id=1, source_target_pairs={{0,4},{4,0},{8,12},{12,8},{16,20},{20,16},{24,28},{28,24},{1,5},{5... | collective-permute-start | bytes 3145736 | tf_op jit(solution)/shard_map/ppermute | solution.py:41
  190.9 24.2 %collective-permute-start.17 = (bf16[256,2048]{1,0:T(8,128)(2,1)}, bf16[256,2048]{1,0:T(8,128)(2,1)S(1)}, u32[]{:S(2)}, u32[]{:S(2)}) collective-permute-start(bf16[256,2048]{1,0:T(8,128)(2,1)} %get-tuple-element.48), channel_id=1, source_target_pairs={{0,16},{4,20},{8,24},{12,28},{16,0},{20,4},{24,8},{28,12},{1,17},{... | collective-permute-start | bytes 3145736 | tf_op jit(solution)/shard_map/ppermute | solution.py:41
  192.3 24.3 %collective-permute-start.15 = (bf16[256,2048]{1,0:T(8,128)(2,1)}, bf16[256,2048]{1,0:T(8,128)(2,1)S(1)}, u32[]{:S(2)}, u32[]{:S(2)}) collective-permute-start(bf16[256,2048]{1,0:T(8,128)(2,1)} %get-tuple-element.48), channel_id=1, source_target_pairs={{0,8},{4,12},{8,0},{12,4},{16,24},{20,28},{24,16},{28,20},{1,9},{5... | collective-permute-start | bytes 3145736 | tf_op jit(solution)/shard_map/ppermute | solution.py:41
  193.2 37.9 %collective-permute-start.14 = (bf16[256,2048]{1,0:T(8,128)(2,1)}, bf16[256,2048]{1,0:T(8,128)(2,1)}, u32[]{:S(2)}, u32[]{:S(2)}) collective-permute-start(bf16[256,2048]{1,0:T(8,128)(2,1)} %get-tuple-element.48), channel_id=1, source_target_pairs={{0,4},{4,0},{8,12},{12,8},{16,20},{20,16},{24,28},{28,24},{1,5},{5... | collective-permute-start | bytes 3145736 | tf_op jit(solution)/shard_map/ppermute | solution.py:41
  310.3 153.3 %reduce-scatter.12.cloned.1.call-start = ((), (), s32[]{:S(2)}) async-start(), calls=%async_computation.12 | async-start | bytes 3932160 | tf_op jit(solution)/shard_map/reduce_scatter | solution.py:108
  322.6 172.0 %reduce-scatter.10.cloned.1.call-start = ((), (), s32[]{:S(2)}) async-start(), calls=%async_computation.11 | async-start | bytes 3932160 | tf_op jit(solution)/shard_map/reduce_scatter | solution.py:108
  342.6 36.2 %collective-permute-start.37 = (bf16[4,256,2048]{2,1,0:T(8,128)(2,1)}, bf16[4,256,2048]{2,1,0:T(8,128)(2,1)}, u32[]{:S(2)}, u32[]{:S(2)}) collective-permute-start(bf16[4,256,2048]{2,1,0:T(8,128)(2,1)} %bitcast.34), channel_id=1, source_target_pairs={{0,4},{4,0},{8,12},{12,8},{16,20},{20,16},{24,28},{28,24},{1,5},{5... | collective-permute-start | bytes 12582920 | tf_op jit(solution)/shard_map/ppermute | solution.py:41
  359.3 30.4 %collective-permute-start.23 = (bf16[4,256,2048]{2,1,0:T(8,128)(2,1)}, bf16[4,256,2048]{2,1,0:T(8,128)(2,1)}, u32[]{:S(2)}, u32[]{:S(2)}) collective-permute-start(bf16[4,256,2048]{2,1,0:T(8,128)(2,1)} %bitcast.22), channel_id=1, source_target_pairs={{0,4},{4,0},{8,12},{12,8},{16,20},{20,16},{24,28},{28,24},{1,5},{5... | collective-permute-start | bytes 12582920 | tf_op jit(solution)/shard_map/ppermute | solution.py:41
  359.8 306.2 %reduce-scatter.8.cloned.1.call-start = ((), (), s32[]{:S(2)}) async-start(), calls=%async_computation.10 | async-start | bytes 1310720 | tf_op jit(solution)/shard_map/reduce_scatter | solution.py:108
  386.7 26.1 %collective-permute-start.38 = (bf16[2,128,2048]{2,1,0:T(8,128)(2,1)S(1)}, bf16[2,128,2048]{2,1,0:T(8,128)(2,1)S(1)}, u32[]{:S(2)}, u32[]{:S(2)}) collective-permute-start(bf16[2,128,2048]{2,1,0:T(8,128)(2,1)S(1)} %pad_maximum_fusion.5), channel_id=1, source_target_pairs={{0,8},{4,12},{8,0},{12,4},{16,24},{20,28},{24,16},{28,20},{1,9},{5... | collective-permute-start | bytes 3145736 | tf_op jit(solution)/shard_map/ppermute | solution.py:41
  388.2 26.1 %collective-permute-start.40 = (bf16[2,128,2048]{2,1,0:T(8,128)(2,1)S(1)}, bf16[2,128,2048]{2,1,0:T(8,128)(2,1)S(1)}, u32[]{:S(2)}, u32[]{:S(2)}) collective-permute-start(bf16[2,128,2048]{2,1,0:T(8,128)(2,1)S(1)} %stack.198), channel_id=1, source_target_pairs={{0,16},{4,20},{8,24},{12,28},{16,0},{20,4},{24,8},{28,12},{1,17},{... | collective-permute-start | bytes 3145736 | tf_op jit(solution)/shard_map/ppermute | solution.py:41
  399.1 36.1 %collective-permute-start.24 = (bf16[2,128,2048]{2,1,0:T(8,128)(2,1)S(1)}, bf16[2,128,2048]{2,1,0:T(8,128)(2,1)S(1)}, u32[]{:S(2)}, u32[]{:S(2)}) collective-permute-start(bf16[2,128,2048]{2,1,0:T(8,128)(2,1)S(1)} %pad_maximum_fusion.4), channel_id=1, source_target_pairs={{0,8},{4,12},{8,0},{12,4},{16,24},{20,28},{24,16},{28,20},{1,9},{5... | collective-permute-start | bytes 3145736 | tf_op jit(solution)/shard_map/ppermute | solution.py:41
  401.1 35.6 %collective-permute-start.26 = (bf16[2,128,2048]{2,1,0:T(8,128)(2,1)S(1)}, bf16[2,128,2048]{2,1,0:T(8,128)(2,1)S(1)}, u32[]{:S(2)}, u32[]{:S(2)}) collective-permute-start(bf16[2,128,2048]{2,1,0:T(8,128)(2,1)S(1)} %stack.197), channel_id=1, source_target_pairs={{0,16},{4,20},{8,24},{12,28},{16,0},{20,4},{24,8},{28,12},{1,17},{... | collective-permute-start | bytes 3145736 | tf_op jit(solution)/shard_map/ppermute | solution.py:41
  416.4 31.6 %collective-permute-start.39 = (bf16[128,2048]{1,0:T(8,128)(2,1)S(1)}, bf16[128,2048]{1,0:T(8,128)(2,1)S(1)}, u32[]{:S(2)}, u32[]{:S(2)}) collective-permute-start(bf16[128,2048]{1,0:T(8,128)(2,1)S(1)} %get-tuple-element.60), channel_id=1, source_target_pairs={{0,16},{4,20},{8,24},{12,28},{16,0},{20,4},{24,8},{28,12},{1,17},{... | collective-permute-start | bytes 1572872 | tf_op jit(solution)/shard_map/ppermute | solution.py:41
  417.9 30.0 %collective-permute-start.41 = (bf16[128,2048]{1,0:T(8,128)(2,1)S(1)}, bf16[128,2048]{1,0:T(8,128)(2,1)S(1)}, u32[]{:S(2)}, u32[]{:S(2)}) collective-permute-start(bf16[128,2048]{1,0:T(8,128)(2,1)S(1)} %get-tuple-element.61), channel_id=1, source_target_pairs={{0,8},{4,12},{8,0},{12,4},{16,24},{20,28},{24,16},{28,20},{1,9},{5... | collective-permute-start | bytes 1572872 | tf_op jit(solution)/shard_map/ppermute | solution.py:41
  437.4 21.9 %collective-permute-start.25 = (bf16[128,2048]{1,0:T(8,128)(2,1)S(1)}, bf16[128,2048]{1,0:T(8,128)(2,1)S(1)}, u32[]{:S(2)}, u32[]{:S(2)}) collective-permute-start(bf16[128,2048]{1,0:T(8,128)(2,1)S(1)} %get-tuple-element.66), channel_id=1, source_target_pairs={{0,16},{4,20},{8,24},{12,28},{16,0},{20,4},{24,8},{28,12},{1,17},{... | collective-permute-start | bytes 1572872 | tf_op jit(solution)/shard_map/ppermute | solution.py:41
  454.2 122.9 %collective-permute-start.45 = (bf16[256,2048]{1,0:T(8,128)(2,1)}, bf16[256,2048]{1,0:T(8,128)(2,1)}, u32[]{:S(2)}, u32[]{:S(2)}) collective-permute-start(bf16[256,2048]{1,0:T(8,128)(2,1)} %get-tuple-element.46), channel_id=1, source_target_pairs={{0,16},{4,20},{8,24},{12,28},{16,0},{20,4},{24,8},{28,12},{1,17},{... | collective-permute-start | bytes 3145736 | tf_op jit(solution)/shard_map/ppermute | solution.py:41
  455.8 115.2 %collective-permute-start.43 = (bf16[256,2048]{1,0:T(8,128)(2,1)}, bf16[256,2048]{1,0:T(8,128)(2,1)}, u32[]{:S(2)}, u32[]{:S(2)}) collective-permute-start(bf16[256,2048]{1,0:T(8,128)(2,1)} %get-tuple-element.46), channel_id=1, source_target_pairs={{0,8},{4,12},{8,0},{12,4},{16,24},{20,28},{24,16},{28,20},{1,9},{5... | collective-permute-start | bytes 3145736 | tf_op jit(solution)/shard_map/ppermute | solution.py:41
  456.3 127.8 %collective-permute-start.42 = (bf16[256,2048]{1,0:T(8,128)(2,1)}, bf16[256,2048]{1,0:T(8,128)(2,1)}, u32[]{:S(2)}, u32[]{:S(2)}) collective-permute-start(bf16[256,2048]{1,0:T(8,128)(2,1)} %get-tuple-element.46), channel_id=1, source_target_pairs={{0,4},{4,0},{8,12},{12,8},{16,20},{20,16},{24,28},{28,24},{1,5},{5... | collective-permute-start | bytes 3145736 | tf_op jit(solution)/shard_map/ppermute | solution.py:41
  468.7 30.4 %collective-permute-start.84 = (bf16[64,768]{1,0:T(8,128)(2,1)}, bf16[64,768]{1,0:T(8,128)(2,1)}, u32[]{:S(2)}, u32[]{:S(2)}) collective-permute-start(bf16[64,768]{1,0:T(8,128)(2,1)} %get-tuple-element.100), channel_id=1, source_target_pairs={{0,4},{4,0},{8,12},{12,8},{16,20},{20,16},{24,28},{28,24},{1,5},{5... | collective-permute-start | bytes 294920 | tf_op jit(solution)/shard_map/ppermute | solution.py:41
  497.4 29.9 %collective-permute-start.90 = (bf16[64,768]{1,0:T(8,128)(2,1)S(1)}, bf16[64,768]{1,0:T(8,128)(2,1)S(1)}, u32[]{:S(2)}, u32[]{:S(2)}) collective-permute-start(bf16[64,768]{1,0:T(8,128)(2,1)S(1)} %get-tuple-element.94), channel_id=1, source_target_pairs={{0,28},{4,24},{8,20},{12,16},{16,12},{20,8},{24,4},{28,0},{1,29},{... | collective-permute-start | bytes 294920 | tf_op jit(solution)/shard_map/ppermute | solution.py:41
  525.6 31.0 %collective-permute-start.83 = (bf16[64,768]{1,0:T(8,128)(2,1)S(1)}, bf16[64,768]{1,0:T(8,128)(2,1)S(1)}, u32[]{:S(2)}, u32[]{:S(2)}) collective-permute-start(bf16[64,768]{1,0:T(8,128)(2,1)S(1)} %get-tuple-element.102), channel_id=1, source_target_pairs={{0,28},{4,24},{8,20},{12,16},{16,12},{20,8},{24,4},{28,0},{1,29},{... | collective-permute-start | bytes 294920 | tf_op jit(solution)/shard_map/ppermute | solution.py:41
  562.9 97.1 %collective-permute-start.76 = (bf16[64,768]{1,0:T(8,128)(2,1)S(1)}, bf16[64,768]{1,0:T(8,128)(2,1)S(1)}, u32[]{:S(2)}, u32[]{:S(2)}) collective-permute-start(bf16[64,768]{1,0:T(8,128)(2,1)S(1)} %get-tuple-element.110), channel_id=1, source_target_pairs={{0,28},{4,24},{8,20},{12,16},{16,12},{20,8},{24,4},{28,0},{1,29},{... | collective-permute-start | bytes 294920 | tf_op jit(solution)/shard_map/ppermute | solution.py:41
  587.8 70.7 %collective-permute-start.75 = (bf16[64,768]{1,0:T(8,128)(2,1)S(1)}, bf16[64,768]{1,0:T(8,128)(2,1)}, u32[]{:S(2)}, u32[]{:S(2)}) collective-permute-start(bf16[64,768]{1,0:T(8,128)(2,1)S(1)} %get-tuple-element.111), channel_id=1, source_target_pairs={{0,24},{4,28},{8,16},{12,20},{16,8},{20,12},{24,0},{28,4},{1,25},{... | collective-permute-start | bytes 294920 | tf_op jit(solution)/shard_map/ppermute | solution.py:41
  596.3 60.6 %collective-permute-start.74 = (bf16[64,768]{1,0:T(8,128)(2,1)S(1)}, bf16[64,768]{1,0:T(8,128)(2,1)}, u32[]{:S(2)}, u32[]{:S(2)}) collective-permute-start(bf16[64,768]{1,0:T(8,128)(2,1)S(1)} %get-tuple-element.112), channel_id=1, source_target_pairs={{0,20},{4,16},{8,28},{12,24},{16,4},{20,0},{24,12},{28,8},{1,21},{... | collective-permute-start | bytes 294920 | tf_op jit(solution)/shard_map/ppermute | solution.py:41
  605.7 95.0 %reduce-scatter.6.cloned.1.call-start = ((), (), s32[]{:S(2)}) async-start(), calls=%async_computation.9 | async-start | bytes 2621440 | tf_op jit(solution)/shard_map/reduce_scatter | solution.py:108
  656.7 51.5 %collective-permute-start.51 = (bf16[4,256,2048]{2,1,0:T(8,128)(2,1)}, bf16[4,256,2048]{2,1,0:T(8,128)(2,1)}, u32[]{:S(2)}, u32[]{:S(2)}) collective-permute-start(bf16[4,256,2048]{2,1,0:T(8,128)(2,1)} %bitcast.47), channel_id=1, source_target_pairs={{0,4},{4,0},{8,12},{12,8},{16,20},{20,16},{24,28},{28,24},{1,5},{5... | collective-permute-start | bytes 12582920 | tf_op jit(solution)/shard_map/ppermute | solution.py:41
  703.2 47.4 %collective-permute-start.62 = (bf16[64,512]{1,0:T(8,128)(2,1)S(1)}, bf16[64,512]{1,0:T(8,128)(2,1)S(1)}, u32[]{:S(2)}, u32[]{:S(2)}) collective-permute-start(bf16[64,512]{1,0:T(8,128)(2,1)S(1)} %get-tuple-element.120), channel_id=1, source_target_pairs={{0,28},{4,24},{8,20},{12,16},{16,12},{20,8},{24,4},{28,0},{1,29},{... | collective-permute-start | bytes 196616 | tf_op jit(solution)/shard_map/ppermute | solution.py:41
  704.9 45.1 %collective-permute-start.61 = (bf16[64,512]{1,0:T(8,128)(2,1)S(1)}, bf16[64,512]{1,0:T(8,128)(2,1)S(1)}, u32[]{:S(2)}, u32[]{:S(2)}) collective-permute-start(bf16[64,512]{1,0:T(8,128)(2,1)S(1)} %get-tuple-element.121), channel_id=1, source_target_pairs={{0,24},{4,28},{8,16},{12,20},{16,8},{20,12},{24,0},{28,4},{1,25},{... | collective-permute-start | bytes 196616 | tf_op jit(solution)/shard_map/ppermute | solution.py:41
  724.2 28.9 %collective-permute-start.52 = (bf16[2,128,2048]{2,1,0:T(8,128)(2,1)}, bf16[2,128,2048]{2,1,0:T(8,128)(2,1)S(1)}, u32[]{:S(2)}, u32[]{:S(2)}) collective-permute-start(bf16[2,128,2048]{2,1,0:T(8,128)(2,1)} %pad_maximum_fusion.6), channel_id=1, source_target_pairs={{0,8},{4,12},{8,0},{12,4},{16,24},{20,28},{24,16},{28,20},{1,9},{5... | collective-permute-start | bytes 3145736 | tf_op jit(solution)/shard_map/ppermute | solution.py:41
  725.4 27.9 %collective-permute-start.54 = (bf16[2,128,2048]{2,1,0:T(8,128)(2,1)}, bf16[2,128,2048]{2,1,0:T(8,128)(2,1)}, u32[]{:S(2)}, u32[]{:S(2)}) collective-permute-start(bf16[2,128,2048]{2,1,0:T(8,128)(2,1)} %stack.199), channel_id=1, source_target_pairs={{0,16},{4,20},{8,24},{12,28},{16,0},{20,4},{24,8},{28,12},{1,17},{... | collective-permute-start | bytes 3145736 | tf_op jit(solution)/shard_map/ppermute | solution.py:41
  726.7 22.7 %collective-permute-start.60 = (bf16[64,512]{1,0:T(8,128)(2,1)S(1)}, bf16[64,512]{1,0:T(8,128)(2,1)S(1)}, u32[]{:S(2)}, u32[]{:S(2)}) collective-permute-start(bf16[64,512]{1,0:T(8,128)(2,1)S(1)} %get-tuple-element.122), channel_id=1, source_target_pairs={{0,20},{4,16},{8,28},{12,24},{16,4},{20,0},{24,12},{28,8},{1,21},{... | collective-permute-start | bytes 196616 | tf_op jit(solution)/shard_map/ppermute | solution.py:41
  (108 other events, 1223.2 us)
Sparse Core Ops, SparseCore 0:
  10.9 49.9 all-gather.14
  63.0 26.5 all-gather.6
  91.2 63.0 all-gather.12
  155.6 62.1 all-gather.10
  219.2 62.1 all-gather.8
  310.5 58.8 reduce-scatter.13
  371.7 60.2 reduce-scatter.11
  434.3 60.2 reduce-scatter.9
  605.8 27.2 reduce-scatter.7
  651.2 49.4 reduce-scatter.5

commit v2 on v1

v2 whole, which is shorter than its diff:
```python
import functools
import math

import jax
import jax.numpy as jnp
from jax import lax
from jax.experimental import pallas as pl
from jax.experimental.pallas import tpu as pltpu
from jax.sharding import PartitionSpec as P

QUERY_HEADS = 16
KEY_VALUE_HEADS = 8
HEAD_SIZE = 128

epsilon = 1e-06
rope_base = 1000000.0
large_negative = -1e30

bf16 = jnp.bfloat16
f32 = jnp.float32
VMEM_LIMIT = 56 * 1024 * 1024


def cost_of(microseconds):
    return pl.CostEstimate(
        flops=int(microseconds * 1.1e9), bytes_accessed=1 << 20, transcendentals=0
    )


def dot_nn(left, right):
    return lax.dot_general(left, right, (((1,), (0,)), ((), ())), preferred_element_type=f32)


def dot_nt(left, right):
    return lax.dot_general(left, right, (((1,), (1,)), ((), ())), preferred_element_type=f32)


def dot_tn(left, right):
    return lax.dot_general(left, right, (((0,), (0,)), ((), ())), preferred_element_type=f32)


def rms_scale(values):
    return lax.rsqrt(jnp.mean(values * values, axis=-1, keepdims=True) + epsilon)


def swap(values, n, bits, axis="ctx"):
    return lax.ppermute(values, axis, [(c, c ^ bits) for c in range(n)])


def swap_first(values, n, first):
    return lax.ppermute(
        values, "ctx", [(c, c ^ (2 if (c % 2 == 0) == first else 4)) for c in range(n)]
    )


def slot_order(n):
    me = lax.axis_index("ctx")
    slots = jnp.arange(n, dtype=jnp.int32)
    if n == 8:
        even = jnp.array([0, 2, 4, 6, 1, 5, 3, 7], jnp.int32)
        odd = jnp.array([0, 4, 2, 6, 1, 3, 5, 7], jnp.int32)
        slots = jnp.where(me % 2 == 0, even, odd)
    return me ^ slots


def any_spec():
    return pl.BlockSpec(memory_space=pl.ANY)


def gather_pieces(rows, n):
    if n != 8:
        full = lax.all_gather(rows, "ctx", axis=0)
        return [jnp.take(full, slot_order(n), axis=0).reshape(-1, rows.shape[1])]
    pair = jnp.concatenate([rows, swap_first(rows, n, True)], axis=0)
    other = swap_first(pair, n, False)
    return [pair, other, swap(pair, n, 1), swap(other, n, 1)]


def piece_copies(pieces, out, sem, rows):
    copies, at = [], 0
    for piece in pieces:
        size = piece.shape[0]
        slot, start = at // rows, at % rows
        if size > rows:
            for k in range(size // rows):
                copies.append(
                    pltpu.make_async_copy(
                        piece.at[pl.ds(k * rows, rows)], out.at[slot + k], sem.at[slot + k]
                    )
                )
        else:
            copies.append(
                pltpu.make_async_copy(piece, out.at[slot, pl.ds(start, size)], sem.at[slot])
            )
        at += size
    return copies


def assemble_kernel(count, rows, *refs):
    out, held, sem, out_sem = refs[count:]
    for copy in piece_copies(refs[:count], held, sem, rows):
        copy.start()
    slots = range(out.shape[0])
    for slot in slots:
        pltpu.make_async_copy(held.at[slot], held.at[slot], sem.at[slot]).wait()
        pltpu.make_async_copy(held.at[slot], out.at[slot], out_sem.at[slot]).start()
    for slot in slots:
        pltpu.make_async_copy(held.at[slot], out.at[slot], out_sem.at[slot]).wait()


def assemble(pieces, n):
    total = sum(p.shape[0] for p in pieces)
    rows, width = total // n, pieces[0].shape[1]
    if len(pieces) == 1:
        return pieces[0].reshape(n, rows, width)
    return pl.pallas_call(
        functools.partial(assemble_kernel, len(pieces), rows),
        in_specs=[any_spec() for _ in pieces],
        out_specs=any_spec(),
        out_shape=jax.ShapeDtypeStruct((n, rows, width), pieces[0].dtype),
        scratch_shapes=[
            pltpu.VMEM((n, rows, width), pieces[0].dtype),
            pltpu.SemaphoreType.DMA((n,)),
            pltpu.SemaphoreType.DMA((n,)),
        ],
        compiler_params=pltpu.CompilerParams(vmem_limit_bytes=VMEM_LIMIT),
        cost_estimate=cost_of(6.0 * total * width / 2**22),
        name="assemble",
    )(*pieces)


def mm_kernel(count, *refs):
    total = dot_nt(refs[0][0], refs[count][...])
    for k in range(1, count):
        total = total + dot_nt(refs[k][0], refs[count + k][...])
    refs[2 * count][0] = total.astype(bf16)


def mm_slots(lefts, ws, column, start, count):
    rows = lefts[0].shape[1]
    width = ws[0].shape[0]
    depths = [left.shape[2] for left in lefts]
    return pl.pallas_call(
        functools.partial(mm_kernel, len(lefts)),
        grid=(count,),
        in_specs=[pl.BlockSpec((1, rows, d), lambda i: (i + start, 0, 0)) for d in depths]
        + [pl.BlockSpec((width, d), lambda i: (0, column)) for d in depths],
        out_specs=pl.BlockSpec((1, rows, width), lambda i: (i, 0, 0)),
        out_shape=jax.ShapeDtypeStruct((count, rows, width), bf16),
        compiler_params=pltpu.CompilerParams(vmem_limit_bytes=VMEM_LIMIT),
        cost_estimate=cost_of(3.5 + 8.0 * count * rows * sum(depths) * width / (1024 * 1536 * 2048)),
        name="mm_slots",
    )(*lefts, *ws)


def add_kernel(mine_ref, got_ref, send_ref, keep_ref):
    half = send_ref.shape[0]
    for i in range(half):
        keep_ref[i] = mine_ref[i].astype(f32) + got_ref[i].astype(f32)
        send_ref[i] = (mine_ref[half + i].astype(f32) + got_ref[half + i].astype(f32)).astype(bf16)


def add_halves(mine, got):
    slots, rows, width = mine.shape
    half, tile = slots // 2, min(width, 512)
    read = pl.BlockSpec((slots, rows, tile), lambda i: (0, 0, i))
    write = pl.BlockSpec((half, rows, tile), lambda i: (0, 0, i))
    return pl.pallas_call(
        add_kernel,
        grid=(width // tile,),
        in_specs=[read, read],
        out_specs=[write, write],
        out_shape=[
            jax.ShapeDtypeStruct((half, rows, width), bf16),
            jax.ShapeDtypeStruct((half, rows, width), f32),
        ],
        compiler_params=pltpu.CompilerParams(vmem_limit_bytes=VMEM_LIMIT),
        cost_estimate=cost_of(6.5 * slots * rows * width / 2**21),
        name="add_halves",
    )(mine, got)


def scatter_slots(lefts, ws, column, n):
    if n != 8:
        index = jnp.argsort(slot_order(n))
        part = jnp.take(mm_slots(lefts, ws, column, 0, n), index, axis=0)
        return lax.psum_scatter(part, "ctx", scatter_dimension=0, tiled=True)[0].astype(f32)
    far = mm_slots(lefts, ws, column, 4, 4)
    got = swap(far, n, 1)
    near = mm_slots(lefts, ws, column, 0, 4)
    send, keep = add_halves(near, got)
    got = swap_first(send, n, False)
    last = (keep[1] + got[1].astype(f32)).astype(bf16)
    return keep[0] + got[0].astype(f32) + swap_first(last, n, True).astype(f32)


def exchange(blocks):
    return lax.all_to_all(blocks, "ctx", 0, 0, tiled=True)


def weight_kernel(counts, *refs):
    refs, out_ref = refs[:-1], refs[-1]
    tops, at = [], 0
    for count in counts:
        left = jnp.concatenate([r[...] for r in refs[at : at + count]], axis=0)
        tops.append(dot_tn(left, refs[at + count][...]))
        at += count + 1
    shards, _, rows, width = out_ref.shape
    out_ref[...] = jnp.concatenate(tops, axis=1).astype(bf16).reshape(shards, 1, rows, width)


def weight_grad(pairs, n, n_fsdp):
    depth = pairs[0][0][0].shape[1]
    rows, tile = depth // (n * n_fsdp), depth // n
    width = sum(right.shape[1] for _, right in pairs)
    total = pairs[0][1].shape[0]
    specs, args = [], []
    for pieces, right in pairs:
        specs += [pl.BlockSpec((p.shape[0], tile), lambda j: (0, j)) for p in pieces]
        specs.append(pl.BlockSpec(right.shape, lambda j: (0, 0)))
        args += [*pieces, right]
    out = pl.pallas_call(
        functools.partial(weight_kernel, [len(pieces) for pieces, _ in pairs]),
        grid=(n,),
        in_specs=specs,
        out_specs=pl.BlockSpec((n_fsdp, 1, rows, width), lambda j: (0, j, 0, 0)),
        out_shape=jax.ShapeDtypeStruct((n_fsdp, n, rows, width), bf16),
        compiler_params=pltpu.CompilerParams(vmem_limit_bytes=VMEM_LIMIT),
        cost_estimate=cost_of(16.0 * total * depth * width / (2048 * 2048 * 1152)),
        name="weight_grad",
    )(*args)
    return out.reshape(depth, width)


def reduce_rows(grad, n):
    summed = lax.psum_scatter(grad, "fsdp", scatter_dimension=0, tiled=True)
    return summed.reshape(n, -1, grad.shape[1])


def join_kernel(parts, got_ref, *out_refs):
    for out_ref, slices in zip(out_refs, parts):
        out_ref[...] = jnp.concatenate(
            [got_ref[0, :, lo:hi].astype(f32) for lo, hi in slices], axis=1
        )


def join_columns(got, parts):
    n, rows, width = got.shape
    sizes = [sum(hi - lo for lo, hi in slices) for slices in parts]
    return pl.pallas_call(
        functools.partial(join_kernel, parts),
        grid=(n,),
        in_specs=[pl.BlockSpec((1, rows, width), lambda i: (i, 0, 0))],
        out_specs=[pl.BlockSpec((rows, size), lambda i: (0, i)) for size in sizes],
        out_shape=[jax.ShapeDtypeStruct((rows, n * size), f32) for size in sizes],
        cost_estimate=cost_of(5.0),
        name="join_columns",
    )(got)


def sum_all(values, n, n_fsdp):
    bits = 1
    while bits < n:
        values = values + swap(values, n, bits)
        bits *= 2
    bits = 1
    while bits < n_fsdp:
        values = values + swap(values, n_fsdp, bits, "fsdp")
        bits *= 2
    return values


def after(values, *others):
    return lax.optimization_barrier((values,) + others)[0]


def project_kernel(count, heads, place_ref, *refs):
    pieces, refs = refs[:count], refs[count:]
    gain_ref, w_ref, qg_ref, kg_ref, cos_ref, sin_ref = refs[:6]
    xn_ref, qraw_ref, kraw_ref, qb_ref, kb_ref, vb_ref, x_all, sem = refs[6:]
    slot = pl.program_id(0)

    @pl.when(slot == 0)
    def _():
        for copy in piece_copies(pieces, x_all, sem, x_all.shape[1]):
            copy.start()

    pltpu.make_async_copy(x_all.at[slot], x_all.at[slot], sem.at[slot]).wait()
    x = x_all[slot].astype(f32)
    xn = (x * rms_scale(x) * gain_ref[...]).astype(bf16)
    xn_ref[0] = xn
    w = w_ref[...].reshape(x.shape[1], w_ref.shape[2])
    y = jnp.dot(xn, w, preferred_element_type=f32)
    blk = x.shape[0] // 2
    for half in range(2):
        place = place_ref[2 * slot + half]
        at = pl.ds(pl.multiple_of(place * blk, blk), blk)
        cosine, sine = cos_ref[at, :], sin_ref[at, :]
        rows = y[half * blk : (half + 1) * blk]
        for head in range(heads + 1):
            raw = rows[:, head * HEAD_SIZE : (head + 1) * HEAD_SIZE]
            gain = (qg_ref if head < heads else kg_ref)[...]
            normed = raw * rms_scale(raw) * gain
            turned = normed * cosine + pltpu.roll(normed, HEAD_SIZE // 2, 1) * sine
            if head < heads:
                cols = slice(head * HEAD_SIZE, (head + 1) * HEAD_SIZE)
                qraw_ref[at, cols] = raw
                qb_ref[at, cols] = turned.astype(bf16)
            else:
                kraw_ref[at, :] = raw
                kb_ref[at, :] = turned.astype(bf16)
        vb_ref[at, :] = rows[:, (heads + 1) * HEAD_SIZE :].astype(bf16)


def project(pieces, n, places, gain, pack, q_gain, k_gain, cosine, sine, heads):
    depth = pieces[0].shape[1]
    total = sum(p.shape[0] for p in pieces)
    rows = total // n
    const = lambda i, p: (0, 0)
    whole = lambda a: pl.BlockSpec(a.shape, const)
    shards = pack.shape[0]
    in_cols = (heads + 2) * HEAD_SIZE
    out = [
        jax.ShapeDtypeStruct((n, rows, depth), bf16),
        jax.ShapeDtypeStruct((total, heads * HEAD_SIZE), f32),
        jax.ShapeDtypeStruct((total, HEAD_SIZE), f32),
        jax.ShapeDtypeStruct((total, heads * HEAD_SIZE), bf16),
        jax.ShapeDtypeStruct((total, HEAD_SIZE), bf16),
        jax.ShapeDtypeStruct((total, HEAD_SIZE), bf16),
    ]
    args = (q_gain, k_gain, cosine, sine)
    return pl.pallas_call(
        functools.partial(project_kernel, len(pieces), heads),
        grid_spec=pltpu.PrefetchScalarGridSpec(
            num_scalar_prefetch=1,
            grid=(n,),
            in_specs=[any_spec() for _ in pieces]
            + [
                whole(gain),
                pl.BlockSpec((shards, depth // shards, in_cols), lambda i, p: (0, 0, 0)),
            ]
            + [whole(a) for a in args],
            out_specs=[pl.BlockSpec((1, rows, depth), lambda i, p: (i, 0, 0))]
            + [pl.BlockSpec(o.shape, const) for o in out[1:]],
            scratch_shapes=[
                pltpu.VMEM((n, rows, depth), bf16),
                pltpu.SemaphoreType.DMA((n,)),
            ],
        ),
        out_shape=out,
        compiler_params=pltpu.CompilerParams(
            dimension_semantics=("arbitrary",), vmem_limit_bytes=VMEM_LIMIT
        ),
        cost_estimate=cost_of(16.0 * total * heads / 4096),
        name="project",
    )(places, *pieces, gain, pack, *args)


def attend_kernel(
    heads, tile, length_ref, place_ref, index_ref, q_ref, k_ref, v_ref, o_ref, a_ref, ai_ref, lse_ref
):
    total = q_ref.shape[0]
    blk = total // place_ref.shape[0]
    scale = 1.0 / math.sqrt(HEAD_SIZE)
    length = length_ref[0]
    key_tiles = (length + tile - 1) // tile

    def q_step(i, unused):
        q_at = pl.ds(pl.multiple_of(i * tile, tile), tile)
        q = [q_ref[q_at, h * HEAD_SIZE : (h + 1) * HEAD_SIZE] for h in range(heads)]

        def tile_step(j, carry, masked):
            k_at = pl.ds(pl.multiple_of(j * tile, tile), tile)
            k, v = k_ref[k_at, :], v_ref[k_at, :]
            if masked:
                key = j * tile + lax.broadcasted_iota(jnp.int32, (tile, tile), 0)
                query = i * tile + lax.broadcasted_iota(jnp.int32, (tile, tile), 1)
                allowed = (key <= query) & (key < length)
            new = []
            for h in range(heads):
                top, tot, out = carry[h]
                s = dot_nt(k, q[h]) * scale
                if masked:
                    s = jnp.where(allowed, s, large_negative)
                top_new = jnp.maximum(top, jnp.max(s, axis=0, keepdims=True))
                shrink = jnp.exp(top - top_new)
                p = jnp.exp(s - top_new)
                tot = tot * shrink + jnp.sum(p, axis=0, keepdims=True)
                out = out * shrink + dot_tn(v, p.astype(bf16))
                new.append((top_new, tot, out))
            return tuple(new)

        start = tuple(
            (
                jnp.full((1, tile), large_negative, f32),
                jnp.zeros((1, tile), f32),
                jnp.zeros((HEAD_SIZE, tile), f32),
            )
            for _ in range(heads)
        )
        full = jnp.minimum(i, length // tile)
        carry = lax.fori_loop(0, full, functools.partial(tile_step, masked=False), start)
        carry = lax.fori_loop(
            full, jnp.minimum(i + 1, key_tiles), functools.partial(tile_step, masked=True), carry
        )
        for h in range(heads):
            top, tot, out = carry[h]
            lse_ref[pl.ds(h, 1), q_at] = top + jnp.log(tot)
            o = jnp.transpose(out / tot)
            cols = slice(h * HEAD_SIZE, (h + 1) * HEAD_SIZE)
            o_ref[q_at, cols] = o
        return unused

    lax.fori_loop(0, total // tile, q_step, 0)

    def place_step(b, unused):
        src = pl.ds(pl.multiple_of(place_ref[b] * blk, blk), blk)
        dst = pl.ds(pl.multiple_of(b * blk, blk), blk)
        a_ref[dst, :] = o_ref[src, :].astype(bf16)
        src = pl.ds(pl.multiple_of(index_ref[b] * blk, blk), blk)
        ai_ref[dst, :] = o_ref[src, :].astype(bf16)
        return unused

    lax.fori_loop(0, place_ref.shape[0], place_step, 0)


def attend(length, places, by_index, q, k, v, heads):
    total = q.shape[0]
    tile = min(512, total)
    vm = lambda: pl.BlockSpec(memory_space=pltpu.VMEM)
    sm = lambda: pl.BlockSpec(memory_space=pltpu.SMEM)
    return pl.pallas_call(
        functools.partial(attend_kernel, heads, tile),
        in_specs=[sm(), sm(), sm(), vm(), vm(), vm()],
        out_specs=[vm(), vm(), vm(), vm()],
        out_shape=[
            jax.ShapeDtypeStruct((total, heads * HEAD_SIZE), f32),
            jax.ShapeDtypeStruct((total, heads * HEAD_SIZE), bf16),
            jax.ShapeDtypeStruct((total, heads * HEAD_SIZE), bf16),
            jax.ShapeDtypeStruct((heads, total), f32),
        ],
        compiler_params=pltpu.CompilerParams(vmem_limit_bytes=VMEM_LIMIT),
        cost_estimate=cost_of(18.5 * total * heads / 4096),
        name="attend",
    )(length, places, by_index, q, k, v)


def unturn(grad, raw, gain, cosine, sine):
    grad = grad * cosine - pltpu.roll(grad, HEAD_SIZE // 2, 1) * sine
    scale = rms_scale(raw)
    hat = raw * scale
    inner = grad * gain
    out = scale * (inner - hat * jnp.mean(inner * hat, axis=-1, keepdims=True))
    return out, jnp.sum(grad * hat, axis=0, keepdims=True)


def attend_back_kernel(
    heads, tile, finish_keys, length_ref, place_ref, index_ref, q_ref, k_ref, v_ref, da_ref, o_ref,
    lse_ref, qraw_ref, kraw_ref, qg_ref, kg_ref, cos_ref, sin_ref,
    d_ref, dqg_ref, dkg_ref, *rest,
):
    if finish_keys:
        da_s, delta_s, dq_s, turned_s, dk_s, dv_s = rest
    else:
        dk_s, dv_s, da_s, delta_s, dq_s, turned_s = rest
    total = q_ref.shape[0]
    blocks = place_ref.shape[0]
    blk = total // blocks
    scale = 1.0 / math.sqrt(HEAD_SIZE)
    length = length_ref[0]
    tiles = total // tile

    def sort_step(b, unused):
        dst = pl.ds(pl.multiple_of(index_ref[b] * blk, blk), blk)
        src = pl.ds(pl.multiple_of(b * blk, blk), blk)
        piece = da_ref[src, :]
        da_s[dst, :] = piece
        prod = piece.astype(f32) * o_ref[dst, :]
        for h in range(heads):
            cols = slice(h * HEAD_SIZE, (h + 1) * HEAD_SIZE)
            delta_s[pl.ds(h, 1), dst] = jnp.sum(jnp.transpose(prod[:, cols]), axis=0, keepdims=True)
        return unused

    lax.fori_loop(0, blocks, sort_step, 0)
    dq_s[...] = jnp.zeros_like(dq_s)
    dk_s[...] = jnp.zeros_like(dk_s)
    dv_s[...] = jnp.zeros_like(dv_s)

    def k_step(j, unused):
        k_at = pl.ds(pl.multiple_of(j * tile, tile), tile)
        k, v = k_ref[k_at, :], v_ref[k_at, :]

        def tile_step(i, carry, masked):
            dk, dv = carry
            q_at = pl.ds(pl.multiple_of(i * tile, tile), tile)
            if masked:
                key = j * tile + lax.broadcasted_iota(jnp.int32, (tile, tile), 0)
                query = i * tile + lax.broadcasted_iota(jnp.int32, (tile, tile), 1)
                allowed = (key <= query) & (key < length)
            for h in range(heads):
                cols = slice(h * HEAD_SIZE, (h + 1) * HEAD_SIZE)
                q, da = q_ref[q_at, cols], da_s[q_at, cols]
                s = dot_nt(k, q) * scale - lse_ref[pl.ds(h, 1), q_at]
                if masked:
                    s = jnp.where(allowed, s, large_negative)
                p = jnp.exp(s)
                dp = dot_nt(v, da)
                ds = (p * (dp - delta_s[pl.ds(h, 1), q_at])).astype(bf16)
                dv = dv + dot_nn(p.astype(bf16), da)
                dk = dk + dot_nn(ds, q)
                dq_s[q_at, cols] += dot_tn(ds, k)
            return dk, dv

        zero = jnp.zeros((tile, HEAD_SIZE), f32)
        carry = (zero, zero)
        whole_tile = (j + 1) * tile <= length
        carry = lax.fori_loop(j, j + 1, functools.partial(tile_step, masked=True), carry)
        first_full = jnp.where(whole_tile, j + 1, tiles)
        carry = lax.fori_loop(
            j + 1, first_full, functools.partial(tile_step, masked=True), carry
        )
        carry = lax.fori_loop(first_full, tiles, functools.partial(tile_step, masked=False), carry)
        dk_s[k_at, :], dv_s[k_at, :] = carry[0] * scale, carry[1]
        return unused

    lax.fori_loop(0, (length + tile - 1) // tile, k_step, 0)

    dqg_ref[...] = jnp.zeros_like(dqg_ref)
    dkg_ref[...] = jnp.zeros_like(dkg_ref)

    def last_step(b, unused):
        src = pl.ds(pl.multiple_of(b * blk, blk), blk)
        cosine, sine = cos_ref[src, :], sin_ref[src, :]
        for h in range(heads):
            cols = slice(h * HEAD_SIZE, (h + 1) * HEAD_SIZE)
            grad = (dq_s[src, cols] * scale).astype(bf16).astype(f32)
            out, gain = unturn(grad, qraw_ref[src, cols], qg_ref[...], cosine, sine)
            turned_s[src, cols] = out.astype(bf16)
            dqg_ref[...] += gain
        if finish_keys:
            grad = dk_s[src, :].astype(bf16).astype(f32)
            out, gain = unturn(grad, kraw_ref[src, :], kg_ref[...], cosine, sine)
            turned_s[src, heads * HEAD_SIZE : (heads + 1) * HEAD_SIZE] = out.astype(bf16)
            dkg_ref[...] += gain
            turned_s[src, (heads + 1) * HEAD_SIZE :] = dv_s[src, :].astype(bf16)
        return unused

    lax.fori_loop(0, blocks, last_step, 0)

    def place_step(b, unused):
        dst = pl.ds(pl.multiple_of(b * blk, blk), blk)
        d_ref[dst, :] = turned_s[pl.ds(pl.multiple_of(place_ref[b] * blk, blk), blk), :]
        return unused

    lax.fori_loop(0, blocks, place_step, 0)


def attend_back(
    length, places, by_index, q, k, v, da, o, lse, qraw, kraw, qg, kg, cosine, sine, heads, finish_keys
):
    total = q.shape[0]
    tile = min(512, total)
    vm = lambda: pl.BlockSpec(memory_space=pltpu.VMEM)
    sm = lambda: pl.BlockSpec(memory_space=pltpu.SMEM)
    width = (heads + 2 if finish_keys else heads) * HEAD_SIZE
    sums = [jax.ShapeDtypeStruct((total, HEAD_SIZE), f32)] * 2
    out = [
        jax.ShapeDtypeStruct((total, width), bf16),
        jax.ShapeDtypeStruct((1, HEAD_SIZE), f32),
        jax.ShapeDtypeStruct((1, HEAD_SIZE), f32),
    ] + ([] if finish_keys else sums)
    scratch = [
        pltpu.VMEM((total, heads * HEAD_SIZE), bf16),
        pltpu.VMEM((heads, total), f32),
        pltpu.VMEM((total, heads * HEAD_SIZE), f32),
        pltpu.VMEM((total, width), bf16),
    ] + ([pltpu.VMEM(s.shape, s.dtype) for s in sums] if finish_keys else [])
    return pl.pallas_call(
        functools.partial(attend_back_kernel, heads, tile, finish_keys),
        in_specs=[sm(), sm(), sm()] + [vm() for _ in range(12)],
        out_specs=[vm() for _ in out],
        out_shape=out,
        scratch_shapes=scratch,
        compiler_params=pltpu.CompilerParams(vmem_limit_bytes=VMEM_LIMIT),
        cost_estimate=cost_of(33.0 * total * heads / 4096),
        name="attend_back",
    )(length, places, by_index, q, k, v, da, o, lse, qraw, kraw, qg, kg, cosine, sine)


def branch_kernel(order_ref, a_ref, wo_ref, x_ref, gain_ref, h1_ref, xn_ref, acc):
    step = pl.program_id(0)

    @pl.when(step == 0)
    def _():
        acc[...] = x_ref[...].astype(f32)

    acc[...] += dot_nt(a_ref[0], wo_ref[0])

    @pl.when(step == pl.num_programs(0) - 1)
    def _():
        h1 = acc[...]
        h1_ref[...] = h1
        xn_ref[...] = (h1 * rms_scale(h1) * gain_ref[...]).astype(bf16)


def branch(order, a_tok, wo_slots, x, gain):
    n, rows, q_cols = a_tok.shape
    depth = x.shape[1]
    const = lambda i, p: (0, 0)
    return pl.pallas_call(
        branch_kernel,
        grid_spec=pltpu.PrefetchScalarGridSpec(
            num_scalar_prefetch=1,
            grid=(n,),
            in_specs=[
                pl.BlockSpec((1, rows, q_cols), lambda i, p: (p[i], 0, 0)),
                pl.BlockSpec((1, depth, q_cols), lambda i, p: (i, 0, 0)),
                pl.BlockSpec((rows, depth), const),
                pl.BlockSpec((1, depth), const),
            ],
            out_specs=[pl.BlockSpec((rows, depth), const)] * 2,
            scratch_shapes=[pltpu.VMEM((rows, depth), f32)],
        ),
        out_shape=[
            jax.ShapeDtypeStruct((rows, depth), f32),
            jax.ShapeDtypeStruct((rows, depth), bf16),
        ],
        compiler_params=pltpu.CompilerParams(vmem_limit_bytes=VMEM_LIMIT),
        cost_estimate=cost_of(11.0),
        name="branch",
    )(order, a_tok, wo_slots, x, gain)


def branch_back_kernel(
    order_ref, dxn_ref, h1_ref, dy_ref, gain_ref, wo_ref, dh_ref, dz_ref, dg_ref, da_ref, dz_s
):
    @pl.when(pl.program_id(0) == 0)
    def _():
        h1, dxn = h1_ref[...], dxn_ref[...]
        scale = rms_scale(h1)
        hat = h1 * scale
        dg_ref[...] = jnp.sum(dxn * hat, axis=0, keepdims=True)
        e = dxn * gain_ref[...]
        dh = dy_ref[...].astype(f32) + scale * (e - hat * jnp.mean(e * hat, axis=-1, keepdims=True))
        dh_ref[...] = dh
        dz = dh.astype(bf16)
        dz_ref[...] = dz
        dz_s[...] = dz

    da_ref[0] = dot_nn(dz_s[...], wo_ref[0]).astype(bf16)


def branch_back(order, dxn, h1, dy, gain, wo_slots):
    n, depth, q_cols = wo_slots.shape
    rows = dxn.shape[0]
    const = lambda i, p: (0, 0)
    own = pl.BlockSpec((rows, depth), const)
    return pl.pallas_call(
        branch_back_kernel,
        grid_spec=pltpu.PrefetchScalarGridSpec(
            num_scalar_prefetch=1,
            grid=(n,),
            in_specs=[
                own, own, own, pl.BlockSpec((1, depth), const),
                pl.BlockSpec((1, depth, q_cols), lambda i, p: (i, 0, 0)),
            ],
            out_specs=[
                own, own, pl.BlockSpec((1, depth), const),
                pl.BlockSpec((1, rows, q_cols), lambda i, p: (p[i], 0, 0)),
            ],
            scratch_shapes=[pltpu.VMEM((rows, depth), bf16)],
        ),
        out_shape=[
            jax.ShapeDtypeStruct((rows, depth), f32),
            jax.ShapeDtypeStruct((rows, depth), bf16),
            jax.ShapeDtypeStruct((1, depth), f32),
            jax.ShapeDtypeStruct((n, rows, q_cols), bf16),
        ],
        compiler_params=pltpu.CompilerParams(vmem_limit_bytes=VMEM_LIMIT),
        cost_estimate=cost_of(13.0),
        name="branch_back",
    )(order, dxn, h1, dy, gain, wo_slots)


def feed_kernel(count, *refs):
    x_pieces, y_pieces = refs[:count], refs[count : 2 * count]
    w_ref, d_ref, hm_ref, x_all, y_all, x_sem, y_sem = refs[2 * count :]
    step = pl.program_id(0)
    _, rows, depth = x_all.shape
    ff = hm_ref.shape[2]

    @pl.when(step == 0)
    def _():
        for xc, yc in zip(
            piece_copies(x_pieces, x_all, x_sem, rows), piece_copies(y_pieces, y_all, y_sem, rows)
        ):
            xc.start()
            yc.start()

    for k in range(2):
        slot = 2 * step + k
        pltpu.make_async_copy(x_all.at[slot], x_all.at[slot], x_sem.at[slot]).wait()
    at = pl.ds(2 * step, 2)
    y = dot_nn(x_all[at].reshape(2 * rows, depth), w_ref[:, : 2 * ff])
    for k in range(2):
        slot = 2 * step + k
        pltpu.make_async_copy(y_all.at[slot], y_all.at[slot], y_sem.at[slot]).wait()
    dhm = dot_nn(y_all[at].reshape(2 * rows, depth), w_ref[:, 2 * ff :])
    g, u = y[:, :ff], y[:, ff:]
    sigma = jax.nn.sigmoid(g)
    silu = g * sigma
    hm_ref[...] = (silu * u).astype(bf16).reshape(2, rows, ff)
    d_ref[:, :, :ff] = (
        (dhm * u * sigma * (1.0 + g * (1.0 - sigma))).astype(bf16).reshape(2, rows, ff)
    )
    d_ref[:, :, ff:] = (dhm * silu).astype(bf16).reshape(2, rows, ff)


def feed(x_pieces, y_pieces, n, w):
    depth, ff = w.shape[0], w.shape[1] // 3
    total = sum(p.shape[0] for p in x_pieces)
    rows = total // n
    return pl.pallas_call(
        functools.partial(feed_kernel, len(x_pieces)),
        grid=(n // 2,),
        in_specs=[any_spec() for _ in x_pieces + y_pieces]
        + [pl.BlockSpec(w.shape, lambda i: (0, 0))],
        out_specs=[
            pl.BlockSpec((2, rows, 2 * ff), lambda i: (i, 0, 0)),
            pl.BlockSpec((2, rows, ff), lambda i: (i, 0, 0)),
        ],
        out_shape=[
            jax.ShapeDtypeStruct((n, rows, 2 * ff), bf16),
            jax.ShapeDtypeStruct((n, rows, ff), bf16),
        ],
        scratch_shapes=[
            pltpu.VMEM((n, rows, depth), bf16),
            pltpu.VMEM((n, rows, depth), bf16),
            pltpu.SemaphoreType.DMA((n,)),
            pltpu.SemaphoreType.DMA((n,)),
        ],
        compiler_params=pltpu.CompilerParams(vmem_limit_bytes=VMEM_LIMIT),
        cost_estimate=cost_of(17.0 * total * ff / (2048 * 384)),
        name="feed",
    )(*x_pieces, *y_pieces, w)


def per_device(
    n, n_fsdp, layer_input, dy, block_order, lengths, attn_gain, wq, wk, wv, q_gain, k_gain, wo,
    mlp_gain, wg, wu, wd,
):
    me = lax.axis_index("ctx")
    x, dy = layer_input[0], dy[0]
    rows, depth = x.shape
    total = n * rows
    shard = wq.shape[0]
    heads = QUERY_HEADS // n
    kv_share = max(n // KEY_VALUE_HEADS, 1)
    ff = wg.shape[1] // n
    q_cols = heads * HEAD_SIZE
    parts = 2 if ff % 256 == 0 else 1
    ff_part = ff // parts

    def cols(w, width, index):
        return lax.dynamic_slice_in_dim(w, index * width, width, axis=1)

    def whole(w):
        return lax.all_gather(w, "fsdp", axis=0, tiled=True)

    kv_index = me // kv_share
    w_in = jnp.concatenate(
        [cols(wq, q_cols, me), cols(wk, HEAD_SIZE, kv_index), cols(wv, HEAD_SIZE, kv_index)], axis=1
    )
    in_cols = w_in.shape[1]
    w_attn = jnp.concatenate([w_in, cols(wo, q_cols, me)], axis=1)
    width = w_attn.shape[1]
    gains = jnp.concatenate([attn_gain, mlp_gain])
    gain_rows = -(-gains.shape[0] // (16 * width)) * 16
    gains = jnp.pad(gains, (0, gain_rows * width - gains.shape[0])).reshape(gain_rows, width)
    pack = lax.all_gather(jnp.concatenate([w_attn, gains], axis=0), "fsdp", axis=0)
    w_in = pack[:, :shard, :in_cols].reshape(depth, in_cols)
    wo_c = pack[:, :shard, in_cols:].reshape(depth, q_cols)
    gains = pack[:, shard:].reshape(n_fsdp, -1)
    attn_gain = gains[:, :shard].reshape(1, depth).astype(f32)
    mlp_gain = gains[:, shard : 2 * shard].reshape(1, depth).astype(f32)
    x_pieces = gather_pieces(x, n)

    def feed_weights(part, gate):
        at = parts * me + part
        w = jnp.concatenate([cols(w, ff_part, at) for w in (wg, wu, wd)], axis=1)
        return whole(after(w, gate))

    w_ff = [feed_weights(0, x_pieces[0])]

    order = slot_order(n)
    by_index = block_order.reshape(-1)
    places = jnp.take(block_order, order, axis=0).reshape(-1)
    half = HEAD_SIZE // 2
    lane = jnp.arange(HEAD_SIZE, dtype=jnp.int32)
    frequency = jnp.exp(-math.log(rope_base) * 2.0 * (lane % half).astype(f32) / HEAD_SIZE)
    angle = jnp.arange(total, dtype=f32)[:, None] * frequency[None, :]
    cosine = jnp.cos(angle)
    sine = jnp.sin(angle) * jnp.where(lane < half, -1.0, 1.0)[None, :]
    qg = q_gain.astype(f32).reshape(1, HEAD_SIZE)
    kg = k_gain.astype(f32).reshape(1, HEAD_SIZE)

    xn, q_raw, k_raw, qb, kb, vb = project(
        x_pieces, n, places, attn_gain, pack, qg, kg, cosine, sine, heads
    )
    w_ff += [feed_weights(part, qb) for part in range(1, parts)]
    wo_pieces = gather_pieces(after(wo_c, x_pieces[-1]), n)
    wo_slots = assemble(wo_pieces, n)
    dy_pieces = gather_pieces(after(dy, wo_pieces[len(wo_pieces) // 2]), n)
    o, a, a_index, lse = attend(lengths, places, by_index, qb, kb, vb, heads)
    a_tok = exchange(a_index.reshape(n, rows, q_cols))
    a_tok = after(a_tok, dy_pieces[len(dy_pieces) // 2])
    h1, xn2 = branch(order, a_tok, wo_slots, x, mlp_gain)

    xn2_pieces = gather_pieces(xn2, n)
    d_gu, hm, grads = [], [], []
    for w in w_ff:
        if grads:
            xn2_pieces = [after(xn2_pieces[0], grads[-1])] + xn2_pieces[1:]
        d_part, hm_part = feed(xn2_pieces, dy_pieces, n, w)
        grads.append(
            weight_grad(
                [
                    (xn2_pieces, d_part.reshape(total, 2 * ff_part)),
                    (dy_pieces, hm_part.reshape(total, ff_part)),
                ],
                n, n_fsdp,
            )
        )
        d_gu.append(d_part)
        hm.append(hm_part)
    d_ff = [reduce_rows(grad, n) for grad in grads]
    d_xn2 = scatter_slots(d_gu, w_ff, 0, n)

    d_h1, dz, d_mlp_gain, da = branch_back(
        order, after(d_xn2, grads[-1]), h1, dy, mlp_gain, wo_slots
    )
    da = exchange(da).reshape(total, q_cols)
    m = scatter_slots([after(hm[0], d_h1)] + hm[1:], w_ff, 2, n)
    output = (h1 + m).astype(bf16)
    dz_pieces = gather_pieces(dz, n)
    d_qkv, d_qg, d_kg, *key_sums = attend_back(
        lengths, places, by_index, qb, kb, vb, da, o, lse, q_raw, k_raw, qg, kg, cosine, sine,
        heads, kv_share == 1,
    )
    if kv_share > 1:
        groups = [list(range(g, g + kv_share)) for g in range(0, n, kv_share)]
        first = (me % kv_share == 0).astype(f32)
        dk, dv = (
            lax.psum(t, "ctx", axis_index_groups=groups).astype(bf16).astype(f32) * first
            for t in key_sums
        )
        grad = dk * cosine - jnp.roll(dk, half, axis=1) * sine
        scale = rms_scale(k_raw)
        hat = k_raw * scale
        d_kg = jnp.sum(grad * hat, axis=0, keepdims=True)
        grad = grad * kg
        dk = scale * (grad - hat * jnp.mean(grad * hat, axis=-1, keepdims=True))
        d_kv = jnp.concatenate([dk, dv], axis=1).astype(bf16).reshape(2 * n, -1, 2 * HEAD_SIZE)
        d_qkv = jnp.concatenate([d_qkv, d_kv[places].reshape(total, -1)], axis=1)
    d_attn = weight_grad([([xn.reshape(total, depth)], d_qkv), (dz_pieces, a)], n, n_fsdp)
    d_xn = scatter_slots([d_qkv.reshape(n, rows, in_cols)], [w_in], 0, n)
    d_attn = reduce_rows(d_attn, n)
    x_float = x.astype(f32)
    scale_one = rms_scale(x_float)
    hat_one = x_float * scale_one
    d_attn_gain = jnp.sum(d_xn * hat_one, axis=0)
    e = d_xn * attn_gain
    dx = d_h1 + scale_one * (e - hat_one * jnp.mean(e * hat_one, axis=-1, keepdims=True))

    sums = sum_all(
        jnp.concatenate([d_attn_gain, d_mlp_gain[0], d_qg[0], d_kg[0]]).reshape(-1, HEAD_SIZE),
        n, n_fsdp,
    ).reshape(-1)
    d_ff = exchange(after(jnp.concatenate(d_ff, axis=2), d_qkv))
    d_attn = exchange(d_attn)
    starts = range(0, 3 * ff, 3 * ff_part)
    d_wg, d_wu, d_wd = join_columns(
        d_ff, [[(t + k * ff_part, t + (k + 1) * ff_part) for t in starts] for k in range(3)]
    )
    k_cols, v_cols = q_cols + HEAD_SIZE, q_cols + 2 * HEAD_SIZE
    d_wq, d_wo = join_columns(d_attn, [[(0, q_cols)], [(v_cols, v_cols + q_cols)]])
    d_wk, d_wv = join_columns(d_attn[::kv_share], [[(q_cols, k_cols)], [(k_cols, v_cols)]])
    return (
        output[None],
        dx[None],
        d_wq,
        d_wk,
        d_wv,
        d_wo,
        d_wg,
        d_wu,
        d_wd,
        sums[:depth],
        sums[depth : 2 * depth],
        sums[2 * depth : 2 * depth + HEAD_SIZE],
        sums[2 * depth + HEAD_SIZE :],
    )


def solution(mesh):
    n, n_fsdp = mesh.shape["ctx"], mesh.shape["fsdp"]
    row, act = P("fsdp", None), P("fsdp", "ctx", None)
    own = P(("ctx", "fsdp"), None)
    return jax.shard_map(
        functools.partial(per_device, n, n_fsdp),
        mesh=mesh,
        in_specs=(
            act, act, P(), P("fsdp"), P("fsdp"), row, row, row, P(), P(), row, P("fsdp"), row, row, row,
        ),
        out_specs=(act, act) + (own,) * 7 + (P(),) * 4,
        check_vma=False,
    )
```

time: 837 us -> 682 us (0.81)
  Pallas kernels: 57.2 us -> 273 us
  matrix products: 143 us -> 0 us
  local copies, waits for them, and re-layouts: 135 us -> 24.9 us
  other arithmetic: 82 us -> 34.6 us
  blocking collectives: 38.7 us -> 0 us
  starting transfers between devices: 67.9 us -> 45.4 us
  waiting for transfers between devices: 289 us -> 279 us
    pallas_call x2 -> x22, Pallas kernels: 42.7 us -> 255 us  [the longest x6 53.3 us: mm_slots(): pl.pallas_call(functools.partial(mm_kernel, len(lefts)), grid=(count,), i...]
    dot_general x19 -> x0, matrix products: 143 us -> none  [the longest x10 56.7 us: dot_nt(): lax.dot_general(left, right, (((1,), (1,)), ((), ())), preferred_element_...]
    unnamed x180 -> x60, local copies, waits for them, and re-layouts: 59.3 us -> 9.06 us
    add x8 -> x6, other arithmetic: 44.2 us -> 1.82 us  [the longest x1 1.79 us: scatter_slots(): return keep[0] + got[0].astype(f32) + swap_first(last, n, True).astype(f32)]
    psum x1 -> x0, blocking collectives: 38.7 us -> none  [per_device(): lax.psum(jnp.concatenate([d_attn_gain, d_mlp_gain, d_qg[0], d_kg[0]]), ('...]
    ppermute x91 -> x34, starting transfers between devices: 66.9 us -> 28.5 us  [the longest x16 20.8 us: swap_first(): lax.ppermute(values, 'ctx', [(c, c ^ (2 if (c % 2 == 0) == first else 4))...]
    reduce_scatter x5 -> x3, waiting for transfers between devices: 35.2 us -> 0.02 us  [reduce_rows(): summed = lax.psum_scatter(grad, 'fsdp', scatter_dimension=0, tiled=True)]
    all_gather x1, waiting for transfers between devices: 0.01 us -> 28.6 us  [per_device(): lax.all_gather(jnp.concatenate([w_attn, gains], axis=0), 'fsdp', axis=0)]
  transfers between devices with their start and end apart: 101 -> 44, of which waited for: 43 -> 21; matrix products, arithmetic and copies ran while one was open for 37% -> 9% of each run, Pallas kernels for 7% -> 35%
where the time goes in v2:
time: 682 us; the launch traced here: 672 us
  waiting for transfers between devices  279 us (41%)
  Pallas kernels  273 us (40%)
  starting transfers between devices  45.4 us (7%)
  other arithmetic  34.6 us (5%)
  local copies, waits for them, and re-layouts  24.9 us (4%)
  between operations  15.6 us (2%)
    ppermute x16, waiting for transfers between devices, swap_first(): lax.ppermute(values, 'ctx', [(c, c ^ (2 if (c % 2 == 0) == first else 4))...  194 us
    pallas_call x6, Pallas kernels, mm_slots(): pl.pallas_call(functools.partial(mm_kernel, len(lefts)), grid=(count,), i...  53.3 us
    pallas_call x3, Pallas kernels, weight_grad(): pl.pallas_call(functools.partial(weight_kernel, [len(pieces) for pieces,...  49.1 us
    pallas_call x2, Pallas kernels, feed(): pl.pallas_call(functools.partial(feed_kernel, len(x_pieces)), grid=(n //...  36.7 us
    pallas_call x1, Pallas kernels, attend_back(): pl.pallas_call(functools.partial(attend_back_kernel, heads, tile, finish_...  32 us
    all_gather x1, waiting for transfers between devices, per_device(): lax.all_gather(jnp.concatenate([w_attn, gains], axis=0), 'fsdp', axis=0)  28.6 us
    all_to_all x4, waiting for transfers between devices, exchange(): return lax.all_to_all(blocks, 'ctx', 0, 0, tiled=True)  27.8 us
    ppermute x16, starting transfers between devices, swap_first(): lax.ppermute(values, 'ctx', [(c, c ^ (2 if (c % 2 == 0) == first else 4))...  20.8 us
  transfers between devices with their start and end apart: 44, of which 21 were waited for; matrix products, arithmetic and copies ran while one was open for 9% of the time, Pallas kernels for 35%

profile of v2, /device:TPU:0, one launch (start us, length us, event | category | flops | bytes accessed | tf_op | source)
XLA Modules:
  0.0 672.4 jit_solution(8523732055887509172)
XLA Ops:
  14.1 9.2 %collective-permute-done = bf16[256,2048]{1,0:T(8,128)(2,1)} collective-permute-done((bf16[256,2048]{1,0:T(8,128)(2,1)}, bf16[256,2048]{1,0:T(8,128)(2,1)}, u32[]{:S(2)}, u32[]{:S(2)}) %collective-permute-start) | collective-permute-done | bytes 1048608 | tf_op jit(solution)/shard_map/ppermute | solution.py:51
  27.0 24.1 %collective-permute-done.1.refs_1_ = bf16[512,2048]{1,0:T(8,128)(2,1)} collective-permute-done((bf16[512,2048]{1,0:T(8,128)(2,1)S(1)}, bf16[512,2048]{1,0:T(8,128)(2,1)}, u32[]{:S(2)}, u32[]{:S(2)}) %collective-permute-start.1) | collective-permute-done | bytes 2097184 | tf_op jit(solution)/shard_map/ppermute | solution.py:51
  51.1 28.6 %all-gather.9.cloned.1.call-done = bf16[2112,768]{1,0:T(8,128)(2,1)} async-done(((bf16[528,768]{1,0:T(8,128)(2,1)}), bf16[2112,768]{1,0:T(8,128)(2,1)}) %all-gather.9.cloned.1.call-update) | async-done | bytes 3244048 | tf_op jit(solution)/shard_map/all_gather | solution.py:780
  83.8 12.2 %collective-permute-done.4 = bf16[2048,256]{1,0:T(8,128)(2,1)} collective-permute-done((bf16[2048,256]{1,0:T(8,128)(2,1)S(1)}, bf16[2048,256]{1,0:T(8,128)(2,1)}, u32[]{:S(2)}, u32[]{:S(2)}) %collective-permute-start.4) | collective-permute-done | bytes 1048608 | tf_op jit(solution)/shard_map/ppermute | solution.py:51
  106.1 4.8 sine_multiply_fusion
  116.0 17.1 %project.1 = (bf16[8,256,2048]{2,1,0:T(8,128)(2,1)}, f32[2048,256]{1,0:T(8,128)}, f32[2048,128]{1,0:T(8,128)}, bf16[2048,256]{1,0:T(8,128)(2,1)}, bf16[2048,128]{1,0:T(8,128)(2,1)}, /*index=5*/bf16[2048,128]{1,0:T(8,128)(2,1)}) custom-call(s32[16]{0:T(128)} %select_n.79.place_ref, bf16[512,2048]{1,0:T(8,128)(2,1)} %copy-done.7, ...), custom_call_target="tpu_custom_call" | custom-call | flops 17600000000 | bytes 1048576 | tf_op jit(solution)/shard_map/project/pallas_call | solution.py:332
  133.2 15.3 %collective-permute-done.8.refs_1_ = bf16[4096,256]{1,0:T(8,128)(2,1)} collective-permute-done((bf16[4096,256]{1,0:T(8,128)(2,1)}, bf16[4096,256]{1,0:T(8,128)(2,1)}, u32[]{:S(2)}, u32[]{:S(2)}) %collective-permute-start.8) | collective-permute-done | bytes 2097184 | tf_op jit(solution)/shard_map/ppermute | solution.py:51
  151.2 18.7 %attend.1 = (f32[2048,256]{1,0:T(8,128)}, bf16[2048,256]{1,0:T(8,128)(2,1)}, bf16[2048,256]{1,0:T(8,128)(2,1)}, f32[2,2048]{1,0:T(2,128)}) custom-call(s32[1]{0:T(128)S(6)} %copy.42.length_ref, s32[16]{0:T(128)} %select_n.79.place_ref, s32[16]{0:T(128)} %reshape.188.index_ref, bf16[2048,256]{1,0:T(8,128)(2,1)} %get-tuple-element.58.q_ref, ...), custom_call_target="tpu_custom_call" | custom-call | flops 20349999104 | bytes 1048576 | tf_op jit(solution)/shard_map/attend/pallas_call | solution.py:432
  169.9 3.7 all-to-all-start
  174.2 6.6 assemble.1.wo_ref
  180.8 8.2 %all-to-all-done.a_ref = bf16[8,256,256]{2,1,0:T(8,128)(2,1)S(1)} async-done(((bf16[8,256,256]{2,1,0:T(8,128)(2,1)}), bf16[8,256,256]{2,1,0:T(8,128)(2,1)S(1)}, u32[]{:S(2)}, u32[]{:S(2)}) %all-to-all-start) | async-done | bytes 1048608 | tf_op jit(solution)/shard_map/all_to_all | solution.py:198
  189.9 11.0 %branch.1 = (f32[256,2048]{1,0:T(8,128)}, bf16[256,2048]{1,0:T(8,128)(2,1)}) custom-call(s32[8]{0:T(128)} %copy-done.20, bf16[8,256,256]{2,1,0:T(8,128)(2,1)} %copy-done.11, bf16[8,2048,256]{2,1,0:T(8,128)(2,1)} %assemble.1.wo_ref, bf16[256,2048]{1,0:T(8,128)(2,1)} %bitcast.89, f32[1,2048]{1,0:T(1,128)} %bitcast.115), custom_call_target="tpu_custom_call" | custom-call | flops 12099999744 | bytes 1048576 | tf_op jit(solution)/shard_map/branch/pallas_call | solution.py:610
  204.5 22.8 %collective-permute-done.10 = bf16[256,2048]{1,0:T(8,128)(2,1)S(1)} collective-permute-done((bf16[256,2048]{1,0:T(8,128)(2,1)}, bf16[256,2048]{1,0:T(8,128)(2,1)S(1)}, u32[]{:S(2)}, u32[]{:S(2)}) %collective-permute-start.10) | collective-permute-done | bytes 1048608 | tf_op jit(solution)/shard_map/ppermute | solution.py:51
  230.2 4.5 collective-permute-done.14.refs_5_.refs_6_
  236.6 20.4 %collective-permute-done.11.refs_1_ = bf16[512,2048]{1,0:T(8,128)(2,1)S(1)} collective-permute-done((bf16[512,2048]{1,0:T(8,128)(2,1)}, bf16[512,2048]{1,0:T(8,128)(2,1)S(1)}, u32[]{:S(2)}, u32[]{:S(2)}) %collective-permute-start.11) | collective-permute-done | bytes 2097184 | tf_op jit(solution)/shard_map/ppermute | solution.py:51
  259.2 3.9 collective-permute-done.13.refs_3_
  263.1 18.3 %feed.2 = (bf16[8,256,768]{2,1,0:T(8,128)(2,1)}, bf16[8,256,384]{2,1,0:T(8,128)(2,1)}) custom-call(bf16[512,2048]{1,0:T(8,128)(2,1)} %constant_dynamic-update-slice_fusion.4.refs_0_, bf16[512,2048]{1,0:T(8,128)(2,1)} %copy-done.23, bf16[512,2048]{1,0:T(8,128)(2,1)} %collective-permute-done.12.refs_2_, bf16[512,2048]{1,0:T(8,128)(2,1)} %collective-permute-done.13.refs_3_, ...), custom_call_target="tpu_custom_call" | custom-call | flops 18699999232 | bytes 1048576 | tf_op jit(solution)/shard_map/feed/pallas_call | solution.py:723
  281.5 17.4 %weight_grad.3 = bf16[4,8,64,1152]{3,2,1,0:T(8,128)(2,1)} custom-call(bf16[512,2048]{1,0:T(8,128)(2,1)} %constant_dynamic-update-slice_fusion.4.refs_0_, bf16[512,2048]{1,0:T(8,128)(2,1)} %copy-done.23, bf16[512,2048]{1,0:T(8,128)(2,1)} %collective-permute-done.12.refs_2_, bf16[512,2048]{1,0:T(8,128)(2,1)} %collective-permute-done.13.refs_3_, ...), custom_call_target="tpu_custom_call" | custom-call | flops 17600000000 | bytes 1048576 | tf_op jit(solution)/shard_map/weight_grad/pallas_call | solution.py:222
  298.9 18.0 %all-gather.7.cloned.1.call-done.refs_8_.refs_3_ = bf16[2048,1152]{1,0:T(8,128)(2,1)} async-done(((bf16[512,1152]{1,0:T(8,128)(2,1)}), bf16[2048,1152]{1,0:T(8,128)(2,1)}) %all-gather.7.cloned.1.call-update) | async-done | bytes 4718608 | tf_op jit(solution)/shard_map/all_gather | solution.py:768
  316.8 18.3 %feed.3 = (bf16[8,256,768]{2,1,0:T(8,128)(2,1)}, bf16[8,256,384]{2,1,0:T(8,128)(2,1)}) custom-call(bf16[512,2048]{1,0:T(8,128)(2,1)} %constant_dynamic-update-slice_fusion.4.refs_0_, bf16[512,2048]{1,0:T(8,128)(2,1)} %copy-done.23, bf16[512,2048]{1,0:T(8,128)(2,1)} %collective-permute-done.12.refs_2_, bf16[512,2048]{1,0:T(8,128)(2,1)} %collective-permute-done.13.refs_3_, ...), custom_call_target="tpu_custom_call" | custom-call | flops 18699999232 | bytes 1048576 | tf_op jit(solution)/shard_map/feed/pallas_call | solution.py:723
  335.2 11.5 %mm_slots.7 = bf16[4,256,2048]{2,1,0:T(8,128)(2,1)} custom-call(bf16[8,256,768]{2,1,0:T(8,128)(2,1)} %get-tuple-element.69.refs_0_, bf16[8,256,768]{2,1,0:T(8,128)(2,1)} %get-tuple-element.72.refs_1_, bf16[2048,1152]{1,0:T(8,128)(2,1)} %all-gather.5.cloned.1.call-done.refs_8_.refs_2_, bf16[2048,1152]{1,0:T(8,128)(2,1)} %all-gather.7.cloned.1.call-done.refs_8_.refs_3_), custom_call_target="tpu_custom_call" | custom-call | flops 12650000384 | bytes 1048576 | tf_op jit(solution)/shard_map/mm_slots/pallas_call | solution.py:143
  346.7 11.4 %mm_slots.6.mine_ref = bf16[4,256,2048]{2,1,0:T(8,128)(2,1)} custom-call(bf16[8,256,768]{2,1,0:T(8,128)(2,1)} %get-tuple-element.69.refs_0_, bf16[8,256,768]{2,1,0:T(8,128)(2,1)} %get-tuple-element.72.refs_1_, bf16[2048,1152]{1,0:T(8,128)(2,1)} %all-gather.5.cloned.1.call-done.refs_8_.refs_2_, bf16[2048,1152]{1,0:T(8,128)(2,1)} %all-gather.7.cloned.1.call-done.refs_8_.refs_3_), custom_call_target="tpu_custom_call" | custom-call | flops 12650000384 | bytes 1048576 | tf_op jit(solution)/shard_map/mm_slots/pallas_call | solution.py:143
  358.2 6.6 add_halves.3
  366.3 24.7 %collective-permute-done.17 = bf16[2,256,2048]{2,1,0:T(8,128)(2,1)S(1)} collective-permute-done((bf16[2,256,2048]{2,1,0:T(8,128)(2,1)}, bf16[2,256,2048]{2,1,0:T(8,128)(2,1)S(1)}, u32[]{:S(2)}, u32[]{:S(2)}) %collective-permute-start.17) | collective-permute-done | bytes 2097184 | tf_op jit(solution)/shard_map/ppermute | solution.py:51
  395.4 17.6 %weight_grad.4 = bf16[4,8,64,1152]{3,2,1,0:T(8,128)(2,1)} custom-call(bf16[512,2048]{1,0:T(8,128)(2,1)} %constant_dynamic-update-slice_fusion.4.refs_0_, bf16[512,2048]{1,0:T(8,128)(2,1)} %copy-done.23, bf16[512,2048]{1,0:T(8,128)(2,1)} %collective-permute-done.12.refs_2_, bf16[512,2048]{1,0:T(8,128)(2,1)} %collective-permute-done.13.refs_3_, ...), custom_call_target="tpu_custom_call" | custom-call | flops 17600000000 | bytes 1048576 | tf_op jit(solution)/shard_map/weight_grad/pallas_call | solution.py:222
  414.8 13.2 %branch_back.1 = (f32[256,2048]{1,0:T(8,128)}, bf16[256,2048]{1,0:T(8,128)(2,1)}, f32[1,2048]{1,0:T(1,128)}, bf16[8,256,256]{2,1,0:T(8,128)(2,1)}) custom-call(s32[8]{0:T(128)} %copy-done.20, f32[256,2048]{1,0:T(8,128)} %bitcast_add_fusion.2.dxn_ref, f32[256,2048]{1,0:T(8,128)} %get-tuple-element.65.h1_ref, bf16[256,2048]{1,0:T(8,128)(2,1)} %bitcast.105, ...), custom_call_target="tpu_custom_call" | custom-call | flops 14300000256 | bytes 1048576 | tf_op jit(solution)/shard_map/branch_back/pallas_call | solution.py:658
  428.0 4.2 all-to-all-start.1
  436.8 10.9 %all-to-all-done.1 = bf16[8,256,256]{2,1,0:T(8,128)(2,1)} async-done(((bf16[8,256,256]{2,1,0:T(8,128)(2,1)}), bf16[8,256,256]{2,1,0:T(8,128)(2,1)}, u32[]{:S(2)}, u32[]{:S(2)}) %all-to-all-start.1) | async-done | bytes 1048608 | tf_op jit(solution)/shard_map/all_to_all | solution.py:198
  447.7 32.0 %attend_back.1 = (bf16[2048,512]{1,0:T(8,128)(2,1)}, f32[1,128]{1,0:T(1,128)}, f32[1,128]{1,0:T(1,128)}) custom-call(s32[1]{0:T(128)S(6)} %copy.42.length_ref, s32[16]{0:T(128)} %select_n.79.place_ref, s32[16]{0:T(128)} %reshape.188.index_ref, bf16[2048,256]{1,0:T(8,128)(2,1)} %get-tuple-element.58.q_ref, bf16[2048,128]{1,0:T(8,128)(2,1)} %get-tuple-element.59.k_ref, ...), custom_call_target="tpu_custom_call" | custom-call | flops 36300001280 | bytes 1048576 | tf_op jit(solution)/shard_map/attend_back/pallas_call | solution.py:578
  479.8 6.3 mm_slots.11
  486.9 8.5 %mm_slots.9 = bf16[4,256,2048]{2,1,0:T(8,128)(2,1)} custom-call(bf16[8,256,384]{2,1,0:T(8,128)(2,1)} %get-tuple-element.78.refs_0_, bf16[8,256,384]{2,1,0:T(8,128)(2,1)} %get-tuple-element.75.refs_1_, bf16[2048,1152]{1,0:T(8,128)(2,1)} %all-gather.5.cloned.1.call-done.refs_8_.refs_2_, bf16[2048,1152]{1,0:T(8,128)(2,1)} %all-gather.7.cloned.1.call-done.refs_8_.refs_3_), custom_call_target="tpu_custom_call" | custom-call | flops 8249999872 | bytes 1048576 | tf_op jit(solution)/shard_map/mm_slots/pallas_call | solution.py:143
  496.0 16.4 %collective-permute-done.26.refs_3_ = bf16[512,2048]{1,0:T(8,128)(2,1)S(1)} collective-permute-done((bf16[512,2048]{1,0:T(8,128)(2,1)S(1)}, bf16[512,2048]{1,0:T(8,128)(2,1)S(1)}, u32[]{:S(2)}, u32[]{:S(2)}) %collective-permute-start.26) | collective-permute-done | bytes 2097184 | tf_op jit(solution)/shard_map/ppermute | solution.py:51
  512.4 7.0 %mm_slots.10.mine_ref = bf16[4,256,2048]{2,1,0:T(8,128)(2,1)} custom-call(bf16[8,256,512]{2,1,0:T(8,128)(2,1)} %bitcast.128, bf16[2048,512]{1,0:T(8,128)(2,1)} %bitcast.101), custom_call_target="tpu_custom_call" | custom-call | flops 6783333376 | bytes 1048576 | tf_op jit(solution)/shard_map/mm_slots/pallas_call | solution.py:143
  519.4 6.5 add_halves.5
  526.6 14.1 %weight_grad.5 = bf16[4,8,64,768]{3,2,1,0:T(8,128)(2,1)} custom-call(bf16[2048,2048]{1,0:T(8,128)(2,1)} %bitcast.124, bf16[2048,512]{1,0:T(8,128)(2,1)} %get-tuple-element.86.refs_1_, bf16[512,2048]{1,0:T(8,128)(2,1)} %copy-done.12, bf16[512,2048]{1,0:T(8,128)(2,1)} %copy-done.24, bf16[512,2048]{1,0:T(8,128)(2,1)} %collective-permute-done.27.refs_4_, ...), custom_call_target="tpu_custom_call" | custom-call | flops 11733332992 | bytes 1048576 | tf_op jit(solution)/shard_map/weight_grad/pallas_call | solution.py:222
  540.7 8.5 %mm_slots.8.mine_ref = bf16[4,256,2048]{2,1,0:T(8,128)(2,1)} custom-call(bf16[8,256,384]{2,1,0:T(8,128)(2,1)} %get-tuple-element.78.refs_0_, bf16[8,256,384]{2,1,0:T(8,128)(2,1)} %get-tuple-element.75.refs_1_, bf16[2048,1152]{1,0:T(8,128)(2,1)} %all-gather.5.cloned.1.call-done.refs_8_.refs_2_, bf16[2048,1152]{1,0:T(8,128)(2,1)} %all-gather.7.cloned.1.call-done.refs_8_.refs_3_), custom_call_target="tpu_custom_call" | custom-call | flops 8249999872 | bytes 1048576 | tf_op jit(solution)/shard_map/mm_slots/pallas_call | solution.py:143
  549.2 6.4 add_halves.4
  560.2 4.4 all-to-all-start.3
  569.0 36.5 %collective-permute-done.20 = bf16[2,256,2048]{2,1,0:T(8,128)(2,1)} collective-permute-done((bf16[2,256,2048]{2,1,0:T(8,128)(2,1)}, bf16[2,256,2048]{2,1,0:T(8,128)(2,1)}, u32[]{:S(2)}, u32[]{:S(2)}) %collective-permute-start.20) | collective-permute-done | bytes 2097184 | tf_op jit(solution)/shard_map/ppermute | solution.py:51
  608.1 7.9 %collective-permute-done.24 = bf16[256,2048]{1,0:T(8,128)(2,1)S(1)} collective-permute-done((bf16[256,2048]{1,0:T(8,128)(2,1)S(1)}, bf16[256,2048]{1,0:T(8,128)(2,1)S(1)}, u32[]{:S(2)}, u32[]{:S(2)}) %collective-permute-start.24) | collective-permute-done | bytes 1048608 | tf_op jit(solution)/shard_map/ppermute | solution.py:51
  621.3 6.1 join_columns.5
  629.9 4.4 fusion.15
  634.4 3.8 collective-permute-done.32
  638.2 4.2 all-to-all-start.2
  642.4 4.8 fusion.7
  648.4 6.7 all-to-all-done.2.got_ref
  655.0 5.0 join_columns.4
  660.0 5.1 join_columns.3
  (175 shorter events, 78.9 us)
Async XLA Ops:
  7.2 72.5 %all-gather.9.cloned.1.call-start = ((), (), s32[]{:S(2)}) async-start(), calls=%async_computation.12 | async-start | bytes 4055040 | tf_op jit(solution)/shard_map/all_gather | solution.py:780
  7.2 16.1 %collective-permute-start = (bf16[256,2048]{1,0:T(8,128)(2,1)}, bf16[256,2048]{1,0:T(8,128)(2,1)}, u32[]{:S(2)}, u32[]{:S(2)}) collective-permute-start(bf16[256,2048]{1,0:T(8,128)(2,1)} %bitcast.88), channel_id=1, source_target_pairs={{0,8},{4,20},{8,0},{12,28},{16,24},{20,4},{24,16},{28,12},{1,9},{5... | collective-permute-start | bytes 3145736 | tf_op jit(solution)/shard_map/ppermute | solution.py:51
  14.1 245.2 %all-gather.5.cloned.1.call-start = ((), (), s32[]{:S(2)}) async-start(), calls=%async_computation.7 | async-start | bytes 5898240 | tf_op jit(solution)/shard_map/all_gather | solution.py:768
  24.8 58.9 %copy-start.7 = (bf16[512,2048]{1,0:T(8,128)(2,1)}, bf16[512,2048]{1,0:T(8,128)(2,1)S(1)}, u32[]{:S(2)}) copy-start(bf16[512,2048]{1,0:T(8,128)(2,1)S(1)} %pad_maximum_fusion.1.refs_0_) | copy-start | bytes 6291460
  24.9 57.7 %copy-start.21 = (s32[8]{0:T(128)S(1)}, s32[8]{0:T(128)}, u32[]{:S(2)}) copy-start(s32[8]{0:T(128)} %constant.100.clone) | copy-start | bytes 100
  24.9 57.7 %copy-start.22 = (s32[8]{0:T(128)S(1)}, s32[8]{0:T(128)}, u32[]{:S(2)}) copy-start(s32[8]{0:T(128)} %constant.99.clone) | copy-start | bytes 100
  24.9 26.2 %collective-permute-start.1 = (bf16[512,2048]{1,0:T(8,128)(2,1)S(1)}, bf16[512,2048]{1,0:T(8,128)(2,1)}, u32[]{:S(2)}, u32[]{:S(2)}) collective-permute-start(bf16[512,2048]{1,0:T(8,128)(2,1)S(1)} %pad_maximum_fusion.1.refs_0_), channel_id=1, source_target_pairs={{0,16},{4,12},{8,24},{12,4},{16,0},{20,28},{24,8},{28,20},{1,17},{... | collective-permute-start | bytes 6291464 | tf_op jit(solution)/shard_map/ppermute | solution.py:51
  51.1 29.9 %collective-permute-start.3 = (bf16[512,2048]{1,0:T(8,128)(2,1)}, bf16[512,2048]{1,0:T(8,128)(2,1)}, u32[]{:S(2)}, u32[]{:S(2)}) collective-permute-start(bf16[512,2048]{1,0:T(8,128)(2,1)} %collective-permute-done.1.refs_1_), channel_id=1, source_target_pairs={{0,4},{4,0},{8,12},{12,8},{16,20},{20,16},{24,28},{28,24},{1,5},{5... | collective-permute-start | bytes 6291464 | tf_op jit(solution)/shard_map/ppermute | solution.py:47
  81.0 15.0 %collective-permute-start.4 = (bf16[2048,256]{1,0:T(8,128)(2,1)S(1)}, bf16[2048,256]{1,0:T(8,128)(2,1)}, u32[]{:S(2)}, u32[]{:S(2)}) collective-permute-start(bf16[2048,256]{1,0:T(8,128)(2,1)S(1)} %bitcast.93), channel_id=1, source_target_pairs={{0,8},{4,20},{8,0},{12,28},{16,24},{20,4},{24,16},{28,12},{1,9},{5... | collective-permute-start | bytes 3145736 | tf_op jit(solution)/shard_map/ppermute | solution.py:51
  82.6 33.5 %collective-permute-start.2 = (bf16[512,2048]{1,0:T(8,128)(2,1)S(1)}, bf16[512,2048]{1,0:T(8,128)(2,1)}, u32[]{:S(2)}, u32[]{:S(2)}) collective-permute-start(bf16[512,2048]{1,0:T(8,128)(2,1)S(1)} %pad_maximum_fusion.1.refs_0_), channel_id=1, source_target_pairs={{0,4},{4,0},{8,12},{12,8},{16,20},{20,16},{24,28},{28,24},{1,5},{5... | collective-permute-start | bytes 6291464 | tf_op jit(solution)/shard_map/ppermute | solution.py:47
  98.2 16.3 %collective-permute-start.5 = (bf16[4096,256]{1,0:T(8,128)(2,1)}, bf16[4096,256]{1,0:T(8,128)(2,1)}, u32[]{:S(2)}, u32[]{:S(2)}) collective-permute-start(bf16[4096,256]{1,0:T(8,128)(2,1)} %constant_dynamic-update-slice_fusion.refs_0_), channel_id=1, source_target_pairs={{0,4},{4,0},{8,12},{12,8},{16,20},{20,16},{24,28},{28,24},{1,5},{5... | collective-permute-start | bytes 6291464 | tf_op jit(solution)/shard_map/ppermute | solution.py:47
  110.9 37.7 %collective-permute-start.8 = (bf16[4096,256]{1,0:T(8,128)(2,1)}, bf16[4096,256]{1,0:T(8,128)(2,1)}, u32[]{:S(2)}, u32[]{:S(2)}) collective-permute-start(bf16[4096,256]{1,0:T(8,128)(2,1)} %constant_dynamic-update-slice_fusion.refs_0_), channel_id=1, source_target_pairs={{0,16},{4,12},{8,24},{12,4},{16,0},{20,28},{24,8},{28,20},{1,17},{... | collective-permute-start | bytes 6291464 | tf_op jit(solution)/shard_map/ppermute | solution.py:51
  114.6 35.0 %collective-permute-start.6 = (bf16[256,2048]{1,0:T(8,128)(2,1)}, bf16[256,2048]{1,0:T(8,128)(2,1)S(1)}, u32[]{:S(2)}, u32[]{:S(2)}) collective-permute-start(bf16[256,2048]{1,0:T(8,128)(2,1)} %bitcast.104), channel_id=1, source_target_pairs={{0,8},{4,20},{8,0},{12,28},{16,24},{20,4},{24,16},{28,12},{1,9},{5... | collective-permute-start | bytes 3145736 | tf_op jit(solution)/shard_map/ppermute | solution.py:51
  148.5 25.7 %collective-permute-start.9 = (bf16[4096,256]{1,0:T(8,128)(2,1)}, bf16[4096,256]{1,0:T(8,128)(2,1)}, u32[]{:S(2)}, u32[]{:S(2)}) collective-permute-start(bf16[4096,256]{1,0:T(8,128)(2,1)} %collective-permute-done.8.refs_1_), channel_id=1, source_target_pairs={{0,4},{4,0},{8,12},{12,8},{16,20},{20,16},{24,28},{28,24},{1,5},{5... | collective-permute-start | bytes 6291464 | tf_op jit(solution)/shard_map/ppermute | solution.py:47
  150.7 38.2 %collective-permute-start.7 = (bf16[512,2048]{1,0:T(8,128)(2,1)}, bf16[512,2048]{1,0:T(8,128)(2,1)}, u32[]{:S(2)}, u32[]{:S(2)}) collective-permute-start(bf16[512,2048]{1,0:T(8,128)(2,1)} %constant_dynamic-update-slice_fusion.2.refs_4_.refs_5_), channel_id=1, source_target_pairs={{0,4},{4,0},{8,12},{12,8},{16,20},{20,16},{24,28},{28,24},{1,5},{5... | collective-permute-start | bytes 6291464 | tf_op jit(solution)/shard_map/ppermute | solution.py:47
  169.9 19.1 %all-to-all-start = ((bf16[8,256,256]{2,1,0:T(8,128)(2,1)}), bf16[8,256,256]{2,1,0:T(8,128)(2,1)S(1)}, u32[]{:S(2)}, u32[]{:S(2)}) async-start(bf16[8,256,256]{2,1,0:T(8,128)(2,1)} %bitcast.107), calls=%async_computation | async-start | bytes 2097152 | tf_op jit(solution)/shard_map/all_to_all | solution.py:198
  173.6 143.3 %all-gather.7.cloned.1.call-start = ((), (), s32[]{:S(2)}) async-start(), calls=%async_computation.8 | async-start | bytes 5898240 | tf_op jit(solution)/shard_map/all_gather | solution.py:768
  201.0 26.3 %collective-permute-start.10 = (bf16[256,2048]{1,0:T(8,128)(2,1)}, bf16[256,2048]{1,0:T(8,128)(2,1)S(1)}, u32[]{:S(2)}, u32[]{:S(2)}) collective-permute-start(bf16[256,2048]{1,0:T(8,128)(2,1)} %get-tuple-element.66), channel_id=1, source_target_pairs={{0,8},{4,20},{8,0},{12,28},{16,24},{20,4},{24,16},{28,12},{1,9},{5... | collective-permute-start | bytes 3145736 | tf_op jit(solution)/shard_map/ppermute | solution.py:51
  201.5 33.2 %collective-permute-start.14 = (bf16[512,2048]{1,0:T(8,128)(2,1)}, bf16[512,2048]{1,0:T(8,128)(2,1)}, u32[]{:S(2)}, u32[]{:S(2)}) collective-permute-start(bf16[512,2048]{1,0:T(8,128)(2,1)} %constant_dynamic-update-slice_fusion.2.refs_4_.refs_5_), channel_id=1, source_target_pairs={{0,16},{4,12},{8,24},{12,4},{16,0},{20,28},{24,8},{28,20},{1,17},{... | collective-permute-start | bytes 6291464 | tf_op jit(solution)/shard_map/ppermute | solution.py:51
  228.3 28.7 %collective-permute-start.11 = (bf16[512,2048]{1,0:T(8,128)(2,1)}, bf16[512,2048]{1,0:T(8,128)(2,1)S(1)}, u32[]{:S(2)}, u32[]{:S(2)}) collective-permute-start(bf16[512,2048]{1,0:T(8,128)(2,1)} %constant_dynamic-update-slice_fusion.4.refs_0_), channel_id=1, source_target_pairs={{0,16},{4,12},{8,24},{12,4},{16,0},{20,28},{24,8},{28,20},{1,17},{... | collective-permute-start | bytes 6291464 | tf_op jit(solution)/shard_map/ppermute | solution.py:51
  229.9 327.1 %reduce-scatter.6.cloned.1.call-start = ((), (), s32[]{:S(2)}) async-start(), calls=%async_computation.10 | async-start | bytes 5898240 | tf_op jit(solution)/shard_map/reduce_scatter | solution.py:236
  234.7 24.6 %collective-permute-start.15 = (bf16[512,2048]{1,0:T(8,128)(2,1)}, bf16[512,2048]{1,0:T(8,128)(2,1)}, u32[]{:S(2)}, u32[]{:S(2)}) collective-permute-start(bf16[512,2048]{1,0:T(8,128)(2,1)} %collective-permute-done.14.refs_5_.refs_6_), channel_id=1, source_target_pairs={{0,4},{4,0},{8,12},{12,8},{16,20},{20,16},{24,28},{28,24},{1,5},{5... | collective-permute-start | bytes 6291464 | tf_op jit(solution)/shard_map/ppermute | solution.py:47
  236.6 22.6 %collective-permute-start.12 = (bf16[512,2048]{1,0:T(8,128)(2,1)}, bf16[512,2048]{1,0:T(8,128)(2,1)}, u32[]{:S(2)}, u32[]{:S(2)}) collective-permute-start(bf16[512,2048]{1,0:T(8,128)(2,1)} %constant_dynamic-update-slice_fusion.4.refs_0_), channel_id=1, source_target_pairs={{0,4},{4,0},{8,12},{12,8},{16,20},{20,16},{24,28},{28,24},{1,5},{5... | collective-permute-start | bytes 6291464 | tf_op jit(solution)/shard_map/ppermute | solution.py:47
  257.0 6.1 collective-permute-start.13
  346.7 11.5 %collective-permute-start.16 = (bf16[4,256,2048]{2,1,0:T(8,128)(2,1)}, bf16[4,256,2048]{2,1,0:T(8,128)(2,1)}, u32[]{:S(2)}, u32[]{:S(2)}) collective-permute-start(bf16[4,256,2048]{2,1,0:T(8,128)(2,1)} %mm_slots.7), channel_id=1, source_target_pairs={{0,4},{4,0},{8,12},{12,8},{16,20},{20,16},{24,28},{28,24},{1,5},{5... | collective-permute-start | bytes 12582920 | tf_op jit(solution)/shard_map/ppermute | solution.py:47
  364.7 26.2 %collective-permute-start.17 = (bf16[2,256,2048]{2,1,0:T(8,128)(2,1)}, bf16[2,256,2048]{2,1,0:T(8,128)(2,1)S(1)}, u32[]{:S(2)}, u32[]{:S(2)}) collective-permute-start(bf16[2,256,2048]{2,1,0:T(8,128)(2,1)} %get-tuple-element.74), channel_id=1, source_target_pairs={{0,16},{4,12},{8,24},{12,4},{16,0},{20,28},{24,8},{28,20},{1,17},{... | collective-permute-start | bytes 6291464 | tf_op jit(solution)/shard_map/ppermute | solution.py:51
  393.8 19.1 %collective-permute-start.18 = (bf16[256,2048]{1,0:T(8,128)(2,1)}, bf16[256,2048]{1,0:T(8,128)(2,1)S(1)}, u32[]{:S(2)}, u32[]{:S(2)}) collective-permute-start(bf16[256,2048]{1,0:T(8,128)(2,1)} %fusion.12), channel_id=1, source_target_pairs={{0,8},{4,20},{8,0},{12,28},{16,24},{20,4},{24,16},{28,12},{1,9},{5... | collective-permute-start | bytes 3145736 | tf_op jit(solution)/shard_map/ppermute | solution.py:51
  428.0 19.8 %all-to-all-start.1 = ((bf16[8,256,256]{2,1,0:T(8,128)(2,1)}), bf16[8,256,256]{2,1,0:T(8,128)(2,1)}, u32[]{:S(2)}, u32[]{:S(2)}) async-start(bf16[8,256,256]{2,1,0:T(8,128)(2,1)} %get-tuple-element.81), calls=%async_computation.1 | async-start | bytes 2097152 | tf_op jit(solution)/shard_map/all_to_all | solution.py:198
  432.2 124.8 %reduce-scatter.8.cloned.1.call-start = ((), (), s32[]{:S(2)}) async-start(), calls=%async_computation.11 | async-start | bytes 5898240 | tf_op jit(solution)/shard_map/reduce_scatter | solution.py:236
  433.8 204.4 %reduce-scatter.4.cloned.1.call-start = ((), (), s32[]{:S(2)}) async-start(), calls=%async_computation.9 | async-start | bytes 3932160 | tf_op jit(solution)/shard_map/reduce_scatter | solution.py:236
  435.0 51.2 %collective-permute-start.25 = (bf16[256,2048]{1,0:T(8,128)(2,1)S(1)}, bf16[256,2048]{1,0:T(8,128)(2,1)S(1)}, u32[]{:S(2)}, u32[]{:S(2)}) collective-permute-start(bf16[256,2048]{1,0:T(8,128)(2,1)S(1)} %copy-done.10), channel_id=1, source_target_pairs={{0,8},{4,20},{8,0},{12,28},{16,24},{20,4},{24,16},{28,12},{1,9},{5... | collective-permute-start | bytes 3145736 | tf_op jit(solution)/shard_map/ppermute | solution.py:51
  486.1 33.3 %collective-permute-start.22 = (bf16[4,256,2048]{2,1,0:T(8,128)(2,1)}, bf16[4,256,2048]{2,1,0:T(8,128)(2,1)}, u32[]{:S(2)}, u32[]{:S(2)}) collective-permute-start(bf16[4,256,2048]{2,1,0:T(8,128)(2,1)} %mm_slots.11), channel_id=1, source_target_pairs={{0,4},{4,0},{8,12},{12,8},{16,20},{20,16},{24,28},{28,24},{1,5},{5... | collective-permute-start | bytes 12582920 | tf_op jit(solution)/shard_map/ppermute | solution.py:47
  486.3 26.1 %collective-permute-start.26 = (bf16[512,2048]{1,0:T(8,128)(2,1)S(1)}, bf16[512,2048]{1,0:T(8,128)(2,1)S(1)}, u32[]{:S(2)}, u32[]{:S(2)}) collective-permute-start(bf16[512,2048]{1,0:T(8,128)(2,1)S(1)} %constant_dynamic-update-slice_fusion.6.refs_2_), channel_id=1, source_target_pairs={{0,16},{4,12},{8,24},{12,4},{16,0},{20,28},{24,8},{28,20},{1,17},{... | collective-permute-start | bytes 6291464 | tf_op jit(solution)/shard_map/ppermute | solution.py:51
  495.3 53.8 %collective-permute-start.19 = (bf16[4,256,2048]{2,1,0:T(8,128)(2,1)}, bf16[4,256,2048]{2,1,0:T(8,128)(2,1)}, u32[]{:S(2)}, u32[]{:S(2)}) collective-permute-start(bf16[4,256,2048]{2,1,0:T(8,128)(2,1)} %mm_slots.9), channel_id=1, source_target_pairs={{0,4},{4,0},{8,12},{12,8},{16,20},{20,16},{24,28},{28,24},{1,5},{5... | collective-permute-start | bytes 12582920 | tf_op jit(solution)/shard_map/ppermute | solution.py:47
  495.9 30.7 %collective-permute-start.27 = (bf16[512,2048]{1,0:T(8,128)(2,1)S(1)}, bf16[512,2048]{1,0:T(8,128)(2,1)}, u32[]{:S(2)}, u32[]{:S(2)}) collective-permute-start(bf16[512,2048]{1,0:T(8,128)(2,1)S(1)} %constant_dynamic-update-slice_fusion.6.refs_2_), channel_id=1, source_target_pairs={{0,4},{4,0},{8,12},{12,8},{16,20},{20,16},{24,28},{28,24},{1,5},{5... | collective-permute-start | bytes 6291464 | tf_op jit(solution)/shard_map/ppermute | solution.py:47
  512.4 14.2 %collective-permute-start.28 = (bf16[512,2048]{1,0:T(8,128)(2,1)S(1)}, bf16[512,2048]{1,0:T(8,128)(2,1)}, u32[]{:S(2)}, u32[]{:S(2)}) collective-permute-start(bf16[512,2048]{1,0:T(8,128)(2,1)S(1)} %collective-permute-done.26.refs_3_), channel_id=1, source_target_pairs={{0,4},{4,0},{8,12},{12,8},{16,20},{20,16},{24,28},{28,24},{1,5},{5... | collective-permute-start | bytes 6291464 | tf_op jit(solution)/shard_map/ppermute | solution.py:47
  525.9 38.7 %collective-permute-start.23 = (bf16[2,256,2048]{2,1,0:T(8,128)(2,1)}, bf16[2,256,2048]{2,1,0:T(8,128)(2,1)S(1)}, u32[]{:S(2)}, u32[]{:S(2)}) collective-permute-start(bf16[2,256,2048]{2,1,0:T(8,128)(2,1)} %get-tuple-element.88), channel_id=1, source_target_pairs={{0,16},{4,12},{8,24},{12,4},{16,0},{20,28},{24,8},{28,20},{1,17},{... | collective-permute-start | bytes 6291464 | tf_op jit(solution)/shard_map/ppermute | solution.py:51
  555.6 49.9 %collective-permute-start.20 = (bf16[2,256,2048]{2,1,0:T(8,128)(2,1)}, bf16[2,256,2048]{2,1,0:T(8,128)(2,1)}, u32[]{:S(2)}, u32[]{:S(2)}) collective-permute-start(bf16[2,256,2048]{2,1,0:T(8,128)(2,1)} %get-tuple-element.80), channel_id=1, source_target_pairs={{0,16},{4,12},{8,24},{12,4},{16,0},{20,28},{24,8},{28,20},{1,17},{... | collective-permute-start | bytes 6291464 | tf_op jit(solution)/shard_map/ppermute | solution.py:51
  560.2 61.0 %all-to-all-start.3 = ((bf16[8,64,2304]{2,1,0:T(8,128)(2,1)}), bf16[8,64,2304]{2,1,0:T(8,128)(2,1)}, u32[]{:S(2)}, u32[]{:S(2)}) async-start(bf16[8,64,2304]{2,1,0:T(8,128)(2,1)} %pad_maximum_fusion), calls=%async_computation.6 | async-start | bytes 4718592 | tf_op jit(solution)/shard_map/all_to_all | solution.py:198
  564.6 40.8 %copy-start.4 = (f32[2,256,2048]{2,1,0:T(8,128)S(1)}, f32[2,256,2048]{2,1,0:T(8,128)}, u32[]{:S(2)}) copy-start(f32[2,256,2048]{2,1,0:T(8,128)} %get-tuple-element.79) | copy-start | bytes 12582916
  566.7 49.4 %collective-permute-start.24 = (bf16[256,2048]{1,0:T(8,128)(2,1)S(1)}, bf16[256,2048]{1,0:T(8,128)(2,1)S(1)}, u32[]{:S(2)}, u32[]{:S(2)}) collective-permute-start(bf16[256,2048]{1,0:T(8,128)(2,1)S(1)} %fusion.14), channel_id=1, source_target_pairs={{0,8},{4,20},{8,0},{12,28},{16,24},{20,4},{24,16},{28,12},{1,9},{5... | collective-permute-start | bytes 3145736 | tf_op jit(solution)/shard_map/ppermute | solution.py:51
  608.1 21.8 %collective-permute-start.21 = (bf16[256,2048]{1,0:T(8,128)(2,1)}, bf16[256,2048]{1,0:T(8,128)(2,1)}, u32[]{:S(2)}, u32[]{:S(2)}) collective-permute-start(bf16[256,2048]{1,0:T(8,128)(2,1)} %fusion.13), channel_id=1, source_target_pairs={{0,8},{4,20},{8,0},{12,28},{16,24},{20,4},{24,16},{28,12},{1,9},{5... | collective-permute-start | bytes 3145736 | tf_op jit(solution)/shard_map/ppermute | solution.py:51
  617.2 1.3 collective-permute-start.29
  618.4 10.1 %collective-permute-start.30 = (f32[34,128]{1,0:T(8,128)S(1)}, f32[34,128]{1,0:T(8,128)S(1)}, u32[]{:S(2)}, u32[]{:S(2)}) collective-permute-start(f32[34,128]{1,0:T(8,128)S(1)} %fusion.24), channel_id=1, source_target_pairs={{0,8},{4,12},{8,0},{12,4},{16,24},{20,28},{24,16},{28,20},{1,9},{5... | collective-permute-start | bytes 52232 | tf_op jit(solution)/shard_map/ppermute | solution.py:47
  628.6 5.7 collective-permute-start.31
  634.3 3.8 collective-permute-start.32
  638.2 9.1 %collective-permute-start.33 = (f32[34,128]{1,0:T(8,128)S(1)}, f32[34,128]{1,0:T(8,128)S(1)}, u32[]{:S(2)}, u32[]{:S(2)}) collective-permute-start(f32[34,128]{1,0:T(8,128)S(1)} %add.152), channel_id=1, source_target_pairs={{0,2},{1,3},{2,0},{3,1},{4,6},{5,7},{6,4},{7,5},{8,10},{9,11},{10,... | collective-permute-start | bytes 52232 | tf_op jit(solution)/shard_map/ppermute | solution.py:47
  638.2 16.9 %all-to-all-start.2 = ((bf16[8,64,768]{2,1,0:T(8,128)(2,1)}), bf16[8,64,768]{2,1,0:T(8,128)(2,1)}, u32[]{:S(2)}, u32[]{:S(2)}) async-start(bf16[8,64,768]{2,1,0:T(8,128)(2,1)} %bitcast.108), calls=%async_computation.3 | async-start | bytes 1572864 | tf_op jit(solution)/shard_map/all_to_all | solution.py:198
  (21 other events, 206.4 us)
Sparse Core Ops, SparseCore 0:
  14.2 65.4 all-gather.8
  111.0 88.1 all-gather.4
  230.1 86.7 all-gather.6
  346.9 83.8 reduce-scatter.5
  435.0 84.0 reduce-scatter.7
  540.8 57.4 reduce-scatter.3

commit v3 on v2

--- a/solution.py
+++ b/solution.py
@@ -67,12 +67,13 @@
     return pl.BlockSpec(memory_space=pl.ANY)
 
 
-def gather_pieces(rows, n):
+def gather_pieces(rows, n, second=(), last=()):
     if n != 8:
         full = lax.all_gather(rows, "ctx", axis=0)
         return [jnp.take(full, slot_order(n), axis=0).reshape(-1, rows.shape[1])]
     pair = jnp.concatenate([rows, swap_first(rows, n, True)], axis=0)
-    other = swap_first(pair, n, False)
+    pair = after(pair, *second)
+    other = after(swap_first(pair, n, False), *last)
     return [pair, other, swap(pair, n, 1), swap(other, n, 1)]
 
 
@@ -124,7 +125,7 @@
             pltpu.SemaphoreType.DMA((n,)),
         ],
         compiler_params=pltpu.CompilerParams(vmem_limit_bytes=VMEM_LIMIT),
-        cost_estimate=cost_of(6.0 * total * width / 2**22),
+        cost_estimate=cost_of(0.3 * 6.0 * total * width / 2**22),
         name="assemble",
     )(*pieces)
 
@@ -180,15 +181,26 @@
     )(mine, got)
 
 
-def scatter_slots(lefts, ws, column, n):
+def scatter_far(lefts, ws, column, n):
     if n != 8:
         index = jnp.argsort(slot_order(n))
-        part = jnp.take(mm_slots(lefts, ws, column, 0, n), index, axis=0)
-        return lax.psum_scatter(part, "ctx", scatter_dimension=0, tiled=True)[0].astype(f32)
-    far = mm_slots(lefts, ws, column, 4, 4)
-    got = swap(far, n, 1)
-    near = mm_slots(lefts, ws, column, 0, 4)
-    send, keep = add_halves(near, got)
+        return jnp.take(mm_slots(lefts, ws, column, 0, n), index, axis=0)
+    return swap(mm_slots(lefts, ws, column, 4, 4), n, 1)
+
+
+def scatter_near(got, near):
+    if near is None:
+        return got, got
+    return add_halves(near, got)
+
+
+def near_product(lefts, ws, column, n):
+    return mm_slots(lefts, ws, column, 0, 4) if n == 8 else None
+
+
+def scatter_last(send, keep, n):
+    if n != 8:
+        return lax.psum_scatter(send, "ctx", scatter_dimension=0, tiled=True)[0].astype(f32)
     got = swap_first(send, n, False)
     last = (keep[1] + got[1].astype(f32)).astype(bf16)
     return keep[0] + got[0].astype(f32) + swap_first(last, n, True).astype(f32)
@@ -198,18 +210,22 @@
     return lax.all_to_all(blocks, "ctx", 0, 0, tiled=True)
 
 
-def weight_kernel(counts, *refs):
+def weight_kernel(counts, gained, *refs):
+    if gained:
+        refs, w_ref, gain_ref, dg_ref = refs[:-4] + refs[-2:-1], refs[-4], refs[-3], refs[-1]
     refs, out_ref = refs[:-1], refs[-1]
     tops, at = [], 0
     for count in counts:
         left = jnp.concatenate([r[...] for r in refs[at : at + count]], axis=0)
         tops.append(dot_tn(left, refs[at + count][...]))
         at += count + 1
+    if gained:
+        dg_ref[...] = jnp.sum(tops[0] * w_ref[...].astype(f32), axis=1, keepdims=True) / gain_ref[...]
     shards, _, rows, width = out_ref.shape
     out_ref[...] = jnp.concatenate(tops, axis=1).astype(bf16).reshape(shards, 1, rows, width)
 
 
-def weight_grad(pairs, n, n_fsdp):
+def weight_grad(pairs, n, n_fsdp, w=None, gain=None):
     depth = pairs[0][0][0].shape[1]
     rows, tile = depth // (n * n_fsdp), depth // n
     width = sum(right.shape[1] for _, right in pairs)
@@ -219,17 +235,25 @@
         specs += [pl.BlockSpec((p.shape[0], tile), lambda j: (0, j)) for p in pieces]
         specs.append(pl.BlockSpec(right.shape, lambda j: (0, 0)))
         args += [*pieces, right]
+    out_specs = [pl.BlockSpec((n_fsdp, 1, rows, width), lambda j: (0, j, 0, 0))]
+    out_shape = [jax.ShapeDtypeStruct((n_fsdp, n, rows, width), bf16)]
+    if w is not None:
+        column = pl.BlockSpec((tile, 1), lambda j: (j, 0))
+        specs += [pl.BlockSpec((tile, w.shape[1]), lambda j: (j, 0)), column]
+        args += [w, gain]
+        out_specs.append(column)
+        out_shape.append(jax.ShapeDtypeStruct((depth, 1), f32))
     out = pl.pallas_call(
-        functools.partial(weight_kernel, [len(pieces) for pieces, _ in pairs]),
+        functools.partial(weight_kernel, [len(pieces) for pieces, _ in pairs], w is not None),
         grid=(n,),
         in_specs=specs,
-        out_specs=pl.BlockSpec((n_fsdp, 1, rows, width), lambda j: (0, j, 0, 0)),
-        out_shape=jax.ShapeDtypeStruct((n_fsdp, n, rows, width), bf16),
+        out_specs=out_specs,
+        out_shape=out_shape,
         compiler_params=pltpu.CompilerParams(vmem_limit_bytes=VMEM_LIMIT),
-        cost_estimate=cost_of(16.0 * total * depth * width / (2048 * 2048 * 1152)),
+        cost_estimate=cost_of(0.3 * 16.0 * total * depth * width / (2048 * 2048 * 1152)),
         name="weight_grad",
     )(*args)
-    return out.reshape(depth, width)
+    return [out[0].reshape(depth, width)] + list(out[1:])
 
 
 def reduce_rows(grad, n):
@@ -237,25 +261,25 @@
     return summed.reshape(n, -1, grad.shape[1])
 
 
-def join_kernel(parts, got_ref, *out_refs):
-    for out_ref, slices in zip(out_refs, parts):
+def join_kernel(count, parts, *refs):
+    for out_ref, slices in zip(refs[count:], parts):
         out_ref[...] = jnp.concatenate(
-            [got_ref[0, :, lo:hi].astype(f32) for lo, hi in slices], axis=1
+            [refs[k][0, :, lo:hi].astype(f32) for k, lo, hi in slices], axis=1
         )
 
 
-def join_columns(got, parts):
-    n, rows, width = got.shape
-    sizes = [sum(hi - lo for lo, hi in slices) for slices in parts]
+def join_columns(gots, parts):
+    n, rows, _ = gots[0].shape
+    sizes = [sum(hi - lo for _, lo, hi in slices) for slices in parts]
     return pl.pallas_call(
-        functools.partial(join_kernel, parts),
+        functools.partial(join_kernel, len(gots), parts),
         grid=(n,),
-        in_specs=[pl.BlockSpec((1, rows, width), lambda i: (i, 0, 0))],
+        in_specs=[pl.BlockSpec((1, rows, got.shape[2]), lambda i: (i, 0, 0)) for got in gots],
         out_specs=[pl.BlockSpec((rows, size), lambda i: (0, i)) for size in sizes],
         out_shape=[jax.ShapeDtypeStruct((rows, n * size), f32) for size in sizes],
         cost_estimate=cost_of(5.0),
         name="join_columns",
-    )(got)
+    )(*gots)
 
 
 def sum_all(values, n, n_fsdp):
@@ -351,7 +375,7 @@
         compiler_params=pltpu.CompilerParams(
             dimension_semantics=("arbitrary",), vmem_limit_bytes=VMEM_LIMIT
         ),
-        cost_estimate=cost_of(16.0 * total * heads / 4096),
+        cost_estimate=cost_of(0.3 * 16.0 * total * heads / 4096),
         name="project",
     )(places, *pieces, gain, pack, *args)
 
@@ -440,7 +464,7 @@
             jax.ShapeDtypeStruct((heads, total), f32),
         ],
         compiler_params=pltpu.CompilerParams(vmem_limit_bytes=VMEM_LIMIT),
-        cost_estimate=cost_of(18.5 * total * heads / 4096),
+        cost_estimate=cost_of(0.3 * 18.5 * total * heads / 4096),
         name="attend",
     )(length, places, by_index, q, k, v)
 
@@ -626,7 +650,7 @@
             jax.ShapeDtypeStruct((rows, depth), bf16),
         ],
         compiler_params=pltpu.CompilerParams(vmem_limit_bytes=VMEM_LIMIT),
-        cost_estimate=cost_of(11.0),
+        cost_estimate=cost_of(0.3 * 11.0),
         name="branch",
     )(order, a_tok, wo_slots, x, gain)
 
@@ -740,7 +764,7 @@
             pltpu.SemaphoreType.DMA((n,)),
         ],
         compiler_params=pltpu.CompilerParams(vmem_limit_bytes=VMEM_LIMIT),
-        cost_estimate=cost_of(17.0 * total * ff / (2048 * 384)),
+        cost_estimate=cost_of(0.3 * 17.0 * total * ff / (2048 * 384)),
         name="feed",
     )(*x_pieces, *y_pieces, w)
 
@@ -778,19 +802,21 @@
     gain_rows = -(-gains.shape[0] // (16 * width)) * 16
     gains = jnp.pad(gains, (0, gain_rows * width - gains.shape[0])).reshape(gain_rows, width)
     pack = lax.all_gather(jnp.concatenate([w_attn, gains], axis=0), "fsdp", axis=0)
+    x_pieces = gather_pieces(x, n)
+
+    def feed_weights(part, gate):
+        at = parts * me + part
+        w = jnp.concatenate([cols(w, ff_part, at) for w in (wg, wu, wd)], axis=1)
+        return whole(after(w, gate))
+
+    w_ff = [feed_weights(0, x_pieces[0])]
+    dy_pieces = gather_pieces(after(dy, x_pieces[0]), n, [x_pieces[len(x_pieces) // 4]])
+    pack = after(pack, dy_pieces[0])
     w_in = pack[:, :shard, :in_cols].reshape(depth, in_cols)
     wo_c = pack[:, :shard, in_cols:].reshape(depth, q_cols)
     gains = pack[:, shard:].reshape(n_fsdp, -1)
     attn_gain = gains[:, :shard].reshape(1, depth).astype(f32)
     mlp_gain = gains[:, shard : 2 * shard].reshape(1, depth).astype(f32)
-    x_pieces = gather_pieces(x, n)
-
-    def feed_weights(part, gate):
-        at = parts * me + part
-        w = jnp.concatenate([cols(w, ff_part, at) for w in (wg, wu, wd)], axis=1)
-        return whole(after(w, gate))
-
-    w_ff = [feed_weights(0, x_pieces[0])]
 
     order = slot_order(n)
     by_index = block_order.reshape(-1)
@@ -808,41 +834,51 @@
         x_pieces, n, places, attn_gain, pack, qg, kg, cosine, sine, heads
     )
     w_ff += [feed_weights(part, qb) for part in range(1, parts)]
-    wo_pieces = gather_pieces(after(wo_c, x_pieces[-1]), n)
-    wo_slots = assemble(wo_pieces, n)
-    dy_pieces = gather_pieces(after(dy, wo_pieces[len(wo_pieces) // 2]), n)
-    o, a, a_index, lse = attend(lengths, places, by_index, qb, kb, vb, heads)
+    o, a, a_index, lse = attend(
+        lengths, places, by_index, after(qb, dy_pieces[len(dy_pieces) // 4]), kb, vb, heads
+    )
     a_tok = exchange(a_index.reshape(n, rows, q_cols))
-    a_tok = after(a_tok, dy_pieces[len(dy_pieces) // 2])
+    wo_slots = assemble(gather_pieces(wo_c, n, [qb], [a_index]), n)
     h1, xn2 = branch(order, a_tok, wo_slots, x, mlp_gain)
 
     xn2_pieces = gather_pieces(xn2, n)
     d_gu, hm, grads = [], [], []
+
+    def ff_grad(d_part, hm_part):
+        return weight_grad(
+            [
+                (xn2_pieces, d_part.reshape(total, 2 * ff_part)),
+                (dy_pieces, hm_part.reshape(total, ff_part)),
+            ],
+            n, n_fsdp,
+        )
+
     for w in w_ff:
-        if grads:
+        if d_gu:
+            grads += ff_grad(d_gu[-1], hm[-1])
             xn2_pieces = [after(xn2_pieces[0], grads[-1])] + xn2_pieces[1:]
         d_part, hm_part = feed(xn2_pieces, dy_pieces, n, w)
-        grads.append(
-            weight_grad(
-                [
-                    (xn2_pieces, d_part.reshape(total, 2 * ff_part)),
-                    (dy_pieces, hm_part.reshape(total, ff_part)),
-                ],
-                n, n_fsdp,
-            )
-        )
         d_gu.append(d_part)
         hm.append(hm_part)
+    got = scatter_far(d_gu, w_ff, 0, n)
+    send, keep = scatter_near(got, near_product(d_gu, w_ff, 0, n))
+    grads += ff_grad(after(d_gu[-1], send), hm[-1])
     d_ff = [reduce_rows(grad, n) for grad in grads]
-    d_xn2 = scatter_slots(d_gu, w_ff, 0, n)
+    hm = [after(hm[0], grads[-1])] + hm[1:]
+    m_got = scatter_far(hm, w_ff, 2, n)
+    m_near = near_product(hm, w_ff, 2, n)
+    d_xn2 = scatter_last(send, keep, n)
 
     d_h1, dz, d_mlp_gain, da = branch_back(
-        order, after(d_xn2, grads[-1]), h1, dy, mlp_gain, wo_slots
+        order, after(d_xn2, grads[-1], m_got if m_near is None else m_near), h1, dy, mlp_gain, wo_slots
     )
     da = exchange(da).reshape(total, q_cols)
-    m = scatter_slots([after(hm[0], d_h1)] + hm[1:], w_ff, 2, n)
+    m_send, m_keep = scatter_near(after(m_got, d_h1), m_near)
+    dz_pieces = gather_pieces(dz, n)
+    da = after(da, dz_pieces[0])
+    m = scatter_last(after(m_send, dz_pieces[len(dz_pieces) // 2]), m_keep, n)
     output = (h1 + m).astype(bf16)
-    dz_pieces = gather_pieces(dz, n)
+    d_ff[0] = exchange(after(d_ff[0], da))
     d_qkv, d_qg, d_kg, *key_sums = attend_back(
         lengths, places, by_index, qb, kb, vb, da, o, lse, q_raw, k_raw, qg, kg, cosine, sine,
         heads, kv_share == 1,
@@ -862,29 +898,37 @@
         dk = scale * (grad - hat * jnp.mean(grad * hat, axis=-1, keepdims=True))
         d_kv = jnp.concatenate([dk, dv], axis=1).astype(bf16).reshape(2 * n, -1, 2 * HEAD_SIZE)
         d_qkv = jnp.concatenate([d_qkv, d_kv[places].reshape(total, -1)], axis=1)
-    d_attn = weight_grad([([xn.reshape(total, depth)], d_qkv), (dz_pieces, a)], n, n_fsdp)
-    d_xn = scatter_slots([d_qkv.reshape(n, rows, in_cols)], [w_in], 0, n)
+    d_attn, d_attn_gain = weight_grad(
+        [([xn.reshape(total, depth)], d_qkv), (dz_pieces, a)], n, n_fsdp, w_in,
+        attn_gain.reshape(depth, 1),
+    )
     d_attn = reduce_rows(d_attn, n)
+    left = [after(d_qkv, d_ff[0]).reshape(n, rows, in_cols)]
+    got = scatter_far(left, [w_in], 0, n)
+    d_xn = scatter_last(*scatter_near(got, near_product(left, [w_in], 0, n)), n)
     x_float = x.astype(f32)
     scale_one = rms_scale(x_float)
     hat_one = x_float * scale_one
-    d_attn_gain = jnp.sum(d_xn * hat_one, axis=0)
     e = d_xn * attn_gain
     dx = d_h1 + scale_one * (e - hat_one * jnp.mean(e * hat_one, axis=-1, keepdims=True))
 
     sums = sum_all(
-        jnp.concatenate([d_attn_gain, d_mlp_gain[0], d_qg[0], d_kg[0]]).reshape(-1, HEAD_SIZE),
+        jnp.concatenate([d_attn_gain[:, 0], d_mlp_gain[0], d_qg[0], d_kg[0]]).reshape(-1, HEAD_SIZE),
         n, n_fsdp,
     ).reshape(-1)
-    d_ff = exchange(after(jnp.concatenate(d_ff, axis=2), d_qkv))
+    d_ff = d_ff[:1] + [exchange(d) for d in d_ff[1:]]
     d_attn = exchange(d_attn)
-    starts = range(0, 3 * ff, 3 * ff_part)
     d_wg, d_wu, d_wd = join_columns(
-        d_ff, [[(t + k * ff_part, t + (k + 1) * ff_part) for t in starts] for k in range(3)]
+        d_ff,
+        [[(p, k * ff_part, (k + 1) * ff_part) for p in range(parts)] for k in range(3)],
     )
     k_cols, v_cols = q_cols + HEAD_SIZE, q_cols + 2 * HEAD_SIZE
-    d_wq, d_wo = join_columns(d_attn, [[(0, q_cols)], [(v_cols, v_cols + q_cols)]])
-    d_wk, d_wv = join_columns(d_attn[::kv_share], [[(q_cols, k_cols)], [(k_cols, v_cols)]])
+    kv_parts = [[(0, q_cols, k_cols)], [(0, k_cols, v_cols)]]
+    d_wq, d_wo, *d_kv = join_columns(
+        [d_attn],
+        [[(0, 0, q_cols)], [(0, v_cols, v_cols + q_cols)]] + (kv_parts if kv_share == 1 else []),
+    )
+    d_wk, d_wv = d_kv or join_columns([d_attn[::kv_share]], kv_parts)
     return (
         output[None],
         dx[None],

time: 682 us -> 623 us (0.913)
  waiting for transfers between devices: 279 us -> 213 us
  other arithmetic: 34.6 us -> 43.6 us
  starting transfers between devices: 45.4 us -> 54 us
    ppermute x16, waiting for transfers between devices: 194 us -> 126 us  [swap_first(): lax.ppermute(values, 'ctx', [(c, c ^ (2 if (c % 2 == 0) == first else 4))...]
    ppermute x18, waiting for transfers between devices: 10.1 us -> 47.1 us  [swap(): return lax.ppermute(values, axis, [(c, c ^ bits) for c in range(n)])]
    all_gather x1, waiting for transfers between devices: 28.6 us -> 6 us  [per_device(): lax.all_gather(jnp.concatenate([w_attn, gains], axis=0), 'fsdp', axis=0)]
    all_gather x2, waiting for transfers between devices: 18 us -> 3.63 us  [whole(): return lax.all_gather(w, 'fsdp', axis=0, tiled=True)]
    concatenate x1 -> x5, other arithmetic: 1.49 us -> 9.75 us  [gather_pieces(): pair = jnp.concatenate([rows, swap_first(rows, n, True)], axis=0)]
    pallas_call x3 -> x2, Pallas kernels: 16.2 us -> 11.5 us  [join_columns(): pl.pallas_call(functools.partial(join_kernel, len(gots), parts), grid=(n,...]
    all_to_all x4 -> x5, starting transfers between devices: 16.5 us -> 20.5 us  [exchange(): return lax.all_to_all(blocks, 'ctx', 0, 0, tiled=True)]
    all_to_all x4 -> x5, waiting for transfers between devices: 27.8 us -> 30.5 us  [exchange(): return lax.all_to_all(blocks, 'ctx', 0, 0, tiled=True)]
  transfers between devices with their start and end apart: 44 -> 45, of which waited for: 21 -> 23; matrix products, arithmetic and copies ran while one was open for 9% -> 9% of each run, Pallas kernels for 35% -> 43%
where the time goes in v3:
time: 623 us; the launch traced here: 615 us
  Pallas kernels  269 us (43%)
  waiting for transfers between devices  213 us (34%)
  starting transfers between devices  54 us (9%)
  other arithmetic  43.6 us (7%)
  local copies, waits for them, and re-layouts  19.6 us (3%)
  between operations  15.7 us (3%)
    ppermute x16, waiting for transfers between devices, swap_first(): lax.ppermute(values, 'ctx', [(c, c ^ (2 if (c % 2 == 0) == first else 4))...  126 us
    pallas_call x6, Pallas kernels, mm_slots(): pl.pallas_call(functools.partial(mm_kernel, len(lefts)), grid=(count,), i...  53 us
    pallas_call x3, Pallas kernels, weight_grad(): pl.pallas_call(functools.partial(weight_kernel, [len(pieces) for pieces,...  49.8 us
    ppermute x18, waiting for transfers between devices, swap(): return lax.ppermute(values, axis, [(c, c ^ bits) for c in range(n)])  47.1 us
    pallas_call x2, Pallas kernels, feed(): pl.pallas_call(functools.partial(feed_kernel, len(x_pieces)), grid=(n //...  36.7 us
    pallas_call x1, Pallas kernels, attend_back(): pl.pallas_call(functools.partial(attend_back_kernel, heads, tile, finish_...  31.7 us
    all_to_all x5, waiting for transfers between devices, exchange(): return lax.all_to_all(blocks, 'ctx', 0, 0, tiled=True)  30.5 us
    ppermute x16, starting transfers between devices, swap_first(): lax.ppermute(values, 'ctx', [(c, c ^ (2 if (c % 2 == 0) == first else 4))...  24.1 us
  transfers between devices with their start and end apart: 45, of which 23 were waited for; matrix products, arithmetic and copies ran while one was open for 9% of the time, Pallas kernels for 43%

profile of v3, /device:TPU:0, one launch (start us, length us, event | category | flops | bytes accessed | tf_op | source)
XLA Modules:
  0.0 614.6 jit_solution(8223517716737635332)
XLA Ops:
  14.2 12.8 %collective-permute-done = bf16[256,2048]{1,0:T(8,128)(2,1)S(1)} collective-permute-done((bf16[256,2048]{1,0:T(8,128)(2,1)S(1)}, bf16[256,2048]{1,0:T(8,128)(2,1)S(1)}, u32[]{:S(2)}, u32[]{:S(2)}) %collective-permute-start) | collective-permute-done | bytes 1048608 | tf_op jit(solution)/shard_map/ppermute | solution.py:51
  37.0 29.1 %collective-permute-done.1.refs_1_ = bf16[512,2048]{1,0:T(8,128)(2,1)} collective-permute-done((bf16[512,2048]{1,0:T(8,128)(2,1)}, bf16[512,2048]{1,0:T(8,128)(2,1)}, u32[]{:S(2)}, u32[]{:S(2)}) %collective-permute-start.1) | collective-permute-done | bytes 2097184 | tf_op jit(solution)/shard_map/ppermute | solution.py:51
  66.9 4.8 sine_multiply_fusion
  73.1 6.0 all-gather.9.cloned.1.call-done
  86.8 16.8 %project.1 = (bf16[8,256,2048]{2,1,0:T(8,128)(2,1)}, f32[2048,256]{1,0:T(8,128)}, f32[2048,128]{1,0:T(8,128)}, bf16[2048,256]{1,0:T(8,128)(2,1)}, bf16[2048,128]{1,0:T(8,128)(2,1)}, /*index=5*/bf16[2048,128]{1,0:T(8,128)(2,1)}) custom-call(s32[16]{0:T(128)} %select_n.79.place_ref, bf16[512,2048]{1,0:T(8,128)(2,1)} %pad_maximum_fusion.refs_0_, ...), custom_call_target="tpu_custom_call" | custom-call | flops 5280000000 | bytes 1048576 | tf_op jit(solution)/shard_map/project/pallas_call | solution.py:356
  111.8 4.9 collective-permute-done.5.refs_5_.refs_6_
  116.7 18.6 %attend.1 = (f32[2048,256]{1,0:T(8,128)}, bf16[2048,256]{1,0:T(8,128)(2,1)}, bf16[2048,256]{1,0:T(8,128)(2,1)}, f32[2,2048]{1,0:T(2,128)}) custom-call(s32[1]{0:T(128)S(6)} %copy.41.length_ref, s32[16]{0:T(128)} %select_n.79.place_ref, s32[16]{0:T(128)} %reshape.201.index_ref, bf16[2048,256]{1,0:T(8,128)(2,1)} %get-tuple-element.72.q_ref, ...), custom_call_target="tpu_custom_call" | custom-call | flops 6104999936 | bytes 1048576 | tf_op jit(solution)/shard_map/attend/pallas_call | solution.py:456
  140.5 4.3 all-to-all-start
  146.8 6.5 %assemble.1.wo_ref = bf16[8,2048,256]{2,1,0:T(8,128)(2,1)} custom-call(bf16[4096,256]{1,0:T(8,128)(2,1)} %pad_maximum_fusion.2.refs_0_, bf16[4096,256]{1,0:T(8,128)(2,1)} %collective-permute-done.7.refs_1_, bf16[4096,256]{1,0:T(8,128)(2,1)} %collective-permute-done.8.refs_2_, bf16[4096,256]{1,0:T(8,128)(2,1)} %collective-permute-done.9.refs_3_), custom_call_target="tpu_custom_call" | custom-call | flops 1980000000 | bytes 1048576 | tf_op jit(solution)/shard_map/assemble/pallas_call | solution.py:117
  153.2 6.9 %all-to-all-done.a_ref = bf16[8,256,256]{2,1,0:T(8,128)(2,1)} async-done(((bf16[8,256,256]{2,1,0:T(8,128)(2,1)}), bf16[8,256,256]{2,1,0:T(8,128)(2,1)}, u32[]{:S(2)}, u32[]{:S(2)}) %all-to-all-start) | async-done | bytes 1048608 | tf_op jit(solution)/shard_map/all_to_all | solution.py:210
  160.2 11.0 %branch.1 = (f32[256,2048]{1,0:T(8,128)}, bf16[256,2048]{1,0:T(8,128)(2,1)}) custom-call(s32[8]{0:T(128)} %copy-done.22, bf16[8,256,256]{2,1,0:T(8,128)(2,1)} %all-to-all-done.a_ref, bf16[8,2048,256]{2,1,0:T(8,128)(2,1)} %assemble.1.wo_ref, bf16[256,2048]{1,0:T(8,128)(2,1)} %bitcast.93, f32[1,2048]{1,0:T(1,128)} %bitcast.130), custom_call_target="tpu_custom_call" | custom-call | flops 3630000128 | bytes 1048576 | tf_op jit(solution)/shard_map/branch/pallas_call | solution.py:634
  171.6 14.5 %collective-permute-done.10 = bf16[256,2048]{1,0:T(8,128)(2,1)S(1)} collective-permute-done((bf16[256,2048]{1,0:T(8,128)(2,1)}, bf16[256,2048]{1,0:T(8,128)(2,1)S(1)}, u32[]{:S(2)}, u32[]{:S(2)}) %collective-permute-start.10) | collective-permute-done | bytes 1048608 | tf_op jit(solution)/shard_map/ppermute | solution.py:51
  190.0 25.3 %collective-permute-done.11.refs_1_ = bf16[512,2048]{1,0:T(8,128)(2,1)} collective-permute-done((bf16[512,2048]{1,0:T(8,128)(2,1)}, bf16[512,2048]{1,0:T(8,128)(2,1)}, u32[]{:S(2)}, u32[]{:S(2)}) %collective-permute-start.11) | collective-permute-done | bytes 2097184 | tf_op jit(solution)/shard_map/ppermute | solution.py:51
  216.6 3.2 collective-permute-done.13.refs_3_
  219.8 18.4 %feed.2 = (bf16[8,256,768]{2,1,0:T(8,128)(2,1)}, bf16[8,256,384]{2,1,0:T(8,128)(2,1)}) custom-call(bf16[512,2048]{1,0:T(8,128)(2,1)} %pad_maximum_fusion.3.refs_0_, bf16[512,2048]{1,0:T(8,128)(2,1)} %collective-permute-done.11.refs_1_, bf16[512,2048]{1,0:T(8,128)(2,1)} %collective-permute-done.12.refs_2_, bf16[512,2048]{1,0:T(8,128)(2,1)} %collective-permute-done.13.refs_3_, ...), custom_call_target="tpu_custom_call" | custom-call | flops 5609999872 | bytes 1048576 | tf_op jit(solution)/shard_map/feed/pallas_call | solution.py:747
  238.1 17.3 %weight_grad.3 = bf16[4,8,64,1152]{3,2,1,0:T(8,128)(2,1)} custom-call(bf16[512,2048]{1,0:T(8,128)(2,1)} %pad_maximum_fusion.3.refs_0_, bf16[512,2048]{1,0:T(8,128)(2,1)} %collective-permute-done.11.refs_1_, bf16[512,2048]{1,0:T(8,128)(2,1)} %collective-permute-done.12.refs_2_, bf16[512,2048]{1,0:T(8,128)(2,1)} %collective-permute-done.13.refs_3_, ...), custom_call_target="tpu_custom_call" | custom-call | flops 5280000000 | bytes 1048576 | tf_op jit(solution)/shard_map/weight_grad/pallas_call | solution.py:246
  255.7 3.6 all-gather.7.cloned.1.call-done.refs_8_.refs_3_
  259.4 18.3 %feed.3 = (bf16[8,256,768]{2,1,0:T(8,128)(2,1)}, bf16[8,256,384]{2,1,0:T(8,128)(2,1)}) custom-call(bf16[512,2048]{1,0:T(8,128)(2,1)} %pad_maximum_fusion.3.refs_0_, bf16[512,2048]{1,0:T(8,128)(2,1)} %collective-permute-done.11.refs_1_, bf16[512,2048]{1,0:T(8,128)(2,1)} %collective-permute-done.12.refs_2_, bf16[512,2048]{1,0:T(8,128)(2,1)} %collective-permute-done.13.refs_3_, ...), custom_call_target="tpu_custom_call" | custom-call | flops 5609999872 | bytes 1048576 | tf_op jit(solution)/shard_map/feed/pallas_call | solution.py:747
  277.7 11.5 %mm_slots.7 = bf16[4,256,2048]{2,1,0:T(8,128)(2,1)} custom-call(bf16[8,256,768]{2,1,0:T(8,128)(2,1)} %get-tuple-element.82.refs_0_, bf16[8,256,768]{2,1,0:T(8,128)(2,1)} %get-tuple-element.87.refs_1_, bf16[2048,1152]{1,0:T(8,128)(2,1)} %all-gather.5.cloned.1.call-done.refs_8_.refs_2_, bf16[2048,1152]{1,0:T(8,128)(2,1)} %all-gather.7.cloned.1.call-done.refs_8_.refs_3_), custom_call_target="tpu_custom_call" | custom-call | flops 12650000384 | bytes 1048576 | tf_op jit(solution)/shard_map/mm_slots/pallas_call | solution.py:144
  289.2 11.4 %mm_slots.6.mine_ref = bf16[4,256,2048]{2,1,0:T(8,128)(2,1)} custom-call(bf16[8,256,768]{2,1,0:T(8,128)(2,1)} %get-tuple-element.82.refs_0_, bf16[8,256,768]{2,1,0:T(8,128)(2,1)} %get-tuple-element.87.refs_1_, bf16[2048,1152]{1,0:T(8,128)(2,1)} %all-gather.5.cloned.1.call-done.refs_8_.refs_2_, bf16[2048,1152]{1,0:T(8,128)(2,1)} %all-gather.7.cloned.1.call-done.refs_8_.refs_3_), custom_call_target="tpu_custom_call" | custom-call | flops 12650000384 | bytes 1048576 | tf_op jit(solution)/shard_map/mm_slots/pallas_call | solution.py:144
  302.7 6.5 %add_halves.3 = (bf16[2,256,2048]{2,1,0:T(8,128)(2,1)}, f32[2,256,2048]{2,1,0:T(8,128)}) custom-call(bf16[4,256,2048]{2,1,0:T(8,128)(2,1)} %mm_slots.6.mine_ref, bf16[4,256,2048]{2,1,0:T(8,128)(2,1)} %copy-done.25), custom_call_target="tpu_custom_call" | custom-call | flops 7150000128 | bytes 1048576 | tf_op jit(solution)/shard_map/add_halves/pallas_call | solution.py:169
  310.7 24.7 %collective-permute-done.18 = bf16[2,256,2048]{2,1,0:T(8,128)(2,1)S(1)} collective-permute-done((bf16[2,256,2048]{2,1,0:T(8,128)(2,1)}, bf16[2,256,2048]{2,1,0:T(8,128)(2,1)S(1)}, u32[]{:S(2)}, u32[]{:S(2)}) %collective-permute-start.18) | collective-permute-done | bytes 2097184 | tf_op jit(solution)/shard_map/ppermute | solution.py:51
  339.7 17.3 %weight_grad.4 = bf16[4,8,64,1152]{3,2,1,0:T(8,128)(2,1)} custom-call(bf16[512,2048]{1,0:T(8,128)(2,1)} %pad_maximum_fusion.3.refs_0_, bf16[512,2048]{1,0:T(8,128)(2,1)} %collective-permute-done.11.refs_1_, bf16[512,2048]{1,0:T(8,128)(2,1)} %collective-permute-done.12.refs_2_, bf16[512,2048]{1,0:T(8,128)(2,1)} %collective-permute-done.13.refs_3_, ...), custom_call_target="tpu_custom_call" | custom-call | flops 5280000000 | bytes 1048576 | tf_op jit(solution)/shard_map/weight_grad/pallas_call | solution.py:246
  357.1 8.6 %mm_slots.8.mine_ref = bf16[4,256,2048]{2,1,0:T(8,128)(2,1)} custom-call(bf16[8,256,384]{2,1,0:T(8,128)(2,1)} %get-tuple-element.89.refs_0_, bf16[8,256,384]{2,1,0:T(8,128)(2,1)} %get-tuple-element.88.refs_1_, bf16[2048,1152]{1,0:T(8,128)(2,1)} %all-gather.5.cloned.1.call-done.refs_8_.refs_2_, bf16[2048,1152]{1,0:T(8,128)(2,1)} %all-gather.7.cloned.1.call-done.refs_8_.refs_3_), custom_call_target="tpu_custom_call" | custom-call | flops 8249999872 | bytes 1048576 | tf_op jit(solution)/shard_map/mm_slots/pallas_call | solution.py:144
  367.5 13.1 %branch_back.1 = (f32[256,2048]{1,0:T(8,128)}, bf16[256,2048]{1,0:T(8,128)(2,1)}, f32[1,2048]{1,0:T(1,128)}, bf16[8,256,256]{2,1,0:T(8,128)(2,1)}) custom-call(s32[8]{0:T(128)} %copy-done.22, f32[256,2048]{1,0:T(8,128)} %bitcast_add_fusion.2.dxn_ref, f32[256,2048]{1,0:T(8,128)} %get-tuple-element.78.h1_ref, bf16[256,2048]{1,0:T(8,128)(2,1)} %bitcast.118, ...), custom_call_target="tpu_custom_call" | custom-call | flops 14300000256 | bytes 1048576 | tf_op jit(solution)/shard_map/branch_back/pallas_call | solution.py:682
  382.8 3.7 all-to-all-start.1
  386.5 8.5 %mm_slots.9 = bf16[4,256,2048]{2,1,0:T(8,128)(2,1)} custom-call(bf16[8,256,384]{2,1,0:T(8,128)(2,1)} %get-tuple-element.89.refs_0_, bf16[8,256,384]{2,1,0:T(8,128)(2,1)} %get-tuple-element.88.refs_1_, bf16[2048,1152]{1,0:T(8,128)(2,1)} %all-gather.5.cloned.1.call-done.refs_8_.refs_2_, bf16[2048,1152]{1,0:T(8,128)(2,1)} %all-gather.7.cloned.1.call-done.refs_8_.refs_3_), custom_call_target="tpu_custom_call" | custom-call | flops 8249999872 | bytes 1048576 | tf_op jit(solution)/shard_map/mm_slots/pallas_call | solution.py:144
  395.5 6.0 collective-permute-done.20
  404.4 7.5 %all-to-all-done.1 = bf16[8,256,256]{2,1,0:T(8,128)(2,1)S(1)} async-done(((bf16[8,256,256]{2,1,0:T(8,128)(2,1)}), bf16[8,256,256]{2,1,0:T(8,128)(2,1)S(1)}, u32[]{:S(2)}, u32[]{:S(2)}) %all-to-all-start.1) | async-done | bytes 1048608 | tf_op jit(solution)/shard_map/all_to_all | solution.py:210
  412.8 3.8 all-to-all-start.2
  416.7 31.7 %attend_back.1 = (bf16[2048,512]{1,0:T(8,128)(2,1)}, f32[1,128]{1,0:T(1,128)}, f32[1,128]{1,0:T(1,128)}) custom-call(s32[1]{0:T(128)S(6)} %copy.41.length_ref, s32[16]{0:T(128)} %select_n.79.place_ref, s32[16]{0:T(128)} %reshape.201.index_ref, bf16[2048,256]{1,0:T(8,128)(2,1)} %get-tuple-element.72.q_ref, bf16[2048,128]{1,0:T(8,128)(2,1)} %get-tuple-element.73.k_ref, ...), custom_call_target="tpu_custom_call" | custom-call | flops 36300001280 | bytes 1048576 | tf_op jit(solution)/shard_map/attend_back/pallas_call | solution.py:602
  448.4 6.7 %mm_slots.11 = bf16[4,256,2048]{2,1,0:T(8,128)(2,1)} custom-call(bf16[8,256,512]{2,1,0:T(8,128)(2,1)} %bitcast.110, bf16[2048,512]{1,0:T(8,128)(2,1)} %bitcast.97), custom_call_target="tpu_custom_call" | custom-call | flops 6783333376 | bytes 1048576 | tf_op jit(solution)/shard_map/mm_slots/pallas_call | solution.py:144
  457.3 8.6 %collective-permute-done.21.refs_4_ = bf16[512,2048]{1,0:T(8,128)(2,1)} collective-permute-done((bf16[512,2048]{1,0:T(8,128)(2,1)S(1)}, bf16[512,2048]{1,0:T(8,128)(2,1)}, u32[]{:S(2)}, u32[]{:S(2)}) %collective-permute-start.21) | collective-permute-done | bytes 2097184 | tf_op jit(solution)/shard_map/ppermute | solution.py:47
  468.6 15.1 %weight_grad.5 = (bf16[4,8,64,768]{3,2,1,0:T(8,128)(2,1)}, f32[2048,1]{1,0:T(8,128)}) custom-call(bf16[2048,2048]{1,0:T(8,128)(2,1)} %bitcast.96, bf16[2048,512]{1,0:T(8,128)(2,1)} %get-tuple-element.106.refs_1_, bf16[512,2048]{1,0:T(8,128)(2,1)} %copy-done.4, bf16[512,2048]{1,0:T(8,128)(2,1)} %collective-permute-done.27.refs_3_, ...), custom_call_target="tpu_custom_call" | custom-call | flops 3520000000 | bytes 1048576 | tf_op jit(solution)/shard_map/weight_grad/pallas_call | solution.py:246
  483.7 6.8 %add_halves.4 = (bf16[2,256,2048]{2,1,0:T(8,128)(2,1)}, f32[2,256,2048]{2,1,0:T(8,128)}) custom-call(bf16[4,256,2048]{2,1,0:T(8,128)(2,1)} %mm_slots.8.mine_ref, bf16[4,256,2048]{2,1,0:T(8,128)(2,1)} %collective-permute-done.17.got_ref), custom_call_target="tpu_custom_call" | custom-call | flops 7150000128 | bytes 1048576 | tf_op jit(solution)/shard_map/add_halves/pallas_call | solution.py:169
  492.5 6.3 %mm_slots.10.mine_ref = bf16[4,256,2048]{2,1,0:T(8,128)(2,1)} custom-call(bf16[8,256,512]{2,1,0:T(8,128)(2,1)} %bitcast.111, bf16[2048,512]{1,0:T(8,128)(2,1)} %bitcast.99), custom_call_target="tpu_custom_call" | custom-call | flops 6783333376 | bytes 1048576 | tf_op jit(solution)/shard_map/mm_slots/pallas_call | solution.py:144
  498.8 6.6 %add_halves.5 = (bf16[2,256,2048]{2,1,0:T(8,128)(2,1)}, f32[2,256,2048]{2,1,0:T(8,128)}) custom-call(bf16[4,256,2048]{2,1,0:T(8,128)(2,1)} %mm_slots.10.mine_ref, bf16[4,256,2048]{2,1,0:T(8,128)(2,1)} %collective-permute-done.24.got_ref), custom_call_target="tpu_custom_call" | custom-call | flops 7150000128 | bytes 1048576 | tf_op jit(solution)/shard_map/add_halves/pallas_call | solution.py:169
  514.8 24.7 %collective-permute-done.31 = f32[34,128]{1,0:T(8,128)S(1)} collective-permute-done((f32[34,128]{1,0:T(8,128)S(1)}, f32[34,128]{1,0:T(8,128)S(1)}, u32[]{:S(2)}, u32[]{:S(2)}) %collective-permute-start.31) | collective-permute-done | bytes 17440 | tf_op jit(solution)/shard_map/ppermute | solution.py:47
  544.7 4.6 collective-permute-done.33
  550.5 4.5 all-to-all-start.4
  560.0 3.7 fusion.14
  563.7 8.2 %all-to-all-done.4.refs_1_ = bf16[8,64,1152]{2,1,0:T(8,128)(2,1)} async-done(((bf16[8,64,1152]{2,1,0:T(8,128)(2,1)}), bf16[8,64,1152]{2,1,0:T(8,128)(2,1)}, u32[]{:S(2)}, u32[]{:S(2)}) %all-to-all-start.4) | async-done | bytes 1179680 | tf_op jit(solution)/shard_map/all_to_all | solution.py:210
  571.9 6.3 %join_columns.3 = (f32[64,6144]{1,0:T(8,128)}, f32[64,6144]{1,0:T(8,128)}, f32[64,6144]{1,0:T(8,128)}) custom-call(bf16[8,64,1152]{2,1,0:T(8,128)(2,1)} %copy-done.10, bf16[8,64,1152]{2,1,0:T(8,128)(2,1)} %all-to-all-done.4.refs_1_), custom_call_target="tpu_custom_call" | custom-call | flops 5500000256 | bytes 1048576 | tf_op jit(solution)/shard_map/join_columns/pallas_call | solution.py:274
  578.3 4.1 collective-permute-done.26
  585.1 4.2 all-to-all-start.3
  589.3 4.8 fusion.6
  594.1 7.9 %all-to-all-done.3.refs_0_ = bf16[8,64,768]{2,1,0:T(8,128)(2,1)} async-done(((bf16[8,64,768]{2,1,0:T(8,128)(2,1)}), bf16[8,64,768]{2,1,0:T(8,128)(2,1)}, u32[]{:S(2)}, u32[]{:S(2)}) %all-to-all-start.3) | async-done | bytes 786464 | tf_op jit(solution)/shard_map/all_to_all | solution.py:210
  602.1 5.2 join_columns.2
  (175 shorter events, 93.8 us)
Async XLA Ops:
  7.2 71.9 %all-gather.9.cloned.1.call-start = ((), (), s32[]{:S(2)}) async-start(), calls=%async_computation.13 | async-start | bytes 4055040 | tf_op jit(solution)/shard_map/all_gather | solution.py:804
  11.1 205.5 %all-gather.5.cloned.1.call-start = ((), (), s32[]{:S(2)}) async-start(), calls=%async_computation.8 | async-start | bytes 5898240 | tf_op jit(solution)/shard_map/all_gather | solution.py:792
  11.2 15.8 %collective-permute-start = (bf16[256,2048]{1,0:T(8,128)(2,1)S(1)}, bf16[256,2048]{1,0:T(8,128)(2,1)S(1)}, u32[]{:S(2)}, u32[]{:S(2)}) collective-permute-start(bf16[256,2048]{1,0:T(8,128)(2,1)S(1)} %bitcast.94), channel_id=1, source_target_pairs={{0,8},{4,20},{8,0},{12,28},{16,24},{20,4},{24,16},{28,12},{1,9},{5... | collective-permute-start | bytes 3145736 | tf_op jit(solution)/shard_map/ppermute | solution.py:51
  28.5 37.6 %collective-permute-start.1 = (bf16[512,2048]{1,0:T(8,128)(2,1)}, bf16[512,2048]{1,0:T(8,128)(2,1)}, u32[]{:S(2)}, u32[]{:S(2)}) collective-permute-start(bf16[512,2048]{1,0:T(8,128)(2,1)} %pad_maximum_fusion.refs_0_), channel_id=1, source_target_pairs={{0,16},{4,12},{8,24},{12,4},{16,0},{20,28},{24,8},{28,20},{1,17},{... | collective-permute-start | bytes 6291464 | tf_op jit(solution)/shard_map/ppermute | solution.py:51
  31.8 34.3 %copy-start.19 = (s32[8,2]{0,1:T(2,128)S(1)}, s32[8,2]{0,1:T(2,128)}, u32[]{:S(2)}) copy-start(s32[8,2]{0,1:T(2,128)} %param.19) | copy-start | bytes 196
  35.5 51.3 %collective-permute-start.2 = (bf16[512,2048]{1,0:T(8,128)(2,1)}, bf16[512,2048]{1,0:T(8,128)(2,1)}, u32[]{:S(2)}, u32[]{:S(2)}) collective-permute-start(bf16[512,2048]{1,0:T(8,128)(2,1)} %pad_maximum_fusion.refs_0_), channel_id=1, source_target_pairs={{0,4},{4,0},{8,12},{12,8},{16,20},{20,16},{24,28},{28,24},{1,5},{5... | collective-permute-start | bytes 6291464 | tf_op jit(solution)/shard_map/ppermute | solution.py:47
  35.5 36.1 %collective-permute-start.4 = (bf16[256,2048]{1,0:T(8,128)(2,1)S(1)}, bf16[256,2048]{1,0:T(8,128)(2,1)}, u32[]{:S(2)}, u32[]{:S(2)}) collective-permute-start(bf16[256,2048]{1,0:T(8,128)(2,1)S(1)} %bitcast.119), channel_id=1, source_target_pairs={{0,8},{4,20},{8,0},{12,28},{16,24},{20,4},{24,16},{28,12},{1,9},{5... | collective-permute-start | bytes 3145736 | tf_op jit(solution)/shard_map/ppermute | solution.py:51
  66.1 20.7 %collective-permute-start.3 = (bf16[512,2048]{1,0:T(8,128)(2,1)}, bf16[512,2048]{1,0:T(8,128)(2,1)}, u32[]{:S(2)}, u32[]{:S(2)}) collective-permute-start(bf16[512,2048]{1,0:T(8,128)(2,1)} %collective-permute-done.1.refs_1_), channel_id=1, source_target_pairs={{0,4},{4,0},{8,12},{12,8},{16,20},{20,16},{24,28},{28,24},{1,5},{5... | collective-permute-start | bytes 6291464 | tf_op jit(solution)/shard_map/ppermute | solution.py:47
  73.1 116.4 %copy-start = (bf16[512,2048]{1,0:T(8,128)(2,1)}, bf16[512,2048]{1,0:T(8,128)(2,1)S(1)}, u32[]{:S(2)}) copy-start(bf16[512,2048]{1,0:T(8,128)(2,1)S(1)} %pad_maximum_fusion.1.refs_4_.refs_5_) | copy-start | bytes 6291460
  80.4 25.0 %collective-permute-start.6 = (bf16[2048,256]{1,0:T(8,128)(2,1)S(1)}, bf16[2048,256]{1,0:T(8,128)(2,1)}, u32[]{:S(2)}, u32[]{:S(2)}) collective-permute-start(bf16[2048,256]{1,0:T(8,128)(2,1)S(1)} %bitcast.101), channel_id=1, source_target_pairs={{0,8},{4,20},{8,0},{12,28},{16,24},{20,4},{24,16},{28,12},{1,9},{5... | collective-permute-start | bytes 3145736 | tf_op jit(solution)/shard_map/ppermute | solution.py:51
  83.2 33.5 %collective-permute-start.5 = (bf16[512,2048]{1,0:T(8,128)(2,1)S(1)}, bf16[512,2048]{1,0:T(8,128)(2,1)}, u32[]{:S(2)}, u32[]{:S(2)}) collective-permute-start(bf16[512,2048]{1,0:T(8,128)(2,1)S(1)} %pad_maximum_fusion.1.refs_4_.refs_5_), channel_id=1, source_target_pairs={{0,16},{4,12},{8,24},{12,4},{16,0},{20,28},{24,8},{28,20},{1,17},{... | collective-permute-start | bytes 6291464 | tf_op jit(solution)/shard_map/ppermute | solution.py:51
  108.1 31.1 %collective-permute-start.7 = (bf16[4096,256]{1,0:T(8,128)(2,1)}, bf16[4096,256]{1,0:T(8,128)(2,1)}, u32[]{:S(2)}, u32[]{:S(2)}) collective-permute-start(bf16[4096,256]{1,0:T(8,128)(2,1)} %pad_maximum_fusion.2.refs_0_), channel_id=1, source_target_pairs={{0,16},{4,12},{8,24},{12,4},{16,0},{20,28},{24,8},{28,20},{1,17},{... | collective-permute-start | bytes 6291464 | tf_op jit(solution)/shard_map/ppermute | solution.py:51
  135.3 11.4 %collective-permute-start.8 = (bf16[4096,256]{1,0:T(8,128)(2,1)}, bf16[4096,256]{1,0:T(8,128)(2,1)}, u32[]{:S(2)}, u32[]{:S(2)}) collective-permute-start(bf16[4096,256]{1,0:T(8,128)(2,1)} %pad_maximum_fusion.2.refs_0_), channel_id=1, source_target_pairs={{0,4},{4,0},{8,12},{12,8},{16,20},{20,16},{24,28},{28,24},{1,5},{5... | collective-permute-start | bytes 6291464 | tf_op jit(solution)/shard_map/ppermute | solution.py:47
  139.2 7.6 %collective-permute-start.9 = (bf16[4096,256]{1,0:T(8,128)(2,1)}, bf16[4096,256]{1,0:T(8,128)(2,1)}, u32[]{:S(2)}, u32[]{:S(2)}) collective-permute-start(bf16[4096,256]{1,0:T(8,128)(2,1)} %collective-permute-done.7.refs_1_), channel_id=1, source_target_pairs={{0,4},{4,0},{8,12},{12,8},{16,20},{20,16},{24,28},{28,24},{1,5},{5... | collective-permute-start | bytes 6291464 | tf_op jit(solution)/shard_map/ppermute | solution.py:47
  140.5 19.7 %all-to-all-start = ((bf16[8,256,256]{2,1,0:T(8,128)(2,1)}), bf16[8,256,256]{2,1,0:T(8,128)(2,1)}, u32[]{:S(2)}, u32[]{:S(2)}) async-start(bf16[8,256,256]{2,1,0:T(8,128)(2,1)} %bitcast.117), calls=%async_computation | async-start | bytes 2097152 | tf_op jit(solution)/shard_map/all_to_all | solution.py:210
  144.7 114.6 %all-gather.7.cloned.1.call-start = ((), (), s32[]{:S(2)}) async-start(), calls=%async_computation.9 | async-start | bytes 5898240 | tf_op jit(solution)/shard_map/all_gather | solution.py:792
  145.9 265.9 %reduce-scatter.4.cloned.1.call-start = ((), (), s32[]{:S(2)}) async-start(), calls=%async_computation.10 | async-start | bytes 5898240 | tf_op jit(solution)/shard_map/reduce_scatter | solution.py:260
  171.1 15.0 %collective-permute-start.10 = (bf16[256,2048]{1,0:T(8,128)(2,1)}, bf16[256,2048]{1,0:T(8,128)(2,1)S(1)}, u32[]{:S(2)}, u32[]{:S(2)}) collective-permute-start(bf16[256,2048]{1,0:T(8,128)(2,1)} %get-tuple-element.79), channel_id=1, source_target_pairs={{0,8},{4,20},{8,0},{12,28},{16,24},{20,4},{24,16},{28,12},{1,9},{5... | collective-permute-start | bytes 3145736 | tf_op jit(solution)/shard_map/ppermute | solution.py:51
  188.9 26.4 %collective-permute-start.11 = (bf16[512,2048]{1,0:T(8,128)(2,1)}, bf16[512,2048]{1,0:T(8,128)(2,1)}, u32[]{:S(2)}, u32[]{:S(2)}) collective-permute-start(bf16[512,2048]{1,0:T(8,128)(2,1)} %pad_maximum_fusion.3.refs_0_), channel_id=1, source_target_pairs={{0,16},{4,12},{8,24},{12,4},{16,0},{20,28},{24,8},{28,20},{1,17},{... | collective-permute-start | bytes 6291464 | tf_op jit(solution)/shard_map/ppermute | solution.py:51
  189.5 25.8 %collective-permute-start.14 = (bf16[512,2048]{1,0:T(8,128)(2,1)S(1)}, bf16[512,2048]{1,0:T(8,128)(2,1)S(1)}, u32[]{:S(2)}, u32[]{:S(2)}) collective-permute-start(bf16[512,2048]{1,0:T(8,128)(2,1)S(1)} %pad_maximum_fusion.1.refs_4_.refs_5_), channel_id=1, source_target_pairs={{0,4},{4,0},{8,12},{12,8},{16,20},{20,16},{24,28},{28,24},{1,5},{5... | collective-permute-start | bytes 6291464 | tf_op jit(solution)/shard_map/ppermute | solution.py:47
  189.5 27.1 %collective-permute-start.15 = (bf16[512,2048]{1,0:T(8,128)(2,1)}, bf16[512,2048]{1,0:T(8,128)(2,1)}, u32[]{:S(2)}, u32[]{:S(2)}) collective-permute-start(bf16[512,2048]{1,0:T(8,128)(2,1)} %collective-permute-done.5.refs_5_.refs_6_), channel_id=1, source_target_pairs={{0,4},{4,0},{8,12},{12,8},{16,20},{20,16},{24,28},{28,24},{1,5},{5... | collective-permute-start | bytes 6291464 | tf_op jit(solution)/shard_map/ppermute | solution.py:47
  190.0 26.6 %collective-permute-start.12 = (bf16[512,2048]{1,0:T(8,128)(2,1)}, bf16[512,2048]{1,0:T(8,128)(2,1)}, u32[]{:S(2)}, u32[]{:S(2)}) collective-permute-start(bf16[512,2048]{1,0:T(8,128)(2,1)} %pad_maximum_fusion.3.refs_0_), channel_id=1, source_target_pairs={{0,4},{4,0},{8,12},{12,8},{16,20},{20,16},{24,28},{28,24},{1,5},{5... | collective-permute-start | bytes 6291464 | tf_op jit(solution)/shard_map/ppermute | solution.py:47
  215.3 4.5 collective-permute-start.13
  255.5 295.0 %reduce-scatter.8.cloned.1.call-start = ((), (), s32[]{:S(2)}) async-start(), calls=%async_computation.12 | async-start | bytes 5898240 | tf_op jit(solution)/shard_map/reduce_scatter | solution.py:260
  289.2 11.4 %collective-permute-start.16 = (bf16[4,256,2048]{2,1,0:T(8,128)(2,1)}, bf16[4,256,2048]{2,1,0:T(8,128)(2,1)S(1)}, u32[]{:S(2)}, u32[]{:S(2)}) collective-permute-start(bf16[4,256,2048]{2,1,0:T(8,128)(2,1)} %mm_slots.7), channel_id=1, source_target_pairs={{0,4},{4,0},{8,12},{12,8},{16,20},{20,16},{24,28},{28,24},{1,5},{5... | collective-permute-start | bytes 12582920 | tf_op jit(solution)/shard_map/ppermute | solution.py:47
  309.2 26.2 %collective-permute-start.18 = (bf16[2,256,2048]{2,1,0:T(8,128)(2,1)}, bf16[2,256,2048]{2,1,0:T(8,128)(2,1)S(1)}, u32[]{:S(2)}, u32[]{:S(2)}) collective-permute-start(bf16[2,256,2048]{2,1,0:T(8,128)(2,1)} %get-tuple-element.86), channel_id=1, source_target_pairs={{0,16},{4,12},{8,24},{12,4},{16,0},{20,28},{24,8},{28,20},{1,17},{... | collective-permute-start | bytes 6291464 | tf_op jit(solution)/shard_map/ppermute | solution.py:51
  338.2 27.4 %collective-permute-start.19 = (bf16[256,2048]{1,0:T(8,128)(2,1)}, bf16[256,2048]{1,0:T(8,128)(2,1)S(1)}, u32[]{:S(2)}, u32[]{:S(2)}) collective-permute-start(bf16[256,2048]{1,0:T(8,128)(2,1)} %fusion.11), channel_id=1, source_target_pairs={{0,8},{4,20},{8,0},{12,28},{16,24},{20,4},{24,16},{28,12},{1,9},{5... | collective-permute-start | bytes 3145736 | tf_op jit(solution)/shard_map/ppermute | solution.py:51
  380.7 20.8 %collective-permute-start.20 = (bf16[256,2048]{1,0:T(8,128)(2,1)}, bf16[256,2048]{1,0:T(8,128)(2,1)}, u32[]{:S(2)}, u32[]{:S(2)}) collective-permute-start(bf16[256,2048]{1,0:T(8,128)(2,1)} %get-tuple-element.96), channel_id=1, source_target_pairs={{0,8},{4,20},{8,0},{12,28},{16,24},{20,4},{24,16},{28,12},{1,9},{5... | collective-permute-start | bytes 3145736 | tf_op jit(solution)/shard_map/ppermute | solution.py:51
  382.8 29.1 %all-to-all-start.1 = ((bf16[8,256,256]{2,1,0:T(8,128)(2,1)}), bf16[8,256,256]{2,1,0:T(8,128)(2,1)S(1)}, u32[]{:S(2)}, u32[]{:S(2)}) async-start(bf16[8,256,256]{2,1,0:T(8,128)(2,1)} %get-tuple-element.98), calls=%async_computation.1 | async-start | bytes 2097152 | tf_op jit(solution)/shard_map/all_to_all | solution.py:210
  395.0 88.7 %collective-permute-start.17 = (bf16[4,256,2048]{2,1,0:T(8,128)(2,1)}, bf16[4,256,2048]{2,1,0:T(8,128)(2,1)}, u32[]{:S(2)}, u32[]{:S(2)}) collective-permute-start(bf16[4,256,2048]{2,1,0:T(8,128)(2,1)} %mm_slots.9), channel_id=1, source_target_pairs={{0,4},{4,0},{8,12},{12,8},{16,20},{20,16},{24,28},{28,24},{1,5},{5... | collective-permute-start | bytes 12582920 | tf_op jit(solution)/shard_map/ppermute | solution.py:47
  402.8 52.6 %copy-start.4 = (bf16[512,2048]{1,0:T(8,128)(2,1)}, bf16[512,2048]{1,0:T(8,128)(2,1)S(1)}, u32[]{:S(2)}) copy-start(bf16[512,2048]{1,0:T(8,128)(2,1)S(1)} %pad_maximum_fusion.4.refs_2_) | copy-start | bytes 6291460
  402.8 52.8 %collective-permute-start.27 = (bf16[512,2048]{1,0:T(8,128)(2,1)S(1)}, bf16[512,2048]{1,0:T(8,128)(2,1)}, u32[]{:S(2)}, u32[]{:S(2)}) collective-permute-start(bf16[512,2048]{1,0:T(8,128)(2,1)S(1)} %pad_maximum_fusion.4.refs_2_), channel_id=1, source_target_pairs={{0,16},{4,12},{8,24},{12,4},{16,0},{20,28},{24,8},{28,20},{1,17},{... | collective-permute-start | bytes 6291464 | tf_op jit(solution)/shard_map/ppermute | solution.py:51
  412.8 35.5 %all-to-all-start.2 = ((bf16[8,64,1152]{2,1,0:T(8,128)(2,1)}), bf16[8,64,1152]{2,1,0:T(8,128)(2,1)S(1)}, u32[]{:S(2)}, u32[]{:S(2)}) async-start(bf16[8,64,1152]{2,1,0:T(8,128)(2,1)} %bitcast.115), calls=%async_computation.3 | async-start | bytes 2359296 | tf_op jit(solution)/shard_map/all_to_all | solution.py:210
  416.6 168.4 %reduce-scatter.6.cloned.1.call-start = ((), (), s32[]{:S(2)}) async-start(), calls=%async_computation.11 | async-start | bytes 3932160 | tf_op jit(solution)/shard_map/reduce_scatter | solution.py:260
  455.1 43.8 %collective-permute-start.24 = (bf16[4,256,2048]{2,1,0:T(8,128)(2,1)}, bf16[4,256,2048]{2,1,0:T(8,128)(2,1)}, u32[]{:S(2)}, u32[]{:S(2)}) collective-permute-start(bf16[4,256,2048]{2,1,0:T(8,128)(2,1)} %mm_slots.11), channel_id=1, source_target_pairs={{0,4},{4,0},{8,12},{12,8},{16,20},{20,16},{24,28},{28,24},{1,5},{5... | collective-permute-start | bytes 12582920 | tf_op jit(solution)/shard_map/ppermute | solution.py:47
  455.4 10.5 %collective-permute-start.21 = (bf16[512,2048]{1,0:T(8,128)(2,1)S(1)}, bf16[512,2048]{1,0:T(8,128)(2,1)}, u32[]{:S(2)}, u32[]{:S(2)}) collective-permute-start(bf16[512,2048]{1,0:T(8,128)(2,1)S(1)} %pad_maximum_fusion.4.refs_2_), channel_id=1, source_target_pairs={{0,4},{4,0},{8,12},{12,8},{16,20},{20,16},{24,28},{28,24},{1,5},{5... | collective-permute-start | bytes 6291464 | tf_op jit(solution)/shard_map/ppermute | solution.py:47
  455.6 13.0 %collective-permute-start.28 = (bf16[512,2048]{1,0:T(8,128)(2,1)}, bf16[512,2048]{1,0:T(8,128)(2,1)}, u32[]{:S(2)}, u32[]{:S(2)}) collective-permute-start(bf16[512,2048]{1,0:T(8,128)(2,1)} %collective-permute-done.27.refs_3_), channel_id=1, source_target_pairs={{0,4},{4,0},{8,12},{12,8},{16,20},{20,16},{24,28},{28,24},{1,5},{5... | collective-permute-start | bytes 6291464 | tf_op jit(solution)/shard_map/ppermute | solution.py:47
  490.6 48.9 %collective-permute-start.22 = (bf16[2,256,2048]{2,1,0:T(8,128)(2,1)}, bf16[2,256,2048]{2,1,0:T(8,128)(2,1)}, u32[]{:S(2)}, u32[]{:S(2)}) collective-permute-start(bf16[2,256,2048]{2,1,0:T(8,128)(2,1)} %get-tuple-element.97), channel_id=1, source_target_pairs={{0,16},{4,12},{8,24},{12,4},{16,0},{20,28},{24,8},{28,20},{1,17},{... | collective-permute-start | bytes 6291464 | tf_op jit(solution)/shard_map/ppermute | solution.py:51
  505.4 49.6 %collective-permute-start.25 = (bf16[2,256,2048]{2,1,0:T(8,128)(2,1)}, bf16[2,256,2048]{2,1,0:T(8,128)(2,1)S(1)}, u32[]{:S(2)}, u32[]{:S(2)}) collective-permute-start(bf16[2,256,2048]{2,1,0:T(8,128)(2,1)} %get-tuple-element.108), channel_id=1, source_target_pairs={{0,16},{4,12},{8,24},{12,4},{16,0},{20,28},{24,8},{28,20},{1,17},{... | collective-permute-start | bytes 6291464 | tf_op jit(solution)/shard_map/ppermute | solution.py:51
  507.1 1.3 collective-permute-start.29
  508.4 4.1 collective-permute-start.30
  512.5 27.0 %collective-permute-start.31 = (f32[34,128]{1,0:T(8,128)S(1)}, f32[34,128]{1,0:T(8,128)S(1)}, u32[]{:S(2)}, u32[]{:S(2)}) collective-permute-start(f32[34,128]{1,0:T(8,128)S(1)} %fusion.25), channel_id=1, source_target_pairs={{0,16},{4,20},{8,24},{12,28},{16,0},{20,4},{24,8},{28,12},{1,17},{... | collective-permute-start | bytes 52232 | tf_op jit(solution)/shard_map/ppermute | solution.py:47
  539.5 5.1 collective-permute-start.32
  542.6 17.4 %collective-permute-start.23 = (bf16[256,2048]{1,0:T(8,128)(2,1)}, bf16[256,2048]{1,0:T(8,128)(2,1)}, u32[]{:S(2)}, u32[]{:S(2)}) collective-permute-start(bf16[256,2048]{1,0:T(8,128)(2,1)} %fusion.12), channel_id=1, source_target_pairs={{0,8},{4,20},{8,0},{12,28},{16,24},{20,4},{24,16},{28,12},{1,9},{5... | collective-permute-start | bytes 3145736 | tf_op jit(solution)/shard_map/ppermute | solution.py:51
  544.6 4.7 collective-permute-start.33
  550.5 21.5 %all-to-all-start.4 = ((bf16[8,64,1152]{2,1,0:T(8,128)(2,1)}), bf16[8,64,1152]{2,1,0:T(8,128)(2,1)}, u32[]{:S(2)}, u32[]{:S(2)}) async-start(bf16[8,64,1152]{2,1,0:T(8,128)(2,1)} %bitcast.114), calls=%async_computation.7 | async-start | bytes 2359296 | tf_op jit(solution)/shard_map/all_to_all | solution.py:210
  558.0 24.4 %collective-permute-start.26 = (bf16[256,2048]{1,0:T(8,128)(2,1)}, bf16[256,2048]{1,0:T(8,128)(2,1)}, u32[]{:S(2)}, u32[]{:S(2)}) collective-permute-start(bf16[256,2048]{1,0:T(8,128)(2,1)} %fusion.13), channel_id=1, source_target_pairs={{0,8},{4,20},{8,0},{12,28},{16,24},{20,4},{24,16},{28,12},{1,9},{5... | collective-permute-start | bytes 3145736 | tf_op jit(solution)/shard_map/ppermute | solution.py:51
  585.1 17.0 %all-to-all-start.3 = ((bf16[8,64,768]{2,1,0:T(8,128)(2,1)}), bf16[8,64,768]{2,1,0:T(8,128)(2,1)}, u32[]{:S(2)}, u32[]{:S(2)}) async-start(bf16[8,64,768]{2,1,0:T(8,128)(2,1)} %bitcast.121), calls=%async_computation.5 | async-start | bytes 1572864 | tf_op jit(solution)/shard_map/all_to_all | solution.py:210
  (23 other events, 190.5 us)
Sparse Core Ops, SparseCore 0:
  11.3 67.8 all-gather.8
  81.3 88.0 all-gather.4
  171.5 87.8 all-gather.6
  261.5 83.6 reduce-scatter.3
  357.2 83.0 reduce-scatter.7
  483.8 58.8 reduce-scatter.5

commit v4 on v3

--- a/solution.py
+++ b/solution.py
@@ -67,14 +67,20 @@
     return pl.BlockSpec(memory_space=pl.ANY)
 
 
-def gather_pieces(rows, n, second=(), last=()):
+def gather_pair(rows, n, gates=()):
     if n != 8:
-        full = lax.all_gather(rows, "ctx", axis=0)
-        return [jnp.take(full, slot_order(n), axis=0).reshape(-1, rows.shape[1])]
-    pair = jnp.concatenate([rows, swap_first(rows, n, True)], axis=0)
+        return rows
+    return jnp.concatenate([after(rows, *gates), swap_first(rows, n, True)], axis=0)
+
+
+def gather_rest(pair, n, second=(), last=(), other=None):
+    if n != 8:
+        full = lax.all_gather(pair, "ctx", axis=0)
+        return [jnp.take(full, slot_order(n), axis=0).reshape(-1, pair.shape[1])]
     pair = after(pair, *second)
-    other = after(swap_first(pair, n, False), *last)
-    return [pair, other, swap(pair, n, 1), swap(other, n, 1)]
+    if other is None:
+        other = swap_first(pair, n, False)
+    return [pair, after(other, *last), swap(pair, n, 1), swap(after(other, *last), n, 1)]
 
 
 def piece_copies(pieces, out, sem, rows):
@@ -130,80 +136,93 @@
     )(*pieces)
 
 
-def mm_kernel(count, *refs):
-    total = dot_nt(refs[0][0], refs[count][...])
-    for k in range(1, count):
-        total = total + dot_nt(refs[k][0], refs[count + k][...])
-    refs[2 * count][0] = total.astype(bf16)
-
-
-def mm_slots(lefts, ws, column, start, count):
+def mm_kernel(count, added, *refs):
+    out_refs = refs[2 * count + added :]
+    slots, rows = refs[0].shape[:2]
+    tile = out_refs[0].shape[2]
+    total = None
+    for k in range(count):
+        left = refs[k][...].reshape(slots * rows, refs[k].shape[2])
+        term = dot_nt(left, refs[count + k][...])
+        total = term if total is None else total + term
+    total = total.reshape(slots, rows, tile)
+    if added:
+        total = total + refs[2 * count][...].astype(f32)
+    at = 0
+    for out_ref in out_refs:
+        out_ref[...] = total[at : at + out_ref.shape[0]].astype(out_ref.dtype)
+        at += out_ref.shape[0]
+
+
+def mm_slots(lefts, ws, column, start, count, add=None, dtypes=(bf16,), cover=1.0):
     rows = lefts[0].shape[1]
     width = ws[0].shape[0]
+    tile = min(width, 512)
     depths = [left.shape[2] for left in lefts]
+    each = count // len(dtypes)
     return pl.pallas_call(
-        functools.partial(mm_kernel, len(lefts)),
-        grid=(count,),
-        in_specs=[pl.BlockSpec((1, rows, d), lambda i: (i + start, 0, 0)) for d in depths]
-        + [pl.BlockSpec((width, d), lambda i: (0, column)) for d in depths],
-        out_specs=pl.BlockSpec((1, rows, width), lambda i: (i, 0, 0)),
-        out_shape=jax.ShapeDtypeStruct((count, rows, width), bf16),
+        functools.partial(mm_kernel, len(lefts), int(add is not None)),
+        grid=(width // tile,),
+        in_specs=[
+            pl.BlockSpec((count, rows, d), lambda j: (start // count, 0, 0)) for d in depths
+        ]
+        + [pl.BlockSpec((tile, d), lambda j: (j, column)) for d in depths]
+        + ([] if add is None else [pl.BlockSpec((count, rows, tile), lambda j: (0, 0, j))]),
+        out_specs=[pl.BlockSpec((each, rows, tile), lambda j: (0, 0, j)) for _ in dtypes],
+        out_shape=[jax.ShapeDtypeStruct((each, rows, width), d) for d in dtypes],
         compiler_params=pltpu.CompilerParams(vmem_limit_bytes=VMEM_LIMIT),
-        cost_estimate=cost_of(3.5 + 8.0 * count * rows * sum(depths) * width / (1024 * 1536 * 2048)),
+        cost_estimate=cost_of(cover * (2.0 + 8.0 * count * rows * sum(depths) * width / (1024 * 1536 * 2048))),
         name="mm_slots",
-    )(*lefts, *ws)
-
-
-def add_kernel(mine_ref, got_ref, send_ref, keep_ref):
-    half = send_ref.shape[0]
-    for i in range(half):
-        keep_ref[i] = mine_ref[i].astype(f32) + got_ref[i].astype(f32)
-        send_ref[i] = (mine_ref[half + i].astype(f32) + got_ref[half + i].astype(f32)).astype(bf16)
-
-
-def add_halves(mine, got):
-    slots, rows, width = mine.shape
-    half, tile = slots // 2, min(width, 512)
-    read = pl.BlockSpec((slots, rows, tile), lambda i: (0, 0, i))
-    write = pl.BlockSpec((half, rows, tile), lambda i: (0, 0, i))
-    return pl.pallas_call(
-        add_kernel,
-        grid=(width // tile,),
-        in_specs=[read, read],
-        out_specs=[write, write],
-        out_shape=[
-            jax.ShapeDtypeStruct((half, rows, width), bf16),
-            jax.ShapeDtypeStruct((half, rows, width), f32),
-        ],
-        compiler_params=pltpu.CompilerParams(vmem_limit_bytes=VMEM_LIMIT),
-        cost_estimate=cost_of(6.5 * slots * rows * width / 2**21),
-        name="add_halves",
-    )(mine, got)
-
-
-def scatter_far(lefts, ws, column, n):
-    if n != 8:
-        index = jnp.argsort(slot_order(n))
-        return jnp.take(mm_slots(lefts, ws, column, 0, n), index, axis=0)
-    return swap(mm_slots(lefts, ws, column, 4, 4), n, 1)
-
-
-def scatter_near(got, near):
-    if near is None:
-        return got, got
-    return add_halves(near, got)
-
-
-def near_product(lefts, ws, column, n):
-    return mm_slots(lefts, ws, column, 0, 4) if n == 8 else None
-
-
-def scatter_last(send, keep, n):
-    if n != 8:
-        return lax.psum_scatter(send, "ctx", scatter_dimension=0, tiled=True)[0].astype(f32)
-    got = swap_first(send, n, False)
-    last = (keep[1] + got[1].astype(f32)).astype(bf16)
-    return keep[0] + got[0].astype(f32) + swap_first(last, n, True).astype(f32)
+    )(*lefts, *ws, *([] if add is None else [add]))
+
+
+class SumScatter:
+    def __init__(self, lefts, ws, column, n, halves=False, cover=1.0):
+        self.n, self.args, self.halves, self.cover = n, (ws, column), halves, cover
+        if n != 8:
+            (part,) = mm_slots(lefts, ws, column, 0, n)
+            self.far = self.send = jnp.take(part, jnp.argsort(slot_order(n)), axis=0)
+        elif halves:
+            self.far = [mm_slots(lefts, ws, column, at, 2)[0] for at in (6, 4)]
+            self.got = [swap(far, n, 1) for far in self.far]
+        else:
+            (self.far,) = mm_slots(lefts, ws, column, 4, 4, cover=cover)
+            self.got = swap(self.far, n, 1)
+
+    def add_send(self, lefts):
+        if self.n == 8 and self.halves:
+            (self.send,) = mm_slots(lefts, *self.args, 2, 2, self.got[0])
+        elif self.n == 8:
+            self.keep, self.send = mm_slots(
+                lefts, *self.args, 0, 4, self.got, (f32, bf16), self.cover
+            )
+        return self.send
+
+    def add_keep(self, lefts):
+        if self.n == 8:
+            (self.keep,) = mm_slots(lefts, *self.args, 0, 2, self.got[1], (f32,))
+
+    def step(self, *gates):
+        if self.n == 8:
+            self.got = swap_first(after(self.send, *gates), self.n, False)
+
+    def second(self, *gates, held=None, stepped=False):
+        if self.n == 8:
+            if held is not None:
+                self.keep = after(self.keep, held)
+            if not stepped:
+                self.step(*gates)
+            got = self.got
+            self.last = (self.keep[1] + got[1].astype(f32)).astype(bf16)
+            self.part = self.keep[0] + got[0].astype(f32)
+            return self.last
+        self.last = self.send
+        return self.last
+
+    def result(self):
+        if self.n == 8:
+            return self.part + swap_first(self.last, self.n, True).astype(f32)
+        return lax.psum_scatter(self.send, "ctx", scatter_dimension=0, tiled=True)[0].astype(f32)
 
 
 def exchange(blocks):
@@ -225,7 +244,7 @@
     out_ref[...] = jnp.concatenate(tops, axis=1).astype(bf16).reshape(shards, 1, rows, width)
 
 
-def weight_grad(pairs, n, n_fsdp, w=None, gain=None):
+def weight_grad(pairs, n, n_fsdp, w=None, gain=None, cover=1.0):
     depth = pairs[0][0][0].shape[1]
     rows, tile = depth // (n * n_fsdp), depth // n
     width = sum(right.shape[1] for _, right in pairs)
@@ -250,7 +269,7 @@
         out_specs=out_specs,
         out_shape=out_shape,
         compiler_params=pltpu.CompilerParams(vmem_limit_bytes=VMEM_LIMIT),
-        cost_estimate=cost_of(0.3 * 16.0 * total * depth * width / (2048 * 2048 * 1152)),
+        cost_estimate=cost_of(cover * 16.0 * total * depth * width / (2048 * 2048 * 1152)),
         name="weight_grad",
     )(*args)
     return [out[0].reshape(depth, width)] + list(out[1:])
@@ -277,19 +296,14 @@
         in_specs=[pl.BlockSpec((1, rows, got.shape[2]), lambda i: (i, 0, 0)) for got in gots],
         out_specs=[pl.BlockSpec((rows, size), lambda i: (0, i)) for size in sizes],
         out_shape=[jax.ShapeDtypeStruct((rows, n * size), f32) for size in sizes],
-        cost_estimate=cost_of(5.0),
+        cost_estimate=cost_of(1.0),
         name="join_columns",
     )(*gots)
 
 
-def sum_all(values, n, n_fsdp):
-    bits = 1
-    while bits < n:
-        values = values + swap(values, n, bits)
-        bits *= 2
-    bits = 1
-    while bits < n_fsdp:
-        values = values + swap(values, n_fsdp, bits, "fsdp")
+def sum_across(values, size, bits, axis):
+    while bits < size:
+        values = values + swap(values, size, bits, axis)
         bits *= 2
     return values
 
@@ -764,7 +778,7 @@
             pltpu.SemaphoreType.DMA((n,)),
         ],
         compiler_params=pltpu.CompilerParams(vmem_limit_bytes=VMEM_LIMIT),
-        cost_estimate=cost_of(0.3 * 17.0 * total * ff / (2048 * 384)),
+        cost_estimate=cost_of(0.05 * 17.0 * total * ff / (2048 * 384)),
         name="feed",
     )(*x_pieces, *y_pieces, w)
 
@@ -782,8 +796,7 @@
     kv_share = max(n // KEY_VALUE_HEADS, 1)
     ff = wg.shape[1] // n
     q_cols = heads * HEAD_SIZE
-    parts = 2 if ff % 256 == 0 else 1
-    ff_part = ff // parts
+    parts = [2 * ff // 3, ff // 3] if ff % 384 == 0 and ff > 384 else [ff]
 
     def cols(w, width, index):
         return lax.dynamic_slice_in_dim(w, index * width, width, axis=1)
@@ -802,16 +815,17 @@
     gain_rows = -(-gains.shape[0] // (16 * width)) * 16
     gains = jnp.pad(gains, (0, gain_rows * width - gains.shape[0])).reshape(gain_rows, width)
     pack = lax.all_gather(jnp.concatenate([w_attn, gains], axis=0), "fsdp", axis=0)
-    x_pieces = gather_pieces(x, n)
+    x_pair = gather_pair(x, n)
+    dy_pair = gather_pair(after(dy, x_pair), n)
+    x_pieces = gather_rest(x_pair, n, last=[dy_pair])
 
     def feed_weights(part, gate):
-        at = parts * me + part
-        w = jnp.concatenate([cols(w, ff_part, at) for w in (wg, wu, wd)], axis=1)
-        return whole(after(w, gate))
-
-    w_ff = [feed_weights(0, x_pieces[0])]
-    dy_pieces = gather_pieces(after(dy, x_pieces[0]), n, [x_pieces[len(x_pieces) // 4]])
-    pack = after(pack, dy_pieces[0])
+        at = ff * me + sum(parts[:part])
+        w = [lax.dynamic_slice_in_dim(w, at, parts[part], axis=1) for w in (wg, wu, wd)]
+        return whole(after(jnp.concatenate(w, axis=1), gate))
+
+    w_ff = [feed_weights(0, x_pair)]
+    dy_pieces = gather_rest(dy_pair, n, [x_pieces[-1]])
     w_in = pack[:, :shard, :in_cols].reshape(depth, in_cols)
     wo_c = pack[:, :shard, in_cols:].reshape(depth, q_cols)
     gains = pack[:, shard:].reshape(n_fsdp, -1)
@@ -833,51 +847,53 @@
     xn, q_raw, k_raw, qb, kb, vb = project(
         x_pieces, n, places, attn_gain, pack, qg, kg, cosine, sine, heads
     )
-    w_ff += [feed_weights(part, qb) for part in range(1, parts)]
+    w_ff += [feed_weights(part, qb) for part in range(1, len(parts))]
     o, a, a_index, lse = attend(
         lengths, places, by_index, after(qb, dy_pieces[len(dy_pieces) // 4]), kb, vb, heads
     )
     a_tok = exchange(a_index.reshape(n, rows, q_cols))
-    wo_slots = assemble(gather_pieces(wo_c, n, [qb], [a_index]), n)
+    wo_slots = assemble(gather_rest(gather_pair(after(wo_c, x_pieces[-1]), n), n, [qb], [a_index]), n)
     h1, xn2 = branch(order, a_tok, wo_slots, x, mlp_gain)
 
-    xn2_pieces = gather_pieces(xn2, n)
+    xn2_pieces = gather_rest(gather_pair(xn2, n), n)
+    xn2_pieces = [after(xn2_pieces[0], w_in)] + xn2_pieces[1:]
     d_gu, hm, grads = [], [], []
 
-    def ff_grad(d_part, hm_part):
+    def ff_grad(d_part, hm_part, cover):
         return weight_grad(
             [
-                (xn2_pieces, d_part.reshape(total, 2 * ff_part)),
-                (dy_pieces, hm_part.reshape(total, ff_part)),
+                (xn2_pieces, d_part.reshape(total, -1)),
+                (dy_pieces, hm_part.reshape(total, -1)),
             ],
-            n, n_fsdp,
+            n, n_fsdp, cover=cover,
         )
 
     for w in w_ff:
         if d_gu:
-            grads += ff_grad(d_gu[-1], hm[-1])
+            grads += ff_grad(d_gu[-1], hm[-1], 0.05)
             xn2_pieces = [after(xn2_pieces[0], grads[-1])] + xn2_pieces[1:]
         d_part, hm_part = feed(xn2_pieces, dy_pieces, n, w)
         d_gu.append(d_part)
         hm.append(hm_part)
-    got = scatter_far(d_gu, w_ff, 0, n)
-    send, keep = scatter_near(got, near_product(d_gu, w_ff, 0, n))
-    grads += ff_grad(after(d_gu[-1], send), hm[-1])
+    to_xn2 = SumScatter(d_gu, w_ff, 0, n, halves=True)
+    send = to_xn2.add_send(d_gu)
+    grads += ff_grad(after(d_gu[-1], send), hm[-1], 1.0)
     d_ff = [reduce_rows(grad, n) for grad in grads]
-    hm = [after(hm[0], grads[-1])] + hm[1:]
-    m_got = scatter_far(hm, w_ff, 2, n)
-    m_near = near_product(hm, w_ff, 2, n)
-    d_xn2 = scatter_last(send, keep, n)
+    to_xn2.add_keep([after(d_gu[0], send)] + d_gu[1:])
+    to_xn2.second(held=grads[-1])
+    hm = [after(hm[0], to_xn2.last)] + hm[1:]
+    to_m = SumScatter(hm, w_ff, 2, n)
+    d_xn2 = after(to_xn2.result(), grads[-1], to_m.far)
 
     d_h1, dz, d_mlp_gain, da = branch_back(
-        order, after(d_xn2, grads[-1], m_got if m_near is None else m_near), h1, dy, mlp_gain, wo_slots
+        order, d_xn2, h1, dy, mlp_gain, wo_slots
     )
     da = exchange(da).reshape(total, q_cols)
-    m_send, m_keep = scatter_near(after(m_got, d_h1), m_near)
-    dz_pieces = gather_pieces(dz, n)
-    da = after(da, dz_pieces[0])
-    m = scatter_last(after(m_send, dz_pieces[len(dz_pieces) // 2]), m_keep, n)
-    output = (h1 + m).astype(bf16)
+    hm = [after(hm[0], d_h1)] + hm[1:]
+    dz_pair = after(gather_pair(dz, n, [to_m.add_send(hm)]), da)
+    dz_other = swap_first(dz_pair, n, False) if n == 8 else dz_pair
+    da = after(da, dz_pair, d_ff[0])
+    to_m.step(dz_pair)
     d_ff[0] = exchange(after(d_ff[0], da))
     d_qkv, d_qg, d_kg, *key_sums = attend_back(
         lengths, places, by_index, qb, kb, vb, da, o, lse, q_raw, k_raw, qg, kg, cosine, sine,
@@ -898,29 +914,34 @@
         dk = scale * (grad - hat * jnp.mean(grad * hat, axis=-1, keepdims=True))
         d_kv = jnp.concatenate([dk, dv], axis=1).astype(bf16).reshape(2 * n, -1, 2 * HEAD_SIZE)
         d_qkv = jnp.concatenate([d_qkv, d_kv[places].reshape(total, -1)], axis=1)
+    dz_pieces = gather_rest(dz_pair, n, last=[d_qkv], other=dz_other)
     d_attn, d_attn_gain = weight_grad(
-        [([xn.reshape(total, depth)], d_qkv), (dz_pieces, a)], n, n_fsdp, w_in,
+        [([after(xn, d_ff[-1]).reshape(total, depth)], d_qkv), (dz_pieces, a)], n, n_fsdp, w_in,
         attn_gain.reshape(depth, 1),
     )
-    d_attn = reduce_rows(d_attn, n)
-    left = [after(d_qkv, d_ff[0]).reshape(n, rows, in_cols)]
-    got = scatter_far(left, [w_in], 0, n)
-    d_xn = scatter_last(*scatter_near(got, near_product(left, [w_in], 0, n)), n)
+    d_attn_sum = reduce_rows(d_attn, n)
+    to_m.second(held=d_attn, stepped=True)
+    sums = jnp.concatenate([d_attn_gain[:, 0], d_mlp_gain[0], d_qg[0], d_kg[0]])
+    sums = sum_across(sums.reshape(-1, HEAD_SIZE), n, 2, "ctx")
+    left = after(d_qkv, d_attn, to_m.last, sums).reshape(n, rows, in_cols)
+    to_xn = SumScatter([left], [w_in], 0, n, cover=0.1)
+    to_xn.add_send([left])
+    to_xn.second(d_ff[0])
+    d_ff = d_ff[:1] + [exchange(after(d, to_xn.last)) for d in d_ff[1:]]
+    sums = sum_across(sums + swap(sums, n, 1), n_fsdp, 1, "fsdp")
+    d_xn = to_xn.result()
+    output = (h1 + to_m.result()).astype(bf16)
+    sums = sums.reshape(-1)
     x_float = x.astype(f32)
     scale_one = rms_scale(x_float)
     hat_one = x_float * scale_one
     e = d_xn * attn_gain
     dx = d_h1 + scale_one * (e - hat_one * jnp.mean(e * hat_one, axis=-1, keepdims=True))
 
-    sums = sum_all(
-        jnp.concatenate([d_attn_gain[:, 0], d_mlp_gain[0], d_qg[0], d_kg[0]]).reshape(-1, HEAD_SIZE),
-        n, n_fsdp,
-    ).reshape(-1)
-    d_ff = d_ff[:1] + [exchange(d) for d in d_ff[1:]]
-    d_attn = exchange(d_attn)
+    d_attn = exchange(d_attn_sum)
     d_wg, d_wu, d_wd = join_columns(
         d_ff,
-        [[(p, k * ff_part, (k + 1) * ff_part) for p in range(parts)] for k in range(3)],
+        [[(p, k * size, (k + 1) * size) for p, size in enumerate(parts)] for k in range(3)],
     )
     k_cols, v_cols = q_cols + HEAD_SIZE, q_cols + 2 * HEAD_SIZE
     kv_parts = [[(0, q_cols, k_cols)], [(0, k_cols, v_cols)]]

time: 623 us -> 594 us (0.953)
  Pallas kernels: 269 us -> 255 us
  waiting for transfers between devices: 213 us -> 202 us
  starting transfers between devices: 54 us -> 47.1 us
    ppermute x18 -> x19, waiting for transfers between devices: 47.1 us -> 18 us  [swap(): return lax.ppermute(values, axis, [(c, c ^ bits) for c in range(n)])]
    reduce_scatter x3, waiting for transfers between devices: 0.02 us -> 27.3 us  [reduce_rows(): summed = lax.psum_scatter(grad, 'fsdp', scatter_dimension=0, tiled=True)]
    pallas_call x9 -> x8, Pallas kernels: 72.9 us -> 60.7 us  [mm_slots(): pl.pallas_call(functools.partial(mm_kernel, len(lefts), int(add is not No...]
    ppermute x16, waiting for transfers between devices: 126 us -> 115 us  [swap_first(): lax.ppermute(values, 'ctx', [(c, c ^ (2 if (c % 2 == 0) == first else 4))...]
  transfers between devices with their start and end apart: 45 -> 46, of which waited for: 23 -> 24; matrix products, arithmetic and copies ran while one was open for 9% -> 8% of each run, Pallas kernels for 43% -> 43%
where the time goes in v4:
time: 594 us; the launch traced here: 585 us
  Pallas kernels  255 us (43%)
  waiting for transfers between devices  202 us (34%)
  starting transfers between devices  47.1 us (8%)
  other arithmetic  43.2 us (7%)
  local copies, waits for them, and re-layouts  22.5 us (4%)
  between operations  15.6 us (3%)
    ppermute x16, waiting for transfers between devices, swap_first(): lax.ppermute(values, 'ctx', [(c, c ^ (2 if (c % 2 == 0) == first else 4))...  115 us
    pallas_call x8, Pallas kernels, mm_slots(): pl.pallas_call(functools.partial(mm_kernel, len(lefts), int(add is not No...  60.7 us
    pallas_call x3, Pallas kernels, weight_grad(): pl.pallas_call(functools.partial(weight_kernel, [len(pieces) for pieces,...  49 us
    pallas_call x2, Pallas kernels, feed(): pl.pallas_call(functools.partial(feed_kernel, len(x_pieces)), grid=(n //...  38.7 us
    all_to_all x5, waiting for transfers between devices, exchange(): return lax.all_to_all(blocks, 'ctx', 0, 0, tiled=True)  35 us
    pallas_call x1, Pallas kernels, attend_back(): pl.pallas_call(functools.partial(attend_back_kernel, heads, tile, finish_...  30 us
    reduce_scatter x3, waiting for transfers between devices, reduce_rows(): summed = lax.psum_scatter(grad, 'fsdp', scatter_dimension=0, tiled=True)  27.3 us
    ppermute x16, starting transfers between devices, swap_first(): lax.ppermute(values, 'ctx', [(c, c ^ (2 if (c % 2 == 0) == first else 4))...  19.4 us
  transfers between devices with their start and end apart: 46, of which 24 were waited for; matrix products, arithmetic and copies ran while one was open for 8% of the time, Pallas kernels for 43%

profile of v4, /device:TPU:0, one launch (start us, length us, event | category | flops | bytes accessed | tf_op | source)
XLA Modules:
  0.0 585.2 jit_solution(6587215171777989695)
XLA Ops:
  14.2 12.8 %collective-permute-done = bf16[256,2048]{1,0:T(8,128)(2,1)S(1)} collective-permute-done((bf16[256,2048]{1,0:T(8,128)(2,1)S(1)}, bf16[256,2048]{1,0:T(8,128)(2,1)S(1)}, u32[]{:S(2)}, u32[]{:S(2)}) %collective-permute-start) | collective-permute-done | bytes 1048608 | tf_op jit(solution)/shard_map/ppermute | solution.py:51
  34.4 22.3 %collective-permute-done.2 = bf16[256,2048]{1,0:T(8,128)(2,1)} collective-permute-done((bf16[256,2048]{1,0:T(8,128)(2,1)S(1)}, bf16[256,2048]{1,0:T(8,128)(2,1)}, u32[]{:S(2)}, u32[]{:S(2)}) %collective-permute-start.2) | collective-permute-done | bytes 1048608 | tf_op jit(solution)/shard_map/ppermute | solution.py:51
  58.1 7.6 %collective-permute-done.1.refs_1_ = bf16[512,2048]{1,0:T(8,128)(2,1)} collective-permute-done((bf16[512,2048]{1,0:T(8,128)(2,1)}, bf16[512,2048]{1,0:T(8,128)(2,1)}, u32[]{:S(2)}, u32[]{:S(2)}) %collective-permute-start.1) | collective-permute-done | bytes 2097184 | tf_op jit(solution)/shard_map/ppermute | solution.py:51
  68.3 4.8 sine_multiply_fusion
  73.1 6.0 %all-gather.9.cloned.1.call-done = bf16[2112,768]{1,0:T(8,128)(2,1)} async-done(((bf16[528,768]{1,0:T(8,128)(2,1)}), bf16[2112,768]{1,0:T(8,128)(2,1)}) %all-gather.9.cloned.1.call-update) | async-done | bytes 3244048 | tf_op jit(solution)/shard_map/all_gather | solution.py:817
  86.8 17.0 %project.1 = (bf16[8,256,2048]{2,1,0:T(8,128)(2,1)}, f32[2048,256]{1,0:T(8,128)}, f32[2048,128]{1,0:T(8,128)}, bf16[2048,256]{1,0:T(8,128)(2,1)}, bf16[2048,128]{1,0:T(8,128)(2,1)}, /*index=5*/bf16[2048,128]{1,0:T(8,128)(2,1)}) custom-call(s32[16]{0:T(128)} %select_n.79.place_ref, bf16[512,2048]{1,0:T(8,128)(2,1)} %pad_maximum_fusion.refs_0_, ...), custom_call_target="tpu_custom_call" | custom-call | flops 5280000000 | bytes 1048576 | tf_op jit(solution)/shard_map/project/pallas_call | solution.py:370
  109.7 7.1 %collective-permute-done.5.refs_5_.refs_6_ = bf16[512,2048]{1,0:T(8,128)(2,1)} collective-permute-done((bf16[512,2048]{1,0:T(8,128)(2,1)S(1)}, bf16[512,2048]{1,0:T(8,128)(2,1)}, u32[]{:S(2)}, u32[]{:S(2)}) %collective-permute-start.5) | collective-permute-done | bytes 2097184 | tf_op jit(solution)/shard_map/ppermute | solution.py:51
  116.7 17.4 %attend.1 = (f32[2048,256]{1,0:T(8,128)}, bf16[2048,256]{1,0:T(8,128)(2,1)}, bf16[2048,256]{1,0:T(8,128)(2,1)}, f32[2,2048]{1,0:T(2,128)}) custom-call(s32[1]{0:T(128)S(6)} %copy.41.length_ref, s32[16]{0:T(128)} %select_n.79.place_ref, s32[16]{0:T(128)} %reshape.201.index_ref, bf16[2048,256]{1,0:T(8,128)(2,1)} %get-tuple-element.81.q_ref, ...), custom_call_target="tpu_custom_call" | custom-call | flops 6104999936 | bytes 1048576 | tf_op jit(solution)/shard_map/attend/pallas_call | solution.py:470
  134.1 5.1 collective-permute-done.7.refs_1_
  140.5 3.7 all-to-all-start
  144.8 6.6 %assemble.1.wo_ref = bf16[8,2048,256]{2,1,0:T(8,128)(2,1)} custom-call(bf16[4096,256]{1,0:T(8,128)(2,1)} %pad_maximum_fusion.2.refs_0_, bf16[4096,256]{1,0:T(8,128)(2,1)} %collective-permute-done.7.refs_1_, bf16[4096,256]{1,0:T(8,128)(2,1)} %collective-permute-done.8.refs_2_, bf16[4096,256]{1,0:T(8,128)(2,1)} %collective-permute-done.9.refs_3_), custom_call_target="tpu_custom_call" | custom-call | flops 1980000000 | bytes 1048576 | tf_op jit(solution)/shard_map/assemble/pallas_call | solution.py:123
  151.4 8.1 %all-to-all-done.a_ref = bf16[8,256,256]{2,1,0:T(8,128)(2,1)S(1)} async-done(((bf16[8,256,256]{2,1,0:T(8,128)(2,1)}), bf16[8,256,256]{2,1,0:T(8,128)(2,1)S(1)}, u32[]{:S(2)}, u32[]{:S(2)}) %all-to-all-start) | async-done | bytes 1048608 | tf_op jit(solution)/shard_map/all_to_all | solution.py:229
  160.5 11.1 %branch.1 = (f32[256,2048]{1,0:T(8,128)}, bf16[256,2048]{1,0:T(8,128)(2,1)}) custom-call(s32[8]{0:T(128)} %copy-done.22, bf16[8,256,256]{2,1,0:T(8,128)(2,1)} %copy-done.10, bf16[8,2048,256]{2,1,0:T(8,128)(2,1)} %assemble.1.wo_ref, bf16[256,2048]{1,0:T(8,128)(2,1)} %bitcast.95, f32[1,2048]{1,0:T(1,128)} %bitcast.126), custom_call_target="tpu_custom_call" | custom-call | flops 3630000128 | bytes 1048576 | tf_op jit(solution)/shard_map/branch/pallas_call | solution.py:648
  175.4 11.3 %collective-permute-done.10 = bf16[256,2048]{1,0:T(8,128)(2,1)} collective-permute-done((bf16[256,2048]{1,0:T(8,128)(2,1)}, bf16[256,2048]{1,0:T(8,128)(2,1)}, u32[]{:S(2)}, u32[]{:S(2)}) %collective-permute-start.10) | collective-permute-done | bytes 1048608 | tf_op jit(solution)/shard_map/ppermute | solution.py:51
  190.6 25.3 %collective-permute-done.11.refs_1_ = bf16[512,2048]{1,0:T(8,128)(2,1)} collective-permute-done((bf16[512,2048]{1,0:T(8,128)(2,1)}, bf16[512,2048]{1,0:T(8,128)(2,1)}, u32[]{:S(2)}, u32[]{:S(2)}) %collective-permute-start.11) | collective-permute-done | bytes 2097184 | tf_op jit(solution)/shard_map/ppermute | solution.py:51
  220.3 21.4 %feed.2 = (bf16[8,256,1024]{2,1,0:T(8,128)(2,1)}, bf16[8,256,512]{2,1,0:T(8,128)(2,1)}) custom-call(bf16[512,2048]{1,0:T(8,128)(2,1)} %pad_maximum_fusion.3.refs_0_, bf16[512,2048]{1,0:T(8,128)(2,1)} %collective-permute-done.11.refs_1_, bf16[512,2048]{1,0:T(8,128)(2,1)} %collective-permute-done.12.refs_2_, ...), custom_call_target="tpu_custom_call" | custom-call | flops 1246666624 | bytes 1048576 | tf_op jit(solution)/shard_map/feed/pallas_call | solution.py:761
  241.8 19.6 %weight_grad.3 = bf16[4,8,64,1536]{3,2,1,0:T(8,128)(2,1)} custom-call(bf16[512,2048]{1,0:T(8,128)(2,1)} %pad_maximum_fusion.3.refs_0_, bf16[512,2048]{1,0:T(8,128)(2,1)} %collective-permute-done.11.refs_1_, bf16[512,2048]{1,0:T(8,128)(2,1)} %collective-permute-done.12.refs_2_, bf16[512,2048]{1,0:T(8,128)(2,1)} %collective-permute-done.13.refs_3_, ...), custom_call_target="tpu_custom_call" | custom-call | flops 1173333376 | bytes 1048576 | tf_op jit(solution)/shard_map/weight_grad/pallas_call | solution.py:265
  261.5 17.3 %feed.3 = (bf16[8,256,512]{2,1,0:T(8,128)(2,1)}, bf16[8,256,256]{2,1,0:T(8,128)(2,1)}) custom-call(bf16[512,2048]{1,0:T(8,128)(2,1)} %pad_maximum_fusion.3.refs_0_, bf16[512,2048]{1,0:T(8,128)(2,1)} %collective-permute-done.11.refs_1_, bf16[512,2048]{1,0:T(8,128)(2,1)} %collective-permute-done.12.refs_2_, bf16[512,2048]{1,0:T(8,128)(2,1)} %collective-permute-done.13.refs_3_, ...), custom_call_target="tpu_custom_call" | custom-call | flops 623333312 | bytes 1048576 | tf_op jit(solution)/shard_map/feed/pallas_call | solution.py:761
  278.7 7.4 %mm_slots.8 = bf16[2,256,2048]{2,1,0:T(8,128)(2,1)} custom-call(bf16[8,256,1024]{2,1,0:T(8,128)(2,1)} %get-tuple-element.97.refs_0_, bf16[8,256,512]{2,1,0:T(8,128)(2,1)} %get-tuple-element.98.refs_1_, bf16[2048,1536]{1,0:T(8,128)(2,1)} %all-gather.5.cloned.1.call-done.refs_8_.refs_2_, bf16[2048,768]{1,0:T(8,128)(2,1)} %all-gather.7.cloned.1.call-done.refs_8_.refs_3_), custom_call_target="tpu_custom_call" | custom-call | flops 6600000000 | bytes 1048576 | tf_op jit(solution)/shard_map/mm_slots/pallas_call | solution.py:163
  286.3 7.5 %mm_slots.10 = bf16[2,256,2048]{2,1,0:T(8,128)(2,1)} custom-call(bf16[8,256,1024]{2,1,0:T(8,128)(2,1)} %get-tuple-element.97.refs_0_, bf16[8,256,512]{2,1,0:T(8,128)(2,1)} %get-tuple-element.98.refs_1_, bf16[2048,1536]{1,0:T(8,128)(2,1)} %all-gather.5.cloned.1.call-done.refs_8_.refs_2_, bf16[2048,768]{1,0:T(8,128)(2,1)} %all-gather.7.cloned.1.call-done.refs_8_.refs_3_), custom_call_target="tpu_custom_call" | custom-call | flops 6600000000 | bytes 1048576 | tf_op jit(solution)/shard_map/mm_slots/pallas_call | solution.py:163
  295.4 7.9 %mm_slots.9 = bf16[2,256,2048]{2,1,0:T(8,128)(2,1)} custom-call(bf16[8,256,1024]{2,1,0:T(8,128)(2,1)} %get-tuple-element.97.refs_0_, bf16[8,256,512]{2,1,0:T(8,128)(2,1)} %get-tuple-element.98.refs_1_, bf16[2048,1536]{1,0:T(8,128)(2,1)} %all-gather.5.cloned.1.call-done.refs_8_.refs_2_, bf16[2048,768]{1,0:T(8,128)(2,1)} %all-gather.7.cloned.1.call-done.refs_8_.refs_3_, ...), custom_call_target="tpu_custom_call" | custom-call | flops 6600000000 | bytes 1048576 | tf_op jit(solution)/shard_map/mm_slots/pallas_call | solution.py:163
  305.3 8.3 %mm_slots.11 = f32[2,256,2048]{2,1,0:T(8,128)} custom-call(bf16[8,256,1024]{2,1,0:T(8,128)(2,1)} %get-tuple-element.97.refs_0_, bf16[8,256,512]{2,1,0:T(8,128)(2,1)} %get-tuple-element.98.refs_1_, bf16[2048,1536]{1,0:T(8,128)(2,1)} %all-gather.5.cloned.1.call-done.refs_8_.refs_2_, bf16[2048,768]{1,0:T(8,128)(2,1)} %all-gather.7.cloned.1.call-done.refs_8_.refs_3_, ...), custom_call_target="tpu_custom_call" | custom-call | flops 6600000000 | bytes 1048576 | tf_op jit(solution)/shard_map/mm_slots/pallas_call | solution.py:163
  313.6 14.2 %weight_grad.4 = bf16[4,8,64,768]{3,2,1,0:T(8,128)(2,1)} custom-call(bf16[512,2048]{1,0:T(8,128)(2,1)} %pad_maximum_fusion.3.refs_0_, bf16[512,2048]{1,0:T(8,128)(2,1)} %collective-permute-done.11.refs_1_, bf16[512,2048]{1,0:T(8,128)(2,1)} %collective-permute-done.12.refs_2_, bf16[512,2048]{1,0:T(8,128)(2,1)} %collective-permute-done.13.refs_3_, ...), custom_call_target="tpu_custom_call" | custom-call | flops 11733332992 | bytes 1048576 | tf_op jit(solution)/shard_map/weight_grad/pallas_call | solution.py:265
  331.5 7.5 %mm_slots.12 = bf16[4,256,2048]{2,1,0:T(8,128)(2,1)} custom-call(bf16[8,256,512]{2,1,0:T(8,128)(2,1)} %get-tuple-element.104.refs_0_, bf16[8,256,256]{2,1,0:T(8,128)(2,1)} %get-tuple-element.99.refs_1_, bf16[2048,1536]{1,0:T(8,128)(2,1)} %all-gather.5.cloned.1.call-done.refs_8_.refs_2_, bf16[2048,768]{1,0:T(8,128)(2,1)} %all-gather.7.cloned.1.call-done.refs_8_.refs_3_), custom_call_target="tpu_custom_call" | custom-call | flops 6600000000 | bytes 1048576 | tf_op jit(solution)/shard_map/mm_slots/pallas_call | solution.py:163
  339.5 14.2 %collective-permute-done.19 = bf16[256,2048]{1,0:T(8,128)(2,1)S(1)} collective-permute-done((bf16[256,2048]{1,0:T(8,128)(2,1)S(1)}, bf16[256,2048]{1,0:T(8,128)(2,1)S(1)}, u32[]{:S(2)}, u32[]{:S(2)}) %collective-permute-start.19) | collective-permute-done | bytes 1048608 | tf_op jit(solution)/shard_map/ppermute | solution.py:51
  355.6 13.0 %branch_back.1 = (f32[256,2048]{1,0:T(8,128)}, bf16[256,2048]{1,0:T(8,128)(2,1)}, f32[1,2048]{1,0:T(1,128)}, bf16[8,256,256]{2,1,0:T(8,128)(2,1)}) custom-call(s32[8]{0:T(128)} %copy-done.22, f32[256,2048]{1,0:T(8,128)} %bitcast_add_fusion.2.dxn_ref, f32[256,2048]{1,0:T(8,128)} %get-tuple-element.88.h1_ref, bf16[256,2048]{1,0:T(8,128)(2,1)} %bitcast.113, ...), custom_call_target="tpu_custom_call" | custom-call | flops 14300000256 | bytes 1048576 | tf_op jit(solution)/shard_map/branch_back/pallas_call | solution.py:696
  373.4 8.4 %mm_slots.13 = (f32[2,256,2048]{2,1,0:T(8,128)}, bf16[2,256,2048]{2,1,0:T(8,128)(2,1)}) custom-call(bf16[8,256,512]{2,1,0:T(8,128)(2,1)} %get-tuple-element.104.refs_0_, bf16[8,256,256]{2,1,0:T(8,128)(2,1)} %get-tuple-element.99.refs_1_, bf16[2048,1536]{1,0:T(8,128)(2,1)} %all-gather.5.cloned.1.call-done.refs_8_.refs_2_, ...), custom_call_target="tpu_custom_call" | custom-call | flops 6600000000 | bytes 1048576 | tf_op jit(solution)/shard_map/mm_slots/pallas_call | solution.py:163
  381.8 7.4 %collective-permute-done.21 = bf16[256,2048]{1,0:T(8,128)(2,1)S(1)} collective-permute-done((bf16[256,2048]{1,0:T(8,128)(2,1)}, bf16[256,2048]{1,0:T(8,128)(2,1)S(1)}, u32[]{:S(2)}, u32[]{:S(2)}) %collective-permute-start.21) | collective-permute-done | bytes 1048608 | tf_op jit(solution)/shard_map/ppermute | solution.py:51
  390.7 4.2 all-to-all-done.1
  396.3 30.0 %attend_back.1 = (bf16[2048,512]{1,0:T(8,128)(2,1)}, f32[1,128]{1,0:T(1,128)}, f32[1,128]{1,0:T(1,128)}) custom-call(s32[1]{0:T(128)S(6)} %copy.41.length_ref, s32[16]{0:T(128)} %select_n.79.place_ref, s32[16]{0:T(128)} %reshape.201.index_ref, bf16[2048,256]{1,0:T(8,128)(2,1)} %get-tuple-element.81.q_ref, bf16[2048,128]{1,0:T(8,128)(2,1)} %get-tuple-element.82.k_ref, ...), custom_call_target="tpu_custom_call" | custom-call | flops 36300001280 | bytes 1048576 | tf_op jit(solution)/shard_map/attend_back/pallas_call | solution.py:616
  429.0 6.3 %reduce-scatter.4.cloned.1.call-done = bf16[512,768]{1,0:T(8,128)(2,1)} async-done(((bf16[2048,768]{1,0:T(8,128)(2,1)}), bf16[512,768]{1,0:T(8,128)(2,1)}) %reduce-scatter.4.cloned.1.call-update) | async-done | bytes 786448 | tf_op jit(solution)/shard_map/reduce_scatter | solution.py:279
  435.3 15.1 %weight_grad.5 = (bf16[4,8,64,768]{3,2,1,0:T(8,128)(2,1)}, f32[2048,1]{1,0:T(8,128)}) custom-call(bf16[2048,2048]{1,0:T(8,128)(2,1)} %bitcast.136, bf16[2048,512]{1,0:T(8,128)(2,1)} %get-tuple-element.128.refs_1_, bf16[512,2048]{1,0:T(8,128)(2,1)} %pad_maximum_fusion.4.refs_2_, bf16[512,2048]{1,0:T(8,128)(2,1)} %collective-permute-done.22.refs_3_, ...), custom_call_target="tpu_custom_call" | custom-call | flops 11733332992 | bytes 1048576 | tf_op jit(solution)/shard_map/weight_grad/pallas_call | solution.py:265
  457.4 3.6 fusion.12
  461.0 6.1 %mm_slots.14 = bf16[4,256,2048]{2,1,0:T(8,128)(2,1)} custom-call(bf16[8,256,512]{2,1,0:T(8,128)(2,1)} %bitcast.98, bf16[2048,512]{1,0:T(8,128)(2,1)} %bitcast.93), custom_call_target="tpu_custom_call" | custom-call | flops 513333344 | bytes 1048576 | tf_op jit(solution)/shard_map/mm_slots/pallas_call | solution.py:163
  470.8 3.8 collective-permute-done.29.refs_2_
  474.6 7.6 %mm_slots.15 = (f32[2,256,2048]{2,1,0:T(8,128)}, bf16[2,256,2048]{2,1,0:T(8,128)(2,1)}) custom-call(bf16[8,256,512]{2,1,0:T(8,128)(2,1)} %bitcast.99, bf16[2048,512]{1,0:T(8,128)(2,1)} %bitcast.94, bf16[4,256,2048]{2,1,0:T(8,128)(2,1)} %collective-permute-done.29.refs_2_), custom_call_target="tpu_custom_call" | custom-call | flops 513333344 | bytes 1048576 | tf_op jit(solution)/shard_map/mm_slots/pallas_call | solution.py:163
  482.2 9.5 %all-to-all-done.2.refs_0_ = bf16[8,64,1536]{2,1,0:T(8,128)(2,1)S(1)} async-done(((bf16[8,64,1536]{2,1,0:T(8,128)(2,1)}), bf16[8,64,1536]{2,1,0:T(8,128)(2,1)S(1)}, u32[]{:S(2)}, u32[]{:S(2)}) %all-to-all-start.2) | async-done | bytes 1572896 | tf_op jit(solution)/shard_map/all_to_all | solution.py:229
  496.6 4.1 collective-permute-done.33
  501.3 4.8 collective-permute-done.34
  506.7 21.0 %reduce-scatter.8.cloned.1.call-done = bf16[512,768]{1,0:T(8,128)(2,1)} async-done(((bf16[2048,768]{1,0:T(8,128)(2,1)}), bf16[512,768]{1,0:T(8,128)(2,1)}) %reduce-scatter.8.cloned.1.call-update) | async-done | bytes 786448 | tf_op jit(solution)/shard_map/reduce_scatter | solution.py:279
  527.7 4.2 all-to-all-start.3
  537.3 7.3 %all-to-all-done.3.refs_0_ = bf16[8,64,768]{2,1,0:T(8,128)(2,1)} async-done(((bf16[8,64,768]{2,1,0:T(8,128)(2,1)}), bf16[8,64,768]{2,1,0:T(8,128)(2,1)}, u32[]{:S(2)}, u32[]{:S(2)}) %all-to-all-start.3) | async-done | bytes 786464 | tf_op jit(solution)/shard_map/all_to_all | solution.py:229
  544.6 4.2 all-to-all-start.4
  548.8 4.4 fusion.14
  553.2 5.2 join_columns.2
  558.4 5.8 all-to-all-done.4.refs_1_
  564.2 6.3 %join_columns.3 = (f32[64,6144]{1,0:T(8,128)}, f32[64,6144]{1,0:T(8,128)}, f32[64,6144]{1,0:T(8,128)}) custom-call(bf16[8,64,1536]{2,1,0:T(8,128)(2,1)} %copy-done.8, bf16[8,64,768]{2,1,0:T(8,128)(2,1)} %all-to-all-done.4.refs_1_), custom_call_target="tpu_custom_call" | custom-call | flops 1100000000 | bytes 1048576 | tf_op jit(solution)/shard_map/join_columns/pallas_call | solution.py:293
  573.7 4.2 fusion.6
  (180 shorter events, 91.4 us)
Async XLA Ops:
  7.2 71.9 %all-gather.9.cloned.1.call-start = ((), (), s32[]{:S(2)}) async-start(), calls=%async_computation.13 | async-start | bytes 4055040 | tf_op jit(solution)/shard_map/all_gather | solution.py:817
  11.1 207.5 %all-gather.5.cloned.1.call-start = ((), (), s32[]{:S(2)}) async-start(), calls=%async_computation.8 | async-start | bytes 7864320 | tf_op jit(solution)/shard_map/all_gather | solution.py:805
  11.2 15.8 %collective-permute-start = (bf16[256,2048]{1,0:T(8,128)(2,1)S(1)}, bf16[256,2048]{1,0:T(8,128)(2,1)S(1)}, u32[]{:S(2)}, u32[]{:S(2)}) collective-permute-start(bf16[256,2048]{1,0:T(8,128)(2,1)S(1)} %bitcast.96), channel_id=1, source_target_pairs={{0,8},{4,20},{8,0},{12,28},{16,24},{20,4},{24,16},{28,12},{1,9},{5... | collective-permute-start | bytes 3145736 | tf_op jit(solution)/shard_map/ppermute | solution.py:51
  28.4 37.2 %collective-permute-start.1 = (bf16[512,2048]{1,0:T(8,128)(2,1)}, bf16[512,2048]{1,0:T(8,128)(2,1)}, u32[]{:S(2)}, u32[]{:S(2)}) collective-permute-start(bf16[512,2048]{1,0:T(8,128)(2,1)} %pad_maximum_fusion.refs_0_), channel_id=1, source_target_pairs={{0,16},{4,12},{8,24},{12,4},{16,0},{20,28},{24,8},{28,20},{1,17},{... | collective-permute-start | bytes 6291464 | tf_op jit(solution)/shard_map/ppermute | solution.py:51
  30.5 26.2 %collective-permute-start.2 = (bf16[256,2048]{1,0:T(8,128)(2,1)S(1)}, bf16[256,2048]{1,0:T(8,128)(2,1)}, u32[]{:S(2)}, u32[]{:S(2)}) collective-permute-start(bf16[256,2048]{1,0:T(8,128)(2,1)S(1)} %bitcast.114), channel_id=1, source_target_pairs={{0,8},{4,20},{8,0},{12,28},{16,24},{20,4},{24,16},{28,12},{1,9},{5... | collective-permute-start | bytes 3145736 | tf_op jit(solution)/shard_map/ppermute | solution.py:51
  58.1 131.9 %copy-start = (bf16[512,2048]{1,0:T(8,128)(2,1)}, bf16[512,2048]{1,0:T(8,128)(2,1)S(1)}, u32[]{:S(2)}) copy-start(bf16[512,2048]{1,0:T(8,128)(2,1)S(1)} %pad_maximum_fusion.1.refs_4_.refs_5_) | copy-start | bytes 6291460
  65.7 14.8 %collective-permute-start.4 = (bf16[512,2048]{1,0:T(8,128)(2,1)}, bf16[512,2048]{1,0:T(8,128)(2,1)}, u32[]{:S(2)}, u32[]{:S(2)}) collective-permute-start(bf16[512,2048]{1,0:T(8,128)(2,1)} %collective-permute-done.1.refs_1_), channel_id=1, source_target_pairs={{0,4},{4,0},{8,12},{12,8},{16,20},{20,16},{24,28},{28,24},{1,5},{5... | collective-permute-start | bytes 6291464 | tf_op jit(solution)/shard_map/ppermute | solution.py:47
  67.0 19.9 %collective-permute-start.3 = (bf16[512,2048]{1,0:T(8,128)(2,1)}, bf16[512,2048]{1,0:T(8,128)(2,1)}, u32[]{:S(2)}, u32[]{:S(2)}) collective-permute-start(bf16[512,2048]{1,0:T(8,128)(2,1)} %pad_maximum_fusion.refs_0_), channel_id=1, source_target_pairs={{0,4},{4,0},{8,12},{12,8},{16,20},{20,16},{24,28},{28,24},{1,5},{5... | collective-permute-start | bytes 6291464 | tf_op jit(solution)/shard_map/ppermute | solution.py:47
  80.5 23.4 %collective-permute-start.6 = (bf16[2048,256]{1,0:T(8,128)(2,1)S(1)}, bf16[2048,256]{1,0:T(8,128)(2,1)}, u32[]{:S(2)}, u32[]{:S(2)}) collective-permute-start(bf16[2048,256]{1,0:T(8,128)(2,1)S(1)} %bitcast.101), channel_id=1, source_target_pairs={{0,8},{4,20},{8,0},{12,28},{16,24},{20,4},{24,16},{28,12},{1,9},{5... | collective-permute-start | bytes 3145736 | tf_op jit(solution)/shard_map/ppermute | solution.py:51
  85.4 31.4 %collective-permute-start.5 = (bf16[512,2048]{1,0:T(8,128)(2,1)S(1)}, bf16[512,2048]{1,0:T(8,128)(2,1)}, u32[]{:S(2)}, u32[]{:S(2)}) collective-permute-start(bf16[512,2048]{1,0:T(8,128)(2,1)S(1)} %pad_maximum_fusion.1.refs_4_.refs_5_), channel_id=1, source_target_pairs={{0,16},{4,12},{8,24},{12,4},{16,0},{20,28},{24,8},{28,20},{1,17},{... | collective-permute-start | bytes 6291464 | tf_op jit(solution)/shard_map/ppermute | solution.py:51
  106.5 32.7 %collective-permute-start.7 = (bf16[4096,256]{1,0:T(8,128)(2,1)}, bf16[4096,256]{1,0:T(8,128)(2,1)}, u32[]{:S(2)}, u32[]{:S(2)}) collective-permute-start(bf16[4096,256]{1,0:T(8,128)(2,1)} %pad_maximum_fusion.2.refs_0_), channel_id=1, source_target_pairs={{0,16},{4,12},{8,24},{12,4},{16,0},{20,28},{24,8},{28,20},{1,17},{... | collective-permute-start | bytes 6291464 | tf_op jit(solution)/shard_map/ppermute | solution.py:51
  109.6 35.2 %collective-permute-start.8 = (bf16[4096,256]{1,0:T(8,128)(2,1)}, bf16[4096,256]{1,0:T(8,128)(2,1)}, u32[]{:S(2)}, u32[]{:S(2)}) collective-permute-start(bf16[4096,256]{1,0:T(8,128)(2,1)} %pad_maximum_fusion.2.refs_0_), channel_id=1, source_target_pairs={{0,4},{4,0},{8,12},{12,8},{16,20},{20,16},{24,28},{28,24},{1,5},{5... | collective-permute-start | bytes 6291464 | tf_op jit(solution)/shard_map/ppermute | solution.py:47
  139.2 5.6 collective-permute-start.9
  140.5 19.1 %all-to-all-start = ((bf16[8,256,256]{2,1,0:T(8,128)(2,1)}), bf16[8,256,256]{2,1,0:T(8,128)(2,1)S(1)}, u32[]{:S(2)}, u32[]{:S(2)}) async-start(bf16[8,256,256]{2,1,0:T(8,128)(2,1)} %bitcast.111), calls=%async_computation | async-start | bytes 2097152 | tf_op jit(solution)/shard_map/all_to_all | solution.py:229
  144.1 117.3 %all-gather.7.cloned.1.call-start = ((), (), s32[]{:S(2)}) async-start(), calls=%async_computation.9 | async-start | bytes 3932160 | tf_op jit(solution)/shard_map/all_gather | solution.py:805
  171.6 15.1 %collective-permute-start.10 = (bf16[256,2048]{1,0:T(8,128)(2,1)}, bf16[256,2048]{1,0:T(8,128)(2,1)}, u32[]{:S(2)}, u32[]{:S(2)}) collective-permute-start(bf16[256,2048]{1,0:T(8,128)(2,1)} %get-tuple-element.89), channel_id=1, source_target_pairs={{0,8},{4,20},{8,0},{12,28},{16,24},{20,4},{24,16},{28,12},{1,9},{5... | collective-permute-start | bytes 3145736 | tf_op jit(solution)/shard_map/ppermute | solution.py:51
  175.1 221.2 %reduce-scatter.6.cloned.1.call-start = ((), (), s32[]{:S(2)}) async-start(), calls=%async_computation.11 | async-start | bytes 7864320 | tf_op jit(solution)/shard_map/reduce_scatter | solution.py:279
  175.4 40.5 %copy-start.6 = (bf16[2112,768]{1,0:T(8,128)(2,1)S(1)}, bf16[2112,768]{1,0:T(8,128)(2,1)}, u32[]{:S(2)}) copy-start(bf16[2112,768]{1,0:T(8,128)(2,1)} %all-gather.9.cloned.1.call-done) | copy-start | bytes 9732100
  189.5 26.4 %collective-permute-start.11 = (bf16[512,2048]{1,0:T(8,128)(2,1)}, bf16[512,2048]{1,0:T(8,128)(2,1)}, u32[]{:S(2)}, u32[]{:S(2)}) collective-permute-start(bf16[512,2048]{1,0:T(8,128)(2,1)} %pad_maximum_fusion.3.refs_0_), channel_id=1, source_target_pairs={{0,16},{4,12},{8,24},{12,4},{16,0},{20,28},{24,8},{28,20},{1,17},{... | collective-permute-start | bytes 6291464 | tf_op jit(solution)/shard_map/ppermute | solution.py:51
  190.0 27.3 %collective-permute-start.14 = (bf16[512,2048]{1,0:T(8,128)(2,1)S(1)}, bf16[512,2048]{1,0:T(8,128)(2,1)S(1)}, u32[]{:S(2)}, u32[]{:S(2)}) collective-permute-start(bf16[512,2048]{1,0:T(8,128)(2,1)S(1)} %pad_maximum_fusion.1.refs_4_.refs_5_), channel_id=1, source_target_pairs={{0,4},{4,0},{8,12},{12,8},{16,20},{20,16},{24,28},{28,24},{1,5},{5... | collective-permute-start | bytes 6291464 | tf_op jit(solution)/shard_map/ppermute | solution.py:47
  190.0 28.6 %collective-permute-start.15 = (bf16[512,2048]{1,0:T(8,128)(2,1)}, bf16[512,2048]{1,0:T(8,128)(2,1)}, u32[]{:S(2)}, u32[]{:S(2)}) collective-permute-start(bf16[512,2048]{1,0:T(8,128)(2,1)} %collective-permute-done.5.refs_5_.refs_6_), channel_id=1, source_target_pairs={{0,4},{4,0},{8,12},{12,8},{16,20},{20,16},{24,28},{28,24},{1,5},{5... | collective-permute-start | bytes 6291464 | tf_op jit(solution)/shard_map/ppermute | solution.py:47
  190.6 28.1 %collective-permute-start.12 = (bf16[512,2048]{1,0:T(8,128)(2,1)}, bf16[512,2048]{1,0:T(8,128)(2,1)}, u32[]{:S(2)}, u32[]{:S(2)}) collective-permute-start(bf16[512,2048]{1,0:T(8,128)(2,1)} %pad_maximum_fusion.3.refs_0_), channel_id=1, source_target_pairs={{0,4},{4,0},{8,12},{12,8},{16,20},{20,16},{24,28},{28,24},{1,5},{5... | collective-permute-start | bytes 6291464 | tf_op jit(solution)/shard_map/ppermute | solution.py:47
  215.8 4.5 collective-permute-start.13
  286.2 8.0 %collective-permute-start.16 = (bf16[2,256,2048]{2,1,0:T(8,128)(2,1)}, bf16[2,256,2048]{2,1,0:T(8,128)(2,1)S(1)}, u32[]{:S(2)}, u32[]{:S(2)}) collective-permute-start(bf16[2,256,2048]{2,1,0:T(8,128)(2,1)} %mm_slots.8), channel_id=1, source_target_pairs={{0,4},{4,0},{8,12},{12,8},{16,20},{20,16},{24,28},{28,24},{1,5},{5... | collective-permute-start | bytes 6291464 | tf_op jit(solution)/shard_map/ppermute | solution.py:47
  293.7 10.2 %collective-permute-start.17 = (bf16[2,256,2048]{2,1,0:T(8,128)(2,1)}, bf16[2,256,2048]{2,1,0:T(8,128)(2,1)S(1)}, u32[]{:S(2)}, u32[]{:S(2)}) collective-permute-start(bf16[2,256,2048]{2,1,0:T(8,128)(2,1)} %mm_slots.10), channel_id=1, source_target_pairs={{0,4},{4,0},{8,12},{12,8},{16,20},{20,16},{24,28},{28,24},{1,5},{5... | collective-permute-start | bytes 6291464 | tf_op jit(solution)/shard_map/ppermute | solution.py:47
  303.3 26.2 %collective-permute-start.18 = (bf16[2,256,2048]{2,1,0:T(8,128)(2,1)}, bf16[2,256,2048]{2,1,0:T(8,128)(2,1)S(1)}, u32[]{:S(2)}, u32[]{:S(2)}) collective-permute-start(bf16[2,256,2048]{2,1,0:T(8,128)(2,1)} %mm_slots.9), channel_id=1, source_target_pairs={{0,16},{4,12},{8,24},{12,4},{16,0},{20,28},{24,8},{28,20},{1,17},{... | collective-permute-start | bytes 6291464 | tf_op jit(solution)/shard_map/ppermute | solution.py:51
  338.9 34.5 %collective-permute-start.20 = (bf16[4,256,2048]{2,1,0:T(8,128)(2,1)}, bf16[4,256,2048]{2,1,0:T(8,128)(2,1)}, u32[]{:S(2)}, u32[]{:S(2)}) collective-permute-start(bf16[4,256,2048]{2,1,0:T(8,128)(2,1)} %mm_slots.12), channel_id=1, source_target_pairs={{0,4},{4,0},{8,12},{12,8},{16,20},{20,16},{24,28},{28,24},{1,5},{5... | collective-permute-start | bytes 12582920 | tf_op jit(solution)/shard_map/ppermute | solution.py:47
  339.0 14.8 %collective-permute-start.19 = (bf16[256,2048]{1,0:T(8,128)(2,1)S(1)}, bf16[256,2048]{1,0:T(8,128)(2,1)S(1)}, u32[]{:S(2)}, u32[]{:S(2)}) collective-permute-start(bf16[256,2048]{1,0:T(8,128)(2,1)S(1)} %fusion.11), channel_id=1, source_target_pairs={{0,8},{4,20},{8,0},{12,28},{16,24},{20,4},{24,16},{28,12},{1,9},{5... | collective-permute-start | bytes 3145736 | tf_op jit(solution)/shard_map/ppermute | solution.py:51
  368.5 20.7 %collective-permute-start.21 = (bf16[256,2048]{1,0:T(8,128)(2,1)}, bf16[256,2048]{1,0:T(8,128)(2,1)S(1)}, u32[]{:S(2)}, u32[]{:S(2)}) collective-permute-start(bf16[256,2048]{1,0:T(8,128)(2,1)} %get-tuple-element.111), channel_id=1, source_target_pairs={{0,8},{4,20},{8,0},{12,28},{16,24},{20,4},{24,16},{28,12},{1,9},{5... | collective-permute-start | bytes 3145736 | tf_op jit(solution)/shard_map/ppermute | solution.py:51
  369.2 25.8 %all-to-all-start.1 = ((bf16[8,256,256]{2,1,0:T(8,128)(2,1)}), bf16[8,256,256]{2,1,0:T(8,128)(2,1)S(1)}, u32[]{:S(2)}, u32[]{:S(2)}) async-start(bf16[8,256,256]{2,1,0:T(8,128)(2,1)} %get-tuple-element.108), calls=%async_computation.2 | async-start | bytes 2097152 | tf_op jit(solution)/shard_map/all_to_all | solution.py:229
  372.8 62.5 %reduce-scatter.4.cloned.1.call-start = ((), (), s32[]{:S(2)}) async-start(), calls=%async_computation.10 | async-start | bytes 3932160 | tf_op jit(solution)/shard_map/reduce_scatter | solution.py:279
  373.3 154.3 %reduce-scatter.8.cloned.1.call-start = ((), (), s32[]{:S(2)}) async-start(), calls=%async_computation.12 | async-start | bytes 3932160 | tf_op jit(solution)/shard_map/reduce_scatter | solution.py:279
  395.0 31.4 %collective-permute-start.22 = (bf16[512,2048]{1,0:T(8,128)(2,1)}, bf16[512,2048]{1,0:T(8,128)(2,1)}, u32[]{:S(2)}, u32[]{:S(2)}) collective-permute-start(bf16[512,2048]{1,0:T(8,128)(2,1)} %pad_maximum_fusion.4.refs_2_), channel_id=1, source_target_pairs={{0,16},{4,12},{8,24},{12,4},{16,0},{20,28},{24,8},{28,20},{1,17},{... | collective-permute-start | bytes 6291464 | tf_op jit(solution)/shard_map/ppermute | solution.py:51
  396.3 38.9 %collective-permute-start.23 = (bf16[512,2048]{1,0:T(8,128)(2,1)}, bf16[512,2048]{1,0:T(8,128)(2,1)}, u32[]{:S(2)}, u32[]{:S(2)}) collective-permute-start(bf16[512,2048]{1,0:T(8,128)(2,1)} %pad_maximum_fusion.4.refs_2_), channel_id=1, source_target_pairs={{0,4},{4,0},{8,12},{12,8},{16,20},{20,16},{24,28},{28,24},{1,5},{5... | collective-permute-start | bytes 6291464 | tf_op jit(solution)/shard_map/ppermute | solution.py:47
  426.4 8.9 %collective-permute-start.24 = (bf16[512,2048]{1,0:T(8,128)(2,1)}, bf16[512,2048]{1,0:T(8,128)(2,1)}, u32[]{:S(2)}, u32[]{:S(2)}) collective-permute-start(bf16[512,2048]{1,0:T(8,128)(2,1)} %collective-permute-done.22.refs_3_), channel_id=1, source_target_pairs={{0,4},{4,0},{8,12},{12,8},{16,20},{20,16},{24,28},{28,24},{1,5},{5... | collective-permute-start | bytes 6291464 | tf_op jit(solution)/shard_map/ppermute | solution.py:47
  426.9 30.5 %collective-permute-start.25 = (bf16[2,256,2048]{2,1,0:T(8,128)(2,1)}, bf16[2,256,2048]{2,1,0:T(8,128)(2,1)S(1)}, u32[]{:S(2)}, u32[]{:S(2)}) collective-permute-start(bf16[2,256,2048]{2,1,0:T(8,128)(2,1)} %get-tuple-element.123), channel_id=1, source_target_pairs={{0,16},{4,12},{8,24},{12,4},{16,0},{20,28},{24,8},{28,20},{1,17},{... | collective-permute-start | bytes 6291464 | tf_op jit(solution)/shard_map/ppermute | solution.py:51
  452.0 3.8 collective-permute-start.27
  455.9 5.2 collective-permute-start.28
  467.1 7.5 %collective-permute-start.29 = (bf16[4,256,2048]{2,1,0:T(8,128)(2,1)}, bf16[4,256,2048]{2,1,0:T(8,128)(2,1)}, u32[]{:S(2)}, u32[]{:S(2)}) collective-permute-start(bf16[4,256,2048]{2,1,0:T(8,128)(2,1)} %mm_slots.14), channel_id=1, source_target_pairs={{0,4},{4,0},{8,12},{12,8},{16,20},{20,16},{24,28},{28,24},{1,5},{5... | collective-permute-start | bytes 12582920 | tf_op jit(solution)/shard_map/ppermute | solution.py:47
  467.1 24.6 %all-to-all-start.2 = ((bf16[8,64,1536]{2,1,0:T(8,128)(2,1)}), bf16[8,64,1536]{2,1,0:T(8,128)(2,1)S(1)}, u32[]{:S(2)}, u32[]{:S(2)}) async-start(bf16[8,64,1536]{2,1,0:T(8,128)(2,1)} %bitcast.19), calls=%async_computation.4 | async-start | bytes 3145728 | tf_op jit(solution)/shard_map/all_to_all | solution.py:229
  492.9 39.0 %collective-permute-start.30 = (bf16[2,256,2048]{2,1,0:T(8,128)(2,1)}, bf16[2,256,2048]{2,1,0:T(8,128)(2,1)S(1)}, u32[]{:S(2)}, u32[]{:S(2)}) collective-permute-start(bf16[2,256,2048]{2,1,0:T(8,128)(2,1)} %get-tuple-element.132), channel_id=1, source_target_pairs={{0,16},{4,12},{8,24},{12,4},{16,0},{20,28},{24,8},{28,20},{1,17},{... | collective-permute-start | bytes 6291464 | tf_op jit(solution)/shard_map/ppermute | solution.py:51
  493.4 1.2 collective-permute-start.32
  494.6 6.0 %collective-permute-start.33 = (f32[34,128]{1,0:T(8,128)S(1)}, f32[34,128]{1,0:T(8,128)S(1)}, u32[]{:S(2)}, u32[]{:S(2)}) collective-permute-start(f32[34,128]{1,0:T(8,128)S(1)} %add.153), channel_id=1, source_target_pairs={{0,1},{1,0},{2,3},{3,2},{4,5},{5,4},{6,7},{7,6},{8,9},{9,8},{10,11... | collective-permute-start | bytes 52232 | tf_op jit(solution)/shard_map/ppermute | solution.py:47
  495.9 53.0 %collective-permute-start.26 = (bf16[256,2048]{1,0:T(8,128)(2,1)}, bf16[256,2048]{1,0:T(8,128)(2,1)}, u32[]{:S(2)}, u32[]{:S(2)}) collective-permute-start(bf16[256,2048]{1,0:T(8,128)(2,1)} %fusion.12), channel_id=1, source_target_pairs={{0,8},{4,20},{8,0},{12,28},{16,24},{20,4},{24,16},{28,12},{1,9},{5... | collective-permute-start | bytes 3145736 | tf_op jit(solution)/shard_map/ppermute | solution.py:51
  500.7 5.4 collective-permute-start.34
  527.7 16.9 %all-to-all-start.3 = ((bf16[8,64,768]{2,1,0:T(8,128)(2,1)}), bf16[8,64,768]{2,1,0:T(8,128)(2,1)}, u32[]{:S(2)}, u32[]{:S(2)}) async-start(bf16[8,64,768]{2,1,0:T(8,128)(2,1)} %bitcast.117), calls=%async_computation.6 | async-start | bytes 1572864 | tf_op jit(solution)/shard_map/all_to_all | solution.py:229
  534.9 35.7 %collective-permute-start.31 = (bf16[256,2048]{1,0:T(8,128)(2,1)}, bf16[256,2048]{1,0:T(8,128)(2,1)}, u32[]{:S(2)}, u32[]{:S(2)}) collective-permute-start(bf16[256,2048]{1,0:T(8,128)(2,1)} %fusion.13), channel_id=1, source_target_pairs={{0,8},{4,20},{8,0},{12,28},{16,24},{20,4},{24,16},{28,12},{1,9},{5... | collective-permute-start | bytes 3145736 | tf_op jit(solution)/shard_map/ppermute | solution.py:51
  544.6 19.6 %all-to-all-start.4 = ((bf16[8,64,768]{2,1,0:T(8,128)(2,1)}), bf16[8,64,768]{2,1,0:T(8,128)(2,1)}, u32[]{:S(2)}, u32[]{:S(2)}) async-start(bf16[8,64,768]{2,1,0:T(8,128)(2,1)} %bitcast.116), calls=%async_computation.7 | async-start | bytes 1572864 | tf_op jit(solution)/shard_map/all_to_all | solution.py:229
  (25 other events, 273.5 us)
Sparse Core Ops, SparseCore 0:
  11.3 67.8 all-gather.8
  81.3 113.9 all-gather.4
  196.8 61.7 all-gather.6
  261.6 108.6 reduce-scatter.5
  375.6 59.5 reduce-scatter.3
  467.3 60.3 reduce-scatter.7

commit v5 on v4

--- a/solution.py
+++ b/solution.py
@@ -938,7 +938,7 @@
     e = d_xn * attn_gain
     dx = d_h1 + scale_one * (e - hat_one * jnp.mean(e * hat_one, axis=-1, keepdims=True))
 
-    d_attn = exchange(d_attn_sum)
+    d_attn = exchange(after(d_attn_sum, d_xn))
     d_wg, d_wu, d_wd = join_columns(
         d_ff,
         [[(p, k * size, (k + 1) * size) for p, size in enumerate(parts)] for k in range(3)],

time: 594 us -> 604 us (1.017)
  waiting for transfers between devices: 202 us -> 210 us
    reduce_scatter x3, waiting for transfers between devices: 27.3 us -> 4.43 us  [reduce_rows(): summed = lax.psum_scatter(grad, 'fsdp', scatter_dimension=0, tiled=True)]
    ppermute x16, waiting for transfers between devices: 115 us -> 137 us  [swap_first(): lax.ppermute(values, 'ctx', [(c, c ^ (2 if (c % 2 == 0) == first else 4))...]
    all_to_all x5, waiting for transfers between devices: 35 us -> 44.8 us  [exchange(): return lax.all_to_all(blocks, 'ctx', 0, 0, tiled=True)]
  transfers between devices with their start and end apart: 46 -> 46, of which waited for: 24 -> 24; matrix products, arithmetic and copies ran while one was open for 8% -> 9% of each run, Pallas kernels for 43% -> 42%
where the time goes in v5:
time: 604 us; the launch traced here: 595 us
  Pallas kernels  258 us (43%)
  waiting for transfers between devices  210 us (35%)
  starting transfers between devices  47.2 us (8%)
  other arithmetic  42.8 us (7%)
  local copies, waits for them, and re-layouts  20.9 us (3%)
  between operations  15.6 us (3%)
    ppermute x16, waiting for transfers between devices, swap_first(): lax.ppermute(values, 'ctx', [(c, c ^ (2 if (c % 2 == 0) == first else 4))...  137 us
    pallas_call x8, Pallas kernels, mm_slots(): pl.pallas_call(functools.partial(mm_kernel, len(lefts), int(add is not No...  60.8 us
    pallas_call x3, Pallas kernels, weight_grad(): pl.pallas_call(functools.partial(weight_kernel, [len(pieces) for pieces,...  49 us
    all_to_all x5, waiting for transfers between devices, exchange(): return lax.all_to_all(blocks, 'ctx', 0, 0, tiled=True)  44.8 us
    pallas_call x2, Pallas kernels, feed(): pl.pallas_call(functools.partial(feed_kernel, len(x_pieces)), grid=(n //...  38.7 us
    pallas_call x1, Pallas kernels, attend_back(): pl.pallas_call(functools.partial(attend_back_kernel, heads, tile, finish_...  31.9 us
    all_to_all x5, starting transfers between devices, exchange(): return lax.all_to_all(blocks, 'ctx', 0, 0, tiled=True)  19.2 us
    pallas_call x1, Pallas kernels, attend(): pl.pallas_call(functools.partial(attend_kernel, heads, tile), in_specs=[s...  18.6 us
  transfers between devices with their start and end apart: 46, of which 24 were waited for; matrix products, arithmetic and copies ran while one was open for 9% of the time, Pallas kernels for 42%

profile of v5, /device:TPU:0, one launch (start us, length us, event | category | flops | bytes accessed | tf_op | source)
XLA Modules:
  0.0 595.1 jit_solution(7074427752936478193)
XLA Ops:
  14.2 12.8 %collective-permute-done = bf16[256,2048]{1,0:T(8,128)(2,1)S(1)} collective-permute-done((bf16[256,2048]{1,0:T(8,128)(2,1)S(1)}, bf16[256,2048]{1,0:T(8,128)(2,1)S(1)}, u32[]{:S(2)}, u32[]{:S(2)}) %collective-permute-start) | collective-permute-done | bytes 1048608 | tf_op jit(solution)/shard_map/ppermute | solution.py:51
  34.4 22.3 %collective-permute-done.2 = bf16[256,2048]{1,0:T(8,128)(2,1)} collective-permute-done((bf16[256,2048]{1,0:T(8,128)(2,1)S(1)}, bf16[256,2048]{1,0:T(8,128)(2,1)}, u32[]{:S(2)}, u32[]{:S(2)}) %collective-permute-start.2) | collective-permute-done | bytes 1048608 | tf_op jit(solution)/shard_map/ppermute | solution.py:51
  58.1 7.6 %collective-permute-done.1.refs_1_ = bf16[512,2048]{1,0:T(8,128)(2,1)} collective-permute-done((bf16[512,2048]{1,0:T(8,128)(2,1)}, bf16[512,2048]{1,0:T(8,128)(2,1)}, u32[]{:S(2)}, u32[]{:S(2)}) %collective-permute-start.1) | collective-permute-done | bytes 2097184 | tf_op jit(solution)/shard_map/ppermute | solution.py:51
  68.3 4.8 sine_multiply_fusion
  73.1 6.0 %all-gather.9.cloned.1.call-done = bf16[2112,768]{1,0:T(8,128)(2,1)} async-done(((bf16[528,768]{1,0:T(8,128)(2,1)}), bf16[2112,768]{1,0:T(8,128)(2,1)}) %all-gather.9.cloned.1.call-update) | async-done | bytes 3244048 | tf_op jit(solution)/shard_map/all_gather | solution.py:817
  86.8 17.0 %project.1 = (bf16[8,256,2048]{2,1,0:T(8,128)(2,1)}, f32[2048,256]{1,0:T(8,128)}, f32[2048,128]{1,0:T(8,128)}, bf16[2048,256]{1,0:T(8,128)(2,1)}, bf16[2048,128]{1,0:T(8,128)(2,1)}, /*index=5*/bf16[2048,128]{1,0:T(8,128)(2,1)}) custom-call(s32[16]{0:T(128)} %select_n.79.place_ref, bf16[512,2048]{1,0:T(8,128)(2,1)} %pad_maximum_fusion.refs_0_, ...), custom_call_target="tpu_custom_call" | custom-call | flops 5280000000 | bytes 1048576 | tf_op jit(solution)/shard_map/project/pallas_call | solution.py:370
  109.6 7.1 %collective-permute-done.5.refs_5_.refs_6_ = bf16[512,2048]{1,0:T(8,128)(2,1)} collective-permute-done((bf16[512,2048]{1,0:T(8,128)(2,1)S(1)}, bf16[512,2048]{1,0:T(8,128)(2,1)}, u32[]{:S(2)}, u32[]{:S(2)}) %collective-permute-start.5) | collective-permute-done | bytes 2097184 | tf_op jit(solution)/shard_map/ppermute | solution.py:51
  116.7 18.6 %attend.1 = (f32[2048,256]{1,0:T(8,128)}, bf16[2048,256]{1,0:T(8,128)(2,1)}, bf16[2048,256]{1,0:T(8,128)(2,1)}, f32[2,2048]{1,0:T(2,128)}) custom-call(s32[1]{0:T(128)S(6)} %copy.41.length_ref, s32[16]{0:T(128)} %select_n.79.place_ref, s32[16]{0:T(128)} %reshape.201.index_ref, bf16[2048,256]{1,0:T(8,128)(2,1)} %get-tuple-element.82.q_ref, ...), custom_call_target="tpu_custom_call" | custom-call | flops 6104999936 | bytes 1048576 | tf_op jit(solution)/shard_map/attend/pallas_call | solution.py:470
  135.4 3.8 collective-permute-done.7.refs_1_
  140.5 3.7 all-to-all-start
  144.8 6.6 %assemble.1.wo_ref = bf16[8,2048,256]{2,1,0:T(8,128)(2,1)} custom-call(bf16[4096,256]{1,0:T(8,128)(2,1)} %pad_maximum_fusion.2.refs_0_, bf16[4096,256]{1,0:T(8,128)(2,1)} %collective-permute-done.7.refs_1_, bf16[4096,256]{1,0:T(8,128)(2,1)} %collective-permute-done.8.refs_2_, bf16[4096,256]{1,0:T(8,128)(2,1)} %collective-permute-done.9.refs_3_), custom_call_target="tpu_custom_call" | custom-call | flops 1980000000 | bytes 1048576 | tf_op jit(solution)/shard_map/assemble/pallas_call | solution.py:123
  151.4 8.2 %all-to-all-done.a_ref = bf16[8,256,256]{2,1,0:T(8,128)(2,1)S(1)} async-done(((bf16[8,256,256]{2,1,0:T(8,128)(2,1)}), bf16[8,256,256]{2,1,0:T(8,128)(2,1)S(1)}, u32[]{:S(2)}, u32[]{:S(2)}) %all-to-all-start) | async-done | bytes 1048608 | tf_op jit(solution)/shard_map/all_to_all | solution.py:229
  160.5 11.1 %branch.1 = (f32[256,2048]{1,0:T(8,128)}, bf16[256,2048]{1,0:T(8,128)(2,1)}) custom-call(s32[8]{0:T(128)} %copy-done.23, bf16[8,256,256]{2,1,0:T(8,128)(2,1)} %copy-done.11, bf16[8,2048,256]{2,1,0:T(8,128)(2,1)} %assemble.1.wo_ref, bf16[256,2048]{1,0:T(8,128)(2,1)} %bitcast.90, f32[1,2048]{1,0:T(1,128)} %bitcast.121), custom_call_target="tpu_custom_call" | custom-call | flops 3630000128 | bytes 1048576 | tf_op jit(solution)/shard_map/branch/pallas_call | solution.py:648
  175.4 11.4 %collective-permute-done.10 = bf16[256,2048]{1,0:T(8,128)(2,1)} collective-permute-done((bf16[256,2048]{1,0:T(8,128)(2,1)}, bf16[256,2048]{1,0:T(8,128)(2,1)}, u32[]{:S(2)}, u32[]{:S(2)}) %collective-permute-start.10) | collective-permute-done | bytes 1048608 | tf_op jit(solution)/shard_map/ppermute | solution.py:51
  190.6 25.3 %collective-permute-done.11.refs_1_ = bf16[512,2048]{1,0:T(8,128)(2,1)} collective-permute-done((bf16[512,2048]{1,0:T(8,128)(2,1)}, bf16[512,2048]{1,0:T(8,128)(2,1)}, u32[]{:S(2)}, u32[]{:S(2)}) %collective-permute-start.11) | collective-permute-done | bytes 2097184 | tf_op jit(solution)/shard_map/ppermute | solution.py:51
  220.4 21.4 %feed.2 = (bf16[8,256,1024]{2,1,0:T(8,128)(2,1)}, bf16[8,256,512]{2,1,0:T(8,128)(2,1)}) custom-call(bf16[512,2048]{1,0:T(8,128)(2,1)} %pad_maximum_fusion.3.refs_0_, bf16[512,2048]{1,0:T(8,128)(2,1)} %collective-permute-done.11.refs_1_, bf16[512,2048]{1,0:T(8,128)(2,1)} %collective-permute-done.12.refs_2_, ...), custom_call_target="tpu_custom_call" | custom-call | flops 1246666624 | bytes 1048576 | tf_op jit(solution)/shard_map/feed/pallas_call | solution.py:761
  241.8 19.6 %weight_grad.3 = bf16[4,8,64,1536]{3,2,1,0:T(8,128)(2,1)} custom-call(bf16[512,2048]{1,0:T(8,128)(2,1)} %pad_maximum_fusion.3.refs_0_, bf16[512,2048]{1,0:T(8,128)(2,1)} %collective-permute-done.11.refs_1_, bf16[512,2048]{1,0:T(8,128)(2,1)} %collective-permute-done.12.refs_2_, bf16[512,2048]{1,0:T(8,128)(2,1)} %collective-permute-done.13.refs_3_, ...), custom_call_target="tpu_custom_call" | custom-call | flops 1173333376 | bytes 1048576 | tf_op jit(solution)/shard_map/weight_grad/pallas_call | solution.py:265
  261.5 17.3 %feed.3 = (bf16[8,256,512]{2,1,0:T(8,128)(2,1)}, bf16[8,256,256]{2,1,0:T(8,128)(2,1)}) custom-call(bf16[512,2048]{1,0:T(8,128)(2,1)} %pad_maximum_fusion.3.refs_0_, bf16[512,2048]{1,0:T(8,128)(2,1)} %collective-permute-done.11.refs_1_, bf16[512,2048]{1,0:T(8,128)(2,1)} %collective-permute-done.12.refs_2_, bf16[512,2048]{1,0:T(8,128)(2,1)} %collective-permute-done.13.refs_3_, ...), custom_call_target="tpu_custom_call" | custom-call | flops 623333312 | bytes 1048576 | tf_op jit(solution)/shard_map/feed/pallas_call | solution.py:761
  278.8 7.4 %mm_slots.8 = bf16[2,256,2048]{2,1,0:T(8,128)(2,1)} custom-call(bf16[8,256,1024]{2,1,0:T(8,128)(2,1)} %get-tuple-element.98.refs_0_, bf16[8,256,512]{2,1,0:T(8,128)(2,1)} %get-tuple-element.99.refs_1_, bf16[2048,1536]{1,0:T(8,128)(2,1)} %all-gather.5.cloned.1.call-done.refs_8_.refs_2_, bf16[2048,768]{1,0:T(8,128)(2,1)} %all-gather.7.cloned.1.call-done.refs_8_.refs_3_), custom_call_target="tpu_custom_call" | custom-call | flops 6600000000 | bytes 1048576 | tf_op jit(solution)/shard_map/mm_slots/pallas_call | solution.py:163
  286.3 7.4 %mm_slots.10 = bf16[2,256,2048]{2,1,0:T(8,128)(2,1)} custom-call(bf16[8,256,1024]{2,1,0:T(8,128)(2,1)} %get-tuple-element.98.refs_0_, bf16[8,256,512]{2,1,0:T(8,128)(2,1)} %get-tuple-element.99.refs_1_, bf16[2048,1536]{1,0:T(8,128)(2,1)} %all-gather.5.cloned.1.call-done.refs_8_.refs_2_, bf16[2048,768]{1,0:T(8,128)(2,1)} %all-gather.7.cloned.1.call-done.refs_8_.refs_3_), custom_call_target="tpu_custom_call" | custom-call | flops 6600000000 | bytes 1048576 | tf_op jit(solution)/shard_map/mm_slots/pallas_call | solution.py:163
  295.5 7.9 %mm_slots.9 = bf16[2,256,2048]{2,1,0:T(8,128)(2,1)} custom-call(bf16[8,256,1024]{2,1,0:T(8,128)(2,1)} %get-tuple-element.98.refs_0_, bf16[8,256,512]{2,1,0:T(8,128)(2,1)} %get-tuple-element.99.refs_1_, bf16[2048,1536]{1,0:T(8,128)(2,1)} %all-gather.5.cloned.1.call-done.refs_8_.refs_2_, bf16[2048,768]{1,0:T(8,128)(2,1)} %all-gather.7.cloned.1.call-done.refs_8_.refs_3_, ...), custom_call_target="tpu_custom_call" | custom-call | flops 6600000000 | bytes 1048576 | tf_op jit(solution)/shard_map/mm_slots/pallas_call | solution.py:163
  305.3 8.4 %mm_slots.11 = f32[2,256,2048]{2,1,0:T(8,128)} custom-call(bf16[8,256,1024]{2,1,0:T(8,128)(2,1)} %get-tuple-element.98.refs_0_, bf16[8,256,512]{2,1,0:T(8,128)(2,1)} %get-tuple-element.99.refs_1_, bf16[2048,1536]{1,0:T(8,128)(2,1)} %all-gather.5.cloned.1.call-done.refs_8_.refs_2_, bf16[2048,768]{1,0:T(8,128)(2,1)} %all-gather.7.cloned.1.call-done.refs_8_.refs_3_, ...), custom_call_target="tpu_custom_call" | custom-call | flops 6600000000 | bytes 1048576 | tf_op jit(solution)/shard_map/mm_slots/pallas_call | solution.py:163
  313.7 14.2 %weight_grad.4 = bf16[4,8,64,768]{3,2,1,0:T(8,128)(2,1)} custom-call(bf16[512,2048]{1,0:T(8,128)(2,1)} %pad_maximum_fusion.3.refs_0_, bf16[512,2048]{1,0:T(8,128)(2,1)} %collective-permute-done.11.refs_1_, bf16[512,2048]{1,0:T(8,128)(2,1)} %collective-permute-done.12.refs_2_, bf16[512,2048]{1,0:T(8,128)(2,1)} %collective-permute-done.13.refs_3_, ...), custom_call_target="tpu_custom_call" | custom-call | flops 11733332992 | bytes 1048576 | tf_op jit(solution)/shard_map/weight_grad/pallas_call | solution.py:265
  331.5 7.5 %mm_slots.12 = bf16[4,256,2048]{2,1,0:T(8,128)(2,1)} custom-call(bf16[8,256,512]{2,1,0:T(8,128)(2,1)} %get-tuple-element.105.refs_0_, bf16[8,256,256]{2,1,0:T(8,128)(2,1)} %get-tuple-element.100.refs_1_, bf16[2048,1536]{1,0:T(8,128)(2,1)} %all-gather.5.cloned.1.call-done.refs_8_.refs_2_, bf16[2048,768]{1,0:T(8,128)(2,1)} %all-gather.7.cloned.1.call-done.refs_8_.refs_3_), custom_call_target="tpu_custom_call" | custom-call | flops 6600000000 | bytes 1048576 | tf_op jit(solution)/shard_map/mm_slots/pallas_call | solution.py:163
  339.5 14.3 %collective-permute-done.19 = bf16[256,2048]{1,0:T(8,128)(2,1)S(1)} collective-permute-done((bf16[256,2048]{1,0:T(8,128)(2,1)S(1)}, bf16[256,2048]{1,0:T(8,128)(2,1)S(1)}, u32[]{:S(2)}, u32[]{:S(2)}) %collective-permute-start.19) | collective-permute-done | bytes 1048608 | tf_op jit(solution)/shard_map/ppermute | solution.py:51
  355.6 13.0 %branch_back.1 = (f32[256,2048]{1,0:T(8,128)}, bf16[256,2048]{1,0:T(8,128)(2,1)}, f32[1,2048]{1,0:T(1,128)}, bf16[8,256,256]{2,1,0:T(8,128)(2,1)}) custom-call(s32[8]{0:T(128)} %copy-done.23, f32[256,2048]{1,0:T(8,128)} %bitcast_add_fusion.2.dxn_ref, f32[256,2048]{1,0:T(8,128)} %get-tuple-element.89.h1_ref, bf16[256,2048]{1,0:T(8,128)(2,1)} %bitcast.108, ...), custom_call_target="tpu_custom_call" | custom-call | flops 14300000256 | bytes 1048576 | tf_op jit(solution)/shard_map/branch_back/pallas_call | solution.py:696
  373.5 8.4 %mm_slots.13 = (f32[2,256,2048]{2,1,0:T(8,128)}, bf16[2,256,2048]{2,1,0:T(8,128)(2,1)}) custom-call(bf16[8,256,512]{2,1,0:T(8,128)(2,1)} %get-tuple-element.105.refs_0_, bf16[8,256,256]{2,1,0:T(8,128)(2,1)} %get-tuple-element.100.refs_1_, bf16[2048,1536]{1,0:T(8,128)(2,1)} %all-gather.5.cloned.1.call-done.refs_8_.refs_2_, ...), custom_call_target="tpu_custom_call" | custom-call | flops 6600000000 | bytes 1048576 | tf_op jit(solution)/shard_map/mm_slots/pallas_call | solution.py:163
  381.9 7.4 %collective-permute-done.21 = bf16[256,2048]{1,0:T(8,128)(2,1)S(1)} collective-permute-done((bf16[256,2048]{1,0:T(8,128)(2,1)}, bf16[256,2048]{1,0:T(8,128)(2,1)S(1)}, u32[]{:S(2)}, u32[]{:S(2)}) %collective-permute-start.21) | collective-permute-done | bytes 1048608 | tf_op jit(solution)/shard_map/ppermute | solution.py:51
  390.8 4.2 all-to-all-done.1
  396.4 31.9 %attend_back.1 = (bf16[2048,512]{1,0:T(8,128)(2,1)}, f32[1,128]{1,0:T(1,128)}, f32[1,128]{1,0:T(1,128)}) custom-call(s32[1]{0:T(128)S(6)} %copy.41.length_ref, s32[16]{0:T(128)} %select_n.79.place_ref, s32[16]{0:T(128)} %reshape.201.index_ref, bf16[2048,256]{1,0:T(8,128)(2,1)} %get-tuple-element.82.q_ref, bf16[2048,128]{1,0:T(8,128)(2,1)} %get-tuple-element.83.k_ref, ...), custom_call_target="tpu_custom_call" | custom-call | flops 36300001280 | bytes 1048576 | tf_op jit(solution)/shard_map/attend_back/pallas_call | solution.py:616
  430.9 4.4 reduce-scatter.4.cloned.1.call-done
  435.3 15.1 %weight_grad.5 = (bf16[4,8,64,768]{3,2,1,0:T(8,128)(2,1)}, f32[2048,1]{1,0:T(8,128)}) custom-call(bf16[2048,2048]{1,0:T(8,128)(2,1)} %bitcast.131, bf16[2048,512]{1,0:T(8,128)(2,1)} %get-tuple-element.129.refs_1_, bf16[512,2048]{1,0:T(8,128)(2,1)} %pad_maximum_fusion.4.refs_2_, bf16[512,2048]{1,0:T(8,128)(2,1)} %collective-permute-done.22.refs_3_, ...), custom_call_target="tpu_custom_call" | custom-call | flops 11733332992 | bytes 1048576 | tf_op jit(solution)/shard_map/weight_grad/pallas_call | solution.py:265
  457.4 3.6 fusion.11
  461.1 6.1 %mm_slots.14 = bf16[4,256,2048]{2,1,0:T(8,128)(2,1)} custom-call(bf16[8,256,512]{2,1,0:T(8,128)(2,1)} %bitcast.93, bf16[2048,512]{1,0:T(8,128)(2,1)} %bitcast.88), custom_call_target="tpu_custom_call" | custom-call | flops 513333344 | bytes 1048576 | tf_op jit(solution)/shard_map/mm_slots/pallas_call | solution.py:163
  467.2 3.6 all-to-all-start.2
  470.8 3.8 collective-permute-done.29.refs_2_
  474.7 7.7 %mm_slots.15 = (f32[2,256,2048]{2,1,0:T(8,128)}, bf16[2,256,2048]{2,1,0:T(8,128)(2,1)}) custom-call(bf16[8,256,512]{2,1,0:T(8,128)(2,1)} %bitcast.94, bf16[2048,512]{1,0:T(8,128)(2,1)} %bitcast.89, bf16[4,256,2048]{2,1,0:T(8,128)(2,1)} %collective-permute-done.29.refs_2_), custom_call_target="tpu_custom_call" | custom-call | flops 513333344 | bytes 1048576 | tf_op jit(solution)/shard_map/mm_slots/pallas_call | solution.py:163
  482.3 9.4 %all-to-all-done.2.refs_0_ = bf16[8,64,1536]{2,1,0:T(8,128)(2,1)S(1)} async-done(((bf16[8,64,1536]{2,1,0:T(8,128)(2,1)}), bf16[8,64,1536]{2,1,0:T(8,128)(2,1)S(1)}, u32[]{:S(2)}, u32[]{:S(2)}) %all-to-all-start.2) | async-done | bytes 1572896 | tf_op jit(solution)/shard_map/all_to_all | solution.py:229
  500.2 5.4 collective-permute-done.34
  505.5 23.7 %collective-permute-done.30 = bf16[2,256,2048]{2,1,0:T(8,128)(2,1)S(1)} collective-permute-done((bf16[2,256,2048]{2,1,0:T(8,128)(2,1)}, bf16[2,256,2048]{2,1,0:T(8,128)(2,1)S(1)}, u32[]{:S(2)}, u32[]{:S(2)}) %collective-permute-start.30) | collective-permute-done | bytes 2097184 | tf_op jit(solution)/shard_map/ppermute | solution.py:51
  529.2 3.7 fusion.12
  534.1 4.2 all-to-all-start.4
  538.8 3.7 fusion.13
  542.6 13.9 %all-to-all-done.4.refs_1_ = bf16[8,64,768]{2,1,0:T(8,128)(2,1)} async-done(((bf16[8,64,768]{2,1,0:T(8,128)(2,1)}), bf16[8,64,768]{2,1,0:T(8,128)(2,1)}, u32[]{:S(2)}, u32[]{:S(2)}) %all-to-all-start.4) | async-done | bytes 786464 | tf_op jit(solution)/shard_map/all_to_all | solution.py:229
  556.5 6.3 %join_columns.3 = (f32[64,6144]{1,0:T(8,128)}, f32[64,6144]{1,0:T(8,128)}, f32[64,6144]{1,0:T(8,128)}) custom-call(bf16[8,64,1536]{2,1,0:T(8,128)(2,1)} %copy-done.9, bf16[8,64,768]{2,1,0:T(8,128)(2,1)} %all-to-all-done.4.refs_1_), custom_call_target="tpu_custom_call" | custom-call | flops 1100000000 | bytes 1048576 | tf_op jit(solution)/shard_map/join_columns/pallas_call | solution.py:293
  565.8 4.2 all-to-all-start.3
  573.5 9.1 %all-to-all-done.3.refs_0_ = bf16[8,64,768]{2,1,0:T(8,128)(2,1)} async-done(((bf16[8,64,768]{2,1,0:T(8,128)(2,1)}), bf16[8,64,768]{2,1,0:T(8,128)(2,1)}, u32[]{:S(2)}, u32[]{:S(2)}) %all-to-all-start.3) | async-done | bytes 786464 | tf_op jit(solution)/shard_map/all_to_all | solution.py:229
  582.6 5.2 join_columns.2
  (182 shorter events, 89.4 us)
Async XLA Ops:
  7.2 71.9 %all-gather.9.cloned.1.call-start = ((), (), s32[]{:S(2)}) async-start(), calls=%async_computation.13 | async-start | bytes 4055040 | tf_op jit(solution)/shard_map/all_gather | solution.py:817
  11.1 207.6 %all-gather.5.cloned.1.call-start = ((), (), s32[]{:S(2)}) async-start(), calls=%async_computation.8 | async-start | bytes 7864320 | tf_op jit(solution)/shard_map/all_gather | solution.py:805
  11.2 15.8 %collective-permute-start = (bf16[256,2048]{1,0:T(8,128)(2,1)S(1)}, bf16[256,2048]{1,0:T(8,128)(2,1)S(1)}, u32[]{:S(2)}, u32[]{:S(2)}) collective-permute-start(bf16[256,2048]{1,0:T(8,128)(2,1)S(1)} %bitcast.91), channel_id=1, source_target_pairs={{0,8},{4,20},{8,0},{12,28},{16,24},{20,4},{24,16},{28,12},{1,9},{5... | collective-permute-start | bytes 3145736 | tf_op jit(solution)/shard_map/ppermute | solution.py:51
  28.4 37.2 %collective-permute-start.1 = (bf16[512,2048]{1,0:T(8,128)(2,1)}, bf16[512,2048]{1,0:T(8,128)(2,1)}, u32[]{:S(2)}, u32[]{:S(2)}) collective-permute-start(bf16[512,2048]{1,0:T(8,128)(2,1)} %pad_maximum_fusion.refs_0_), channel_id=1, source_target_pairs={{0,16},{4,12},{8,24},{12,4},{16,0},{20,28},{24,8},{28,20},{1,17},{... | collective-permute-start | bytes 6291464 | tf_op jit(solution)/shard_map/ppermute | solution.py:51
  30.5 26.2 %collective-permute-start.2 = (bf16[256,2048]{1,0:T(8,128)(2,1)S(1)}, bf16[256,2048]{1,0:T(8,128)(2,1)}, u32[]{:S(2)}, u32[]{:S(2)}) collective-permute-start(bf16[256,2048]{1,0:T(8,128)(2,1)S(1)} %bitcast.109), channel_id=1, source_target_pairs={{0,8},{4,20},{8,0},{12,28},{16,24},{20,4},{24,16},{28,12},{1,9},{5... | collective-permute-start | bytes 3145736 | tf_op jit(solution)/shard_map/ppermute | solution.py:51
  58.1 132.0 %copy-start = (bf16[512,2048]{1,0:T(8,128)(2,1)}, bf16[512,2048]{1,0:T(8,128)(2,1)S(1)}, u32[]{:S(2)}) copy-start(bf16[512,2048]{1,0:T(8,128)(2,1)S(1)} %pad_maximum_fusion.1.refs_4_.refs_5_) | copy-start | bytes 6291460
  65.7 14.8 %collective-permute-start.4 = (bf16[512,2048]{1,0:T(8,128)(2,1)}, bf16[512,2048]{1,0:T(8,128)(2,1)}, u32[]{:S(2)}, u32[]{:S(2)}) collective-permute-start(bf16[512,2048]{1,0:T(8,128)(2,1)} %collective-permute-done.1.refs_1_), channel_id=1, source_target_pairs={{0,4},{4,0},{8,12},{12,8},{16,20},{20,16},{24,28},{28,24},{1,5},{5... | collective-permute-start | bytes 6291464 | tf_op jit(solution)/shard_map/ppermute | solution.py:47
  67.0 19.9 %collective-permute-start.3 = (bf16[512,2048]{1,0:T(8,128)(2,1)}, bf16[512,2048]{1,0:T(8,128)(2,1)}, u32[]{:S(2)}, u32[]{:S(2)}) collective-permute-start(bf16[512,2048]{1,0:T(8,128)(2,1)} %pad_maximum_fusion.refs_0_), channel_id=1, source_target_pairs={{0,4},{4,0},{8,12},{12,8},{16,20},{20,16},{24,28},{28,24},{1,5},{5... | collective-permute-start | bytes 6291464 | tf_op jit(solution)/shard_map/ppermute | solution.py:47
  80.5 23.4 %collective-permute-start.6 = (bf16[2048,256]{1,0:T(8,128)(2,1)S(1)}, bf16[2048,256]{1,0:T(8,128)(2,1)}, u32[]{:S(2)}, u32[]{:S(2)}) collective-permute-start(bf16[2048,256]{1,0:T(8,128)(2,1)S(1)} %bitcast.96), channel_id=1, source_target_pairs={{0,8},{4,20},{8,0},{12,28},{16,24},{20,4},{24,16},{28,12},{1,9},{5... | collective-permute-start | bytes 3145736 | tf_op jit(solution)/shard_map/ppermute | solution.py:51
  85.4 31.4 %collective-permute-start.5 = (bf16[512,2048]{1,0:T(8,128)(2,1)S(1)}, bf16[512,2048]{1,0:T(8,128)(2,1)}, u32[]{:S(2)}, u32[]{:S(2)}) collective-permute-start(bf16[512,2048]{1,0:T(8,128)(2,1)S(1)} %pad_maximum_fusion.1.refs_4_.refs_5_), channel_id=1, source_target_pairs={{0,16},{4,12},{8,24},{12,4},{16,0},{20,28},{24,8},{28,20},{1,17},{... | collective-permute-start | bytes 6291464 | tf_op jit(solution)/shard_map/ppermute | solution.py:51
  106.5 32.7 %collective-permute-start.7 = (bf16[4096,256]{1,0:T(8,128)(2,1)}, bf16[4096,256]{1,0:T(8,128)(2,1)}, u32[]{:S(2)}, u32[]{:S(2)}) collective-permute-start(bf16[4096,256]{1,0:T(8,128)(2,1)} %pad_maximum_fusion.2.refs_0_), channel_id=1, source_target_pairs={{0,16},{4,12},{8,24},{12,4},{16,0},{20,28},{24,8},{28,20},{1,17},{... | collective-permute-start | bytes 6291464 | tf_op jit(solution)/shard_map/ppermute | solution.py:51
  109.5 35.3 %collective-permute-start.8 = (bf16[4096,256]{1,0:T(8,128)(2,1)}, bf16[4096,256]{1,0:T(8,128)(2,1)}, u32[]{:S(2)}, u32[]{:S(2)}) collective-permute-start(bf16[4096,256]{1,0:T(8,128)(2,1)} %pad_maximum_fusion.2.refs_0_), channel_id=1, source_target_pairs={{0,4},{4,0},{8,12},{12,8},{16,20},{20,16},{24,28},{28,24},{1,5},{5... | collective-permute-start | bytes 6291464 | tf_op jit(solution)/shard_map/ppermute | solution.py:47
  139.2 5.6 collective-permute-start.9
  140.5 19.1 %all-to-all-start = ((bf16[8,256,256]{2,1,0:T(8,128)(2,1)}), bf16[8,256,256]{2,1,0:T(8,128)(2,1)S(1)}, u32[]{:S(2)}, u32[]{:S(2)}) async-start(bf16[8,256,256]{2,1,0:T(8,128)(2,1)} %bitcast.106), calls=%async_computation | async-start | bytes 2097152 | tf_op jit(solution)/shard_map/all_to_all | solution.py:229
  144.1 117.4 %all-gather.7.cloned.1.call-start = ((), (), s32[]{:S(2)}) async-start(), calls=%async_computation.9 | async-start | bytes 3932160 | tf_op jit(solution)/shard_map/all_gather | solution.py:805
  171.6 15.1 %collective-permute-start.10 = (bf16[256,2048]{1,0:T(8,128)(2,1)}, bf16[256,2048]{1,0:T(8,128)(2,1)}, u32[]{:S(2)}, u32[]{:S(2)}) collective-permute-start(bf16[256,2048]{1,0:T(8,128)(2,1)} %get-tuple-element.90), channel_id=1, source_target_pairs={{0,8},{4,20},{8,0},{12,28},{16,24},{20,4},{24,16},{28,12},{1,9},{5... | collective-permute-start | bytes 3145736 | tf_op jit(solution)/shard_map/ppermute | solution.py:51
  175.2 221.2 %reduce-scatter.6.cloned.1.call-start = ((), (), s32[]{:S(2)}) async-start(), calls=%async_computation.11 | async-start | bytes 7864320 | tf_op jit(solution)/shard_map/reduce_scatter | solution.py:279
  175.4 40.5 %copy-start.5 = (bf16[2112,768]{1,0:T(8,128)(2,1)S(1)}, bf16[2112,768]{1,0:T(8,128)(2,1)}, u32[]{:S(2)}) copy-start(bf16[2112,768]{1,0:T(8,128)(2,1)} %all-gather.9.cloned.1.call-done) | copy-start | bytes 9732100
  189.5 26.4 %collective-permute-start.11 = (bf16[512,2048]{1,0:T(8,128)(2,1)}, bf16[512,2048]{1,0:T(8,128)(2,1)}, u32[]{:S(2)}, u32[]{:S(2)}) collective-permute-start(bf16[512,2048]{1,0:T(8,128)(2,1)} %pad_maximum_fusion.3.refs_0_), channel_id=1, source_target_pairs={{0,16},{4,12},{8,24},{12,4},{16,0},{20,28},{24,8},{28,20},{1,17},{... | collective-permute-start | bytes 6291464 | tf_op jit(solution)/shard_map/ppermute | solution.py:51
  190.1 27.3 %collective-permute-start.14 = (bf16[512,2048]{1,0:T(8,128)(2,1)S(1)}, bf16[512,2048]{1,0:T(8,128)(2,1)S(1)}, u32[]{:S(2)}, u32[]{:S(2)}) collective-permute-start(bf16[512,2048]{1,0:T(8,128)(2,1)S(1)} %pad_maximum_fusion.1.refs_4_.refs_5_), channel_id=1, source_target_pairs={{0,4},{4,0},{8,12},{12,8},{16,20},{20,16},{24,28},{28,24},{1,5},{5... | collective-permute-start | bytes 6291464 | tf_op jit(solution)/shard_map/ppermute | solution.py:47
  190.1 28.6 %collective-permute-start.15 = (bf16[512,2048]{1,0:T(8,128)(2,1)}, bf16[512,2048]{1,0:T(8,128)(2,1)}, u32[]{:S(2)}, u32[]{:S(2)}) collective-permute-start(bf16[512,2048]{1,0:T(8,128)(2,1)} %collective-permute-done.5.refs_5_.refs_6_), channel_id=1, source_target_pairs={{0,4},{4,0},{8,12},{12,8},{16,20},{20,16},{24,28},{28,24},{1,5},{5... | collective-permute-start | bytes 6291464 | tf_op jit(solution)/shard_map/ppermute | solution.py:47
  190.6 28.1 %collective-permute-start.12 = (bf16[512,2048]{1,0:T(8,128)(2,1)}, bf16[512,2048]{1,0:T(8,128)(2,1)}, u32[]{:S(2)}, u32[]{:S(2)}) collective-permute-start(bf16[512,2048]{1,0:T(8,128)(2,1)} %pad_maximum_fusion.3.refs_0_), channel_id=1, source_target_pairs={{0,4},{4,0},{8,12},{12,8},{16,20},{20,16},{24,28},{28,24},{1,5},{5... | collective-permute-start | bytes 6291464 | tf_op jit(solution)/shard_map/ppermute | solution.py:47
  215.9 4.5 collective-permute-start.13
  286.2 8.0 %collective-permute-start.16 = (bf16[2,256,2048]{2,1,0:T(8,128)(2,1)}, bf16[2,256,2048]{2,1,0:T(8,128)(2,1)S(1)}, u32[]{:S(2)}, u32[]{:S(2)}) collective-permute-start(bf16[2,256,2048]{2,1,0:T(8,128)(2,1)} %mm_slots.8), channel_id=1, source_target_pairs={{0,4},{4,0},{8,12},{12,8},{16,20},{20,16},{24,28},{28,24},{1,5},{5... | collective-permute-start | bytes 6291464 | tf_op jit(solution)/shard_map/ppermute | solution.py:47
  293.8 10.2 %collective-permute-start.17 = (bf16[2,256,2048]{2,1,0:T(8,128)(2,1)}, bf16[2,256,2048]{2,1,0:T(8,128)(2,1)S(1)}, u32[]{:S(2)}, u32[]{:S(2)}) collective-permute-start(bf16[2,256,2048]{2,1,0:T(8,128)(2,1)} %mm_slots.10), channel_id=1, source_target_pairs={{0,4},{4,0},{8,12},{12,8},{16,20},{20,16},{24,28},{28,24},{1,5},{5... | collective-permute-start | bytes 6291464 | tf_op jit(solution)/shard_map/ppermute | solution.py:47
  303.4 26.2 %collective-permute-start.18 = (bf16[2,256,2048]{2,1,0:T(8,128)(2,1)}, bf16[2,256,2048]{2,1,0:T(8,128)(2,1)S(1)}, u32[]{:S(2)}, u32[]{:S(2)}) collective-permute-start(bf16[2,256,2048]{2,1,0:T(8,128)(2,1)} %mm_slots.9), channel_id=1, source_target_pairs={{0,16},{4,12},{8,24},{12,4},{16,0},{20,28},{24,8},{28,20},{1,17},{... | collective-permute-start | bytes 6291464 | tf_op jit(solution)/shard_map/ppermute | solution.py:51
  339.0 34.4 %collective-permute-start.20 = (bf16[4,256,2048]{2,1,0:T(8,128)(2,1)}, bf16[4,256,2048]{2,1,0:T(8,128)(2,1)}, u32[]{:S(2)}, u32[]{:S(2)}) collective-permute-start(bf16[4,256,2048]{2,1,0:T(8,128)(2,1)} %mm_slots.12), channel_id=1, source_target_pairs={{0,4},{4,0},{8,12},{12,8},{16,20},{20,16},{24,28},{28,24},{1,5},{5... | collective-permute-start | bytes 12582920 | tf_op jit(solution)/shard_map/ppermute | solution.py:47
  339.0 14.8 %collective-permute-start.19 = (bf16[256,2048]{1,0:T(8,128)(2,1)S(1)}, bf16[256,2048]{1,0:T(8,128)(2,1)S(1)}, u32[]{:S(2)}, u32[]{:S(2)}) collective-permute-start(bf16[256,2048]{1,0:T(8,128)(2,1)S(1)} %fusion.10), channel_id=1, source_target_pairs={{0,8},{4,20},{8,0},{12,28},{16,24},{20,4},{24,16},{28,12},{1,9},{5... | collective-permute-start | bytes 3145736 | tf_op jit(solution)/shard_map/ppermute | solution.py:51
  368.6 20.6 %collective-permute-start.21 = (bf16[256,2048]{1,0:T(8,128)(2,1)}, bf16[256,2048]{1,0:T(8,128)(2,1)S(1)}, u32[]{:S(2)}, u32[]{:S(2)}) collective-permute-start(bf16[256,2048]{1,0:T(8,128)(2,1)} %get-tuple-element.112), channel_id=1, source_target_pairs={{0,8},{4,20},{8,0},{12,28},{16,24},{20,4},{24,16},{28,12},{1,9},{5... | collective-permute-start | bytes 3145736 | tf_op jit(solution)/shard_map/ppermute | solution.py:51
  369.2 25.8 %all-to-all-start.1 = ((bf16[8,256,256]{2,1,0:T(8,128)(2,1)}), bf16[8,256,256]{2,1,0:T(8,128)(2,1)S(1)}, u32[]{:S(2)}, u32[]{:S(2)}) async-start(bf16[8,256,256]{2,1,0:T(8,128)(2,1)} %get-tuple-element.109), calls=%async_computation.2 | async-start | bytes 2097152 | tf_op jit(solution)/shard_map/all_to_all | solution.py:229
  372.8 62.5 %reduce-scatter.4.cloned.1.call-start = ((), (), s32[]{:S(2)}) async-start(), calls=%async_computation.10 | async-start | bytes 3932160 | tf_op jit(solution)/shard_map/reduce_scatter | solution.py:279
  373.4 192.4 %reduce-scatter.8.cloned.1.call-start = ((), (), s32[]{:S(2)}) async-start(), calls=%async_computation.12 | async-start | bytes 3932160 | tf_op jit(solution)/shard_map/reduce_scatter | solution.py:279
  395.0 33.3 %collective-permute-start.22 = (bf16[512,2048]{1,0:T(8,128)(2,1)}, bf16[512,2048]{1,0:T(8,128)(2,1)}, u32[]{:S(2)}, u32[]{:S(2)}) collective-permute-start(bf16[512,2048]{1,0:T(8,128)(2,1)} %pad_maximum_fusion.4.refs_2_), channel_id=1, source_target_pairs={{0,16},{4,12},{8,24},{12,4},{16,0},{20,28},{24,8},{28,20},{1,17},{... | collective-permute-start | bytes 6291464 | tf_op jit(solution)/shard_map/ppermute | solution.py:51
  396.4 38.9 %collective-permute-start.23 = (bf16[512,2048]{1,0:T(8,128)(2,1)}, bf16[512,2048]{1,0:T(8,128)(2,1)}, u32[]{:S(2)}, u32[]{:S(2)}) collective-permute-start(bf16[512,2048]{1,0:T(8,128)(2,1)} %pad_maximum_fusion.4.refs_2_), channel_id=1, source_target_pairs={{0,4},{4,0},{8,12},{12,8},{16,20},{20,16},{24,28},{28,24},{1,5},{5... | collective-permute-start | bytes 6291464 | tf_op jit(solution)/shard_map/ppermute | solution.py:47
  428.3 6.9 %collective-permute-start.24 = (bf16[512,2048]{1,0:T(8,128)(2,1)}, bf16[512,2048]{1,0:T(8,128)(2,1)}, u32[]{:S(2)}, u32[]{:S(2)}) collective-permute-start(bf16[512,2048]{1,0:T(8,128)(2,1)} %collective-permute-done.22.refs_3_), channel_id=1, source_target_pairs={{0,4},{4,0},{8,12},{12,8},{16,20},{20,16},{24,28},{28,24},{1,5},{5... | collective-permute-start | bytes 6291464 | tf_op jit(solution)/shard_map/ppermute | solution.py:47
  428.8 28.6 %collective-permute-start.25 = (bf16[2,256,2048]{2,1,0:T(8,128)(2,1)}, bf16[2,256,2048]{2,1,0:T(8,128)(2,1)S(1)}, u32[]{:S(2)}, u32[]{:S(2)}) collective-permute-start(bf16[2,256,2048]{2,1,0:T(8,128)(2,1)} %get-tuple-element.124), channel_id=1, source_target_pairs={{0,16},{4,12},{8,24},{12,4},{16,0},{20,28},{24,8},{28,20},{1,17},{... | collective-permute-start | bytes 6291464 | tf_op jit(solution)/shard_map/ppermute | solution.py:51
  452.0 3.8 collective-permute-start.27
  455.9 5.2 collective-permute-start.28
  467.2 7.5 %collective-permute-start.29 = (bf16[4,256,2048]{2,1,0:T(8,128)(2,1)}, bf16[4,256,2048]{2,1,0:T(8,128)(2,1)}, u32[]{:S(2)}, u32[]{:S(2)}) collective-permute-start(bf16[4,256,2048]{2,1,0:T(8,128)(2,1)} %mm_slots.14), channel_id=1, source_target_pairs={{0,4},{4,0},{8,12},{12,8},{16,20},{20,16},{24,28},{28,24},{1,5},{5... | collective-permute-start | bytes 12582920 | tf_op jit(solution)/shard_map/ppermute | solution.py:47
  467.2 24.6 %all-to-all-start.2 = ((bf16[8,64,1536]{2,1,0:T(8,128)(2,1)}), bf16[8,64,1536]{2,1,0:T(8,128)(2,1)S(1)}, u32[]{:S(2)}, u32[]{:S(2)}) async-start(bf16[8,64,1536]{2,1,0:T(8,128)(2,1)} %bitcast.19), calls=%async_computation.4 | async-start | bytes 3145728 | tf_op jit(solution)/shard_map/all_to_all | solution.py:229
  491.8 37.5 %collective-permute-start.30 = (bf16[2,256,2048]{2,1,0:T(8,128)(2,1)}, bf16[2,256,2048]{2,1,0:T(8,128)(2,1)S(1)}, u32[]{:S(2)}, u32[]{:S(2)}) collective-permute-start(bf16[2,256,2048]{2,1,0:T(8,128)(2,1)} %get-tuple-element.133), channel_id=1, source_target_pairs={{0,16},{4,12},{8,24},{12,4},{16,0},{20,28},{24,8},{28,20},{1,17},{... | collective-permute-start | bytes 6291464 | tf_op jit(solution)/shard_map/ppermute | solution.py:51
  492.3 1.2 collective-permute-start.32
  493.5 4.4 collective-permute-start.33
  494.8 44.1 %collective-permute-start.26 = (bf16[256,2048]{1,0:T(8,128)(2,1)}, bf16[256,2048]{1,0:T(8,128)(2,1)}, u32[]{:S(2)}, u32[]{:S(2)}) collective-permute-start(bf16[256,2048]{1,0:T(8,128)(2,1)} %fusion.11), channel_id=1, source_target_pairs={{0,8},{4,20},{8,0},{12,28},{16,24},{20,4},{24,16},{28,12},{1,9},{5... | collective-permute-start | bytes 3145736 | tf_op jit(solution)/shard_map/ppermute | solution.py:51
  497.9 7.6 %collective-permute-start.34 = (f32[34,128]{1,0:T(8,128)S(1)}, f32[34,128]{1,0:T(8,128)S(1)}, u32[]{:S(2)}, u32[]{:S(2)}) collective-permute-start(f32[34,128]{1,0:T(8,128)S(1)} %add.154), channel_id=1, source_target_pairs={{0,2},{1,3},{2,0},{3,1},{4,6},{5,7},{6,4},{7,5},{8,10},{9,11},{10,... | collective-permute-start | bytes 52232 | tf_op jit(solution)/shard_map/ppermute | solution.py:47
  533.0 29.9 %collective-permute-start.31 = (bf16[256,2048]{1,0:T(8,128)(2,1)}, bf16[256,2048]{1,0:T(8,128)(2,1)}, u32[]{:S(2)}, u32[]{:S(2)}) collective-permute-start(bf16[256,2048]{1,0:T(8,128)(2,1)} %fusion.12), channel_id=1, source_target_pairs={{0,8},{4,20},{8,0},{12,28},{16,24},{20,4},{24,16},{28,12},{1,9},{5... | collective-permute-start | bytes 3145736 | tf_op jit(solution)/shard_map/ppermute | solution.py:51
  534.1 22.4 %all-to-all-start.4 = ((bf16[8,64,768]{2,1,0:T(8,128)(2,1)}), bf16[8,64,768]{2,1,0:T(8,128)(2,1)}, u32[]{:S(2)}, u32[]{:S(2)}) async-start(bf16[8,64,768]{2,1,0:T(8,128)(2,1)} %bitcast.111), calls=%async_computation.7 | async-start | bytes 1572864 | tf_op jit(solution)/shard_map/all_to_all | solution.py:229
  565.8 16.8 %all-to-all-start.3 = ((bf16[8,64,768]{2,1,0:T(8,128)(2,1)}), bf16[8,64,768]{2,1,0:T(8,128)(2,1)}, u32[]{:S(2)}, u32[]{:S(2)}) async-start(bf16[8,64,768]{2,1,0:T(8,128)(2,1)} %bitcast.112), calls=%async_computation.6 | async-start | bytes 1572864 | tf_op jit(solution)/shard_map/all_to_all | solution.py:229
  (26 other events, 319.5 us)
Sparse Core Ops, SparseCore 0:
  11.3 67.8 all-gather.8
  81.3 113.9 all-gather.4
  196.8 61.7 all-gather.6
  261.6 108.5 reduce-scatter.5
  375.6 59.5 reduce-scatter.3
  467.3 60.3 reduce-scatter.7
